TPU v7x, 256 devices: a whole 4x4x8 slice. The times are simulated.
256 devices in a mesh: cal: 2 (over x_lo), gr: 16 (over x_hi, y, core), gc: 8 (over z).
Axes of the slice: x: 4 (x_hi: 2, x_lo: 2; x = x_hi * 2 + x_lo), y: 4, z: 8, core: 2. Of those that a mesh axis runs over, the one named last changes fastest.
Arguments:
- tokens: bfloat16 [512, 8192], P(('gr', 'gc'), 'cal'), may hold values from -12 to 12
- gate_weight: bfloat16 [8192, 28672], P(None, ('cal', 'gr', 'gc')), may hold values from -0.0625 to 0.0625
- up_weight: bfloat16 [8192, 28672], P(None, ('cal', 'gr', 'gc')), may hold values from -0.0625 to 0.0625
- hessian_slab: float32 [28672, 8192], P(('cal', 'gr'), 'gc'), may hold values from -1.2 to 1.2
- weight_error: float32 [512, 28672], P(None, ('cal', 'gr')), may hold values from -0.18 to 0.18
- slab_offset: int32 [1], replicated, may hold values from 0 to 20480
- token_count: int32 [1], replicated, may hold values from 512 to 1023
Outputs:
- new_slab: float32 [28672, 8192], P(('cal', 'gr'), 'gc')
- gradient: float32 [512, 8192], P(('cal', 'gr'), 'gc')
Inputs may be any that keep to these rules, and one draw needn't show every extreme that they name: The slab holds the Hessian's columns slab_offset[0] to slab_offset[0] + 8191.
All inputs are finite; a program needn't handle non-finite values.
Results may differ from a plain program's by a relative error of at most 0.0038.
Values may be sent and summed in bfloat16 or wider, within the bound.
No kernel may reach another device: no remote copies, remote signals or barrier semaphores. Data moves between devices by JAX's collectives and lax.ppermute only.
A program may use at most 64 MiB of HBM per device.

v0:
```python
import jax
import jax.numpy as jnp
from jax import lax
from jax.experimental import pallas as pl
from jax.experimental.pallas import tpu as pltpu
from jax.sharding import Mesh
from jax.sharding import PartitionSpec as P

GR_GC = ("gr_0", "gr_1", "gr_2", "gc")
PLANE = ("cal", "gr_0", "gr_1")
CAL_GR = ("cal", "gr_0", "gr_1", "gr_2")
CAL_GR_GC = ("cal", "gr_0", "gr_1", "gr_2", "gc")


F32 = jnp.float32
BF16 = jnp.bfloat16
NT = (((1,), (1,)), ((), ()))
VMEM = pl.BlockSpec(memory_space=pltpu.VMEM)
SMEM = pl.BlockSpec(memory_space=pltpu.SMEM)


def plane_index(x, y, c):
    return (((x & 1) * 2 + (x >> 1)) * 4 + y) * 2 + c


def plane_permute(array, on_x_of_core, k):
    pairs = []
    for x in range(4):
        for y in range(4):
            for c in range(2):
                to = (x ^ k, y) if c == on_x_of_core else (x, y ^ k)
                pairs.append((plane_index(x, y, c), plane_index(*to, c)))
    return lax.ppermute(array, CAL_GR, pairs)


def core_swap(array):
    return lax.ppermute(array, "gr_2", [(0, 1), (1, 0)])


def shift_z(array, d):
    return lax.ppermute(array, "gc", [(i, (i + d) % 8) for i in range(8)])


def exchange(array, axes):
    return lax.all_to_all(array, axes, split_axis=0, concat_axis=0, tiled=True)


def split_bf16(a):
    high = a.astype(BF16)
    return high, (a - high.astype(F32)).astype(BF16)


DEPTH = 1024


def weights_kernel(pos_ref, gate, up, far, out_ref):
    n = gate.shape[0]
    for i, part in enumerate((gate[...], up[...], far[0, 0], far[0, 1])):
        out_ref[0, i * 128 : i * 128 + n, :] = part
        out_ref[0, i * 128 + n : (i + 1) * 128, :] = jnp.zeros((128 - n, part.shape[1]), BF16)


def weights_call(pos, gate_t, up_t, far_w):
    n, depth = far_w.shape[2:]
    columns = pl.BlockSpec((n, depth), lambda f, pos: (0, (f ^ pos[0]) * 2 + pos[3]))
    return pl.pallas_call(
        weights_kernel,
        grid_spec=pltpu.PrefetchScalarGridSpec(
            num_scalar_prefetch=1,
            grid=(2,),
            in_specs=[columns, columns, pl.BlockSpec((1, 2, n, depth), lambda f, pos: (f ^ pos[0], 0, 0, 0))],
            out_specs=pl.BlockSpec((1, 512, depth), lambda f, pos: (f, 0, 0)),
        ),
        out_shape=jax.ShapeDtypeStruct((2, 512, depth), BF16),
        name="weights",
    )(pos, gate_t, up_t, far_w)


def product_kernel(rows_of_group, n_tok, finish, pos_ref, *refs):
    toks = refs[:n_tok]
    w_ref, own_p, far_p = refs[n_tok:]
    c = pos_ref[3]

    @pl.when(pl.program_id(0) == 0)
    def _():
        own_p[...] = jnp.zeros_like(own_p)
        far_p[...] = jnp.zeros_like(far_p)

    for (odd, g), rows in rows_of_group.items():
        t = jnp.concatenate([toks[i][...] for i, _ in rows], 0)
        f = jnp.where(c == 0, g, odd)
        out = lax.dot_general(t, w_ref[f], NT, preferred_element_type=F32)
        for a, (_, m) in enumerate(rows):
            for j in range(2):
                block = finish(pos_ref, c, m, g, j)
                at = pl.ds(pl.multiple_of(block * 64, 64), 64)
                part = out[a * 128 + j * 64 : a * 128 + (j + 1) * 64]
                own_p[at, :] += part[:, :256]
                far_p[at, :] += part[:, 256:]


def block_of(pos_ref, c, m, g, j):
    xh, y = pos_ref[1], pos_ref[2]
    return jnp.where(c == 0, (xh ^ j) * 4 + (y ^ m), (xh ^ (m >> 1)) * 4 + (y ^ (g + 2 * j)))


def late_block(pos_ref, c, m, g, j):
    return jnp.where(c == 0, j, g + 2 * j)


def product_call(pos, tokens, rows_of_group, finish, blocks, weights):
    depth = weights.shape[2]

    def kernel(pos_ref, *refs):
        product_kernel(rows_of_group, len(tokens), finish, pos_ref, *refs)

    out = jax.ShapeDtypeStruct((blocks * 64, 256), F32)
    whole = pl.BlockSpec((blocks * 64, 256), lambda k, pos: (0, 0))
    rows = 128 * len(tokens)
    return pl.pallas_call(
        kernel,
        grid_spec=pltpu.PrefetchScalarGridSpec(
            num_scalar_prefetch=1,
            grid=(depth // DEPTH,),
            in_specs=[pl.BlockSpec((128, DEPTH), lambda k, pos: (0, k)) for _ in tokens]
            + [pl.BlockSpec((2, 512, DEPTH), lambda k, pos: (0, 0, k))],
            out_specs=(whole, whole),
        ),
        out_shape=(out, out),
        cost_estimate=pl.CostEstimate(
            flops=2 * rows * depth * 512, bytes_accessed=8 << 20, transcendentals=0
        ),
        name="products",
    )(pos, *tokens, weights)


def activate(pos_ref, own_ref, far_ref, own_late, far_late, high_ref, low_ref, wh_ref, out_ref, ht_ref, sum_ref):
    c = pos_ref[3]
    xh, y = pos_ref[1], pos_ref[2]
    sum_ref[...] = own_ref[...] + far_ref[...]
    for late, core in ((own_late, c), (far_late, 1 - c)):
        for q in range(4):
            block = jnp.where(core == 0, (xh ^ (q & 1)) * 4 + (y ^ 2 ^ (q & 2)), (xh ^ 1) * 4 + (y ^ q))
            at = pl.ds(pl.multiple_of(block * 64, 64), 64)
            sum_ref[at, :] += late[q * 64 : (q + 1) * 64, :]
    both = sum_ref[...]
    gate, up = both[:, :128], both[:, 128:]
    hidden = gate / (1.0 + jnp.exp(-gate)) * up
    low = hidden.astype(BF16)
    for q in range(32):
        chunk = (q & 1) * 16 + (q >> 1)
        out_ref[q, :, :128] = low[chunk * 16 : (chunk + 1) * 16, :]
    n = ht_ref.shape[0]
    for half in range(2):
        at = pl.ds(pl.multiple_of((half ^ c) * 256, 256), 256)
        ht_ref[:, at] = hidden[half * 256 : (half + 1) * 256, :].T[:n].astype(BF16)
    part = lax.dot_general(high_ref[...], low, NT, preferred_element_type=F32)
    part += lax.dot_general(low_ref[...], low, NT, preferred_element_type=F32)
    part = part.astype(BF16)
    for q in range(32):
        out_ref[q, :, 128:640] = part[q * 16 : (q + 1) * 16, :]
        out_ref[q, :, 640:] = wh_ref[q * 16 : (q + 1) * 16, :]


def activate_call(pos, own_p, far_p, own_late, far_late, error, wh, n):
    return pl.pallas_call(
        activate,
        out_shape=(
            jax.ShapeDtypeStruct((32, 16, 640 + wh.shape[1]), BF16),
            jax.ShapeDtypeStruct((n, 512), BF16),
        ),
        in_specs=[SMEM] + [VMEM] * 7,
        out_specs=(VMEM, VMEM),
        scratch_shapes=[pltpu.VMEM((512, 256), F32)],
        name="activate",
    )(pos, own_p, far_p, own_late, far_late, *error, wh)


def choose(first_ref, arrived_ref, out_ref, wh_ref):
    total = jnp.sum(arrived_ref[:, :, 128:640].astype(F32), axis=0).astype(BF16)
    half = wh_ref.shape[1] // 2
    for core in range(2):
        sums = arrived_ref[core, :, 640:].astype(F32)
        for k in range(1, 16):
            sums += arrived_ref[2 * k + core, :, 640:].astype(F32)
        wh_ref[:, core * half : (core + 1) * half] = sums
    for k in range(8):
        for p in range(3):
            out_ref[k, :, p * 128 : (p + 1) * 128] = arrived_ref[first_ref[k] + p, :, :128]
        out_ref[k, :, 384:] = total


def choose_call(first, arrived):
    return pl.pallas_call(
        choose,
        out_shape=(
            jax.ShapeDtypeStruct((8, 16, 3 * 128 + 512), BF16),
            jax.ShapeDtypeStruct((16, 2 * (arrived.shape[2] - 640)), F32),
        ),
        in_specs=[SMEM, VMEM],
        out_specs=(VMEM, VMEM),
        name="choose",
    )(first, arrived)


def assemble(n, shift_ref, y_ref, chunk_ref, total_ref, line_ref):
    for p in range(3):
        for z in range(8):
            line_ref[:, pl.ds((p * 8 + z) * n, n)] = y_ref[z, :, p * 128 : p * 128 + n].astype(F32)
    width = chunk_ref.shape[2]
    d, c = shift_ref[0], shift_ref[1]
    base = pl.multiple_of((d // 128) * 128, 128)
    near = line_ref[:, pl.ds(base, width + 128)]
    turned = pltpu.roll(near, width + 128 - (d - base), 1)
    chunk = turned[:, :width].astype(BF16)
    for k in range(chunk_ref.shape[0]):
        chunk_ref[k] = chunk
    high, low = split_bf16(jnp.sum(y_ref[:, :, 384:].astype(F32), axis=0))
    for half in range(2):
        at = pl.ds(pl.multiple_of((half ^ c) * 256, 256), 256)
        total_ref[:16, at] = high[:, half * 256 : (half + 1) * 256]
        total_ref[16:, at] = low[:, half * 256 : (half + 1) * 256]


def assemble_call(pieces, shift, width, n):
    def kernel(*refs):
        assemble(n, *refs)

    return pl.pallas_call(
        kernel,
        out_shape=(
            jax.ShapeDtypeStruct((16, 16, width), BF16),
            jax.ShapeDtypeStruct((32, 512), BF16),
        ),
        in_specs=[SMEM, VMEM],
        out_specs=(VMEM, VMEM),
        scratch_shapes=[pltpu.VMEM((16, 24 * n), F32)],
        name="assemble",
    )(shift, pieces)


def slab_kernel(pos_ref, count_ref, *refs):
    pieces = refs[:9]
    near, far, total_ref, wh_ref, slab_ref, new_ref, grad_ref, panel_ref = refs[9:]
    z = pos_ref[4]
    n = pieces[0].shape[0]

    @pl.when(pl.program_id(0) == 0)
    def _():
        for piece, d, r0 in zip(pieces, (0, -1, 1, -2, 2, -3, 3, -4, 4), (0,) * 8 + (64,)):
            at = pl.multiple_of(((z + d + 8) % 8) * n + r0, 16)
            panel_ref[pl.ds(at, piece.shape[0]), :] = piece[...]

    scale = 1.0 / jnp.full((1, 1), count_ref[0].astype(F32), F32)
    gram = jnp.dot(panel_ref[:, :256], near[...], preferred_element_type=F32)
    gram += jnp.dot(panel_ref[:, 256:], far[...], preferred_element_type=F32)
    new_ref[...] = slab_ref[...] + gram * scale
    added = jnp.dot(total_ref[:, :256], near[...], preferred_element_type=F32)
    added += jnp.dot(total_ref[:, 256:], far[...], preferred_element_type=F32)
    grad_ref[...] = wh_ref[...] + (added[:16] + added[16:]) * scale


def slab_call(pos, count, pieces, near, far, total, wh, slab):
    rows, width = slab.shape
    step = 256

    def fixed(a):
        return pl.BlockSpec(a.shape, lambda k, *_: (0,) * a.ndim)

    def columns(r):
        return pl.BlockSpec((r, step), lambda k, *_: (0, k))

    return pl.pallas_call(
        slab_kernel,
        grid_spec=pltpu.PrefetchScalarGridSpec(
            num_scalar_prefetch=2,
            grid=(width // step,),
            in_specs=[fixed(p) for p in pieces]
            + [columns(256), columns(256), fixed(total), columns(16), columns(rows)],
            out_specs=(columns(rows), columns(16)),
            scratch_shapes=[pltpu.VMEM((rows, 512), BF16)],
        ),
        out_shape=(
            jax.ShapeDtypeStruct((rows, width), F32),
            jax.ShapeDtypeStruct((16, width), F32),
        ),
        name="slab",
    )(pos, count, *pieces, near, far, total, wh, slab)


def on_device(tokens, gate_weight, up_weight, hessian_slab, weight_error, slab_offset, token_count):
    xl, xh, y, c, z = (lax.axis_index(a) for a in CAL_GR_GC)
    pos = jnp.stack([xl, xh, y, c, z]).astype(jnp.int32)
    n = gate_weight.shape[1]
    width = hessian_slab.shape[1]
    quarter = tokens.shape[1] // 2

    mine = lax.dynamic_slice_in_dim(tokens, c * quarter, quarter, 1)
    theirs = core_swap(lax.dynamic_slice_in_dim(tokens, (1 - c) * quarter, quarter, 1))
    piece = jnp.concatenate([jnp.where(c == 0, mine, theirs), jnp.where(c == 0, theirs, mine)], 0)
    copies = jnp.broadcast_to(piece[None], (8, *piece.shape))
    copies, gate_weight, up_weight, weight_error = lax.optimization_barrier(
        (copies, gate_weight, up_weight, weight_error)
    )
    b0 = exchange(copies, "gc").reshape(64, quarter)
    gate_t, up_t = gate_weight.T, up_weight.T
    far_w = core_swap(
        jnp.stack(
            [
                lax.dynamic_slice_in_dim(w, (2 * f + 1 - c) * quarter, quarter, 1)
                for f in range(2)
                for w in (gate_t, up_t)
            ]
        )
    )

    error = jnp.pad(lax.dynamic_slice_in_dim(weight_error, z * n, n, 1), ((0, 0), (0, 128 - n)))
    wh = jnp.dot(weight_error, hessian_slab, precision=lax.Precision.HIGH, preferred_element_type=F32)
    b0, wh, far_w, high, low = lax.optimization_barrier((b0, wh, far_w, *split_bf16(error)))

    b1 = plane_permute(b0, 0, 1)
    b3 = plane_permute(b0, 0, 3)
    half = width // 2
    wh_far = core_swap(lax.dynamic_slice_in_dim(wh, (1 - c) * half, half, 1))
    wh = (lax.dynamic_slice_in_dim(wh, c * half, half, 1) + wh_far).astype(BF16)
    weights = weights_call(pos, gate_t, up_t, far_w.reshape(2, 2, n, quarter))
    b1, b3, weights = lax.optimization_barrier((b1, b3, weights))
    b2a = plane_permute(b1[:32], 0, 3)
    b2b = plane_permute(b3[32:], 0, 1)
    b2a, b2b, wh = lax.optimization_barrier((b2a, b2b, wh))
    sb = jnp.concatenate([b1, b3], 0)
    s3b = plane_permute(sb, 1, 3)
    s1b = plane_permute(sb, 1, 1)
    sa = jnp.concatenate([b0, b2a, b2b], 0)
    s1a = plane_permute(sa, 1, 1)
    s3a = plane_permute(sa, 1, 3)
    s2b = plane_permute(s3b, 1, 1)
    s2a = plane_permute(s1a, 1, 3)
    early = {(0, 0): [(0, 0)], (0, 1): [(1, 0)], (1, 0): [(2, 1), (3, 3)], (1, 1): [(4, 1), (5, 3)]}
    late = {(0, 0): [(0, 2)], (0, 1): [(1, 2)]}
    own_p, far_p = product_call(pos, (sa, sb, s1a, s3a, s1b, s3b), early, block_of, 8, weights)
    own_q, far_q = product_call(pos, (s2a, s2b), late, late_block, 4, weights)
    sent, hidden_t = activate_call(
        pos, own_p, core_swap(far_p), own_q, core_swap(far_q), (high, low), wh, n
    )

    f1, g1 = shift_z(hidden_t, 1), shift_z(hidden_t, -1)
    f2, g2 = shift_z(f1, 1), shift_z(g1, -1)
    f3, g3 = shift_z(f2, 1), shift_z(g2, -1)
    arrived = exchange(sent, CAL_GR)
    arrived, f3, g3 = lax.optimization_barrier((arrived, f3, g3))
    f4, g4 = shift_z(f3[:64], 1), shift_z(g3[64:], -1)
    panel_width = 8 * n
    starts = slab_offset[0] + jnp.arange(8, dtype=jnp.int32) * width
    wanted, wh = choose_call(jnp.minimum(starts // panel_width, 29), arrived)
    pieces = exchange(wanted, "gc")
    pieces, f4, g4 = lax.optimization_barrier((pieces, f4, g4))
    start = slab_offset[0] + z * width
    shift = start - jnp.minimum(start // panel_width, 29) * panel_width
    chunk, total = assemble_call(pieces, jnp.stack([shift, c]).astype(jnp.int32), width, n)
    near = exchange(chunk, PLANE).reshape(256, width)
    far = core_swap(near)
    return slab_call(
        pos, token_count, (hidden_t, f1, g1, f2, g2, f3, g3, f4, g4), near, far, total, wh, hessian_slab
    )


def solution(mesh):
    split = Mesh(
        mesh.devices.reshape(mesh.shape["cal"], 2, 4, 2, mesh.shape["gc"]),
        ("cal", "gr_0", "gr_1", "gr_2", "gc"),
    )

    return jax.shard_map(
        on_device,
        mesh=split,
        in_specs=(
            P(GR_GC, "cal"),
            P(None, CAL_GR_GC),
            P(None, CAL_GR_GC),
            P(CAL_GR, "gc"),
            P(None, CAL_GR),
            P(),
            P(),
        ),
        out_specs=(P(CAL_GR, "gc"), P(CAL_GR, "gc")),
        check_vma=False,
    )
```

profile of v0, /device:TPU:1, one launch (start us, length us, event | category | flops | bytes accessed | tf_op | source)
XLA Modules:
  0.0 152.9 jit_solution(5586693863578668578)
XLA Ops:
  0.7 0.9 constant_dynamic-slice_fusion.2
  1.5 3.2 %collective-permute-start = (bf16[4,2048]{1,0:T(4,128)(2,1)S(1)}, bf16[4,2048]{1,0:T(4,128)(2,1)S(1)}, u32[]{:S(2)}, u32[]{:S(2)}) collective-permute-start(bf16[4,2048]{1,0:T(4,128)(2,1)S(1)} %constant_dynamic-slice_fusion.2), channel_id=1, source_target_pairs={{0,8},{8,0},{1,9},{9,1},{2,10},{10,2},{3,11},{11,3},{4,12},{12,4},... | collective-permute-start | bytes 49160 | tf_op jit(solution)/shard_map/ppermute | solution.py:37
  4.7 0.8 collective-permute-done
  5.6 0.7 broadcast_select_fusion.1
  6.3 0.7 broadcast_in_dim.2
  7.0 1.6 %dynamic-slice_bitcast_fusion.2 = (bf16[1,112,2048]{2,1,0:T(8,128)(2,1)S(1)}, bf16[1,112,2048]{2,1,0:T(8,128)(2,1)S(1)}, bf16[1,112,2048]{2,1,0:T(8,128)(2,1)S(1)}, bf16[1,112,2048]{2,1,0:T(8,128)(2,1)S(1)}) fusion(bf16[8192,112]{0,1:T(8,128)(2,1)} %param.9, s32[]{:T(128)S(6)} %select_n.50, s32[]{:T(128)S(6)} %select_n.51, bf16[8192,112]{0,1:T(8,128)(2,1)} %param.8), kind=kLoop, calls=%fused_computation.4 | loop fusion | bytes 3670024 | tf_op jit(solution)/shard_map/stack | solution.py:308
  8.6 1.5 pad_maximum_fusion
  10.1 0.3 collective-permute-start.1
  10.5 6.5 %all-to-all-start = ((bf16[8,8,2048]{2,1,0:T(8,128)(2,1)}), bf16[8,8,2048]{2,1,0:T(8,128)(2,1)S(1)}, u32[]{:S(2)}, u32[]{:S(2)}) async-start(bf16[8,8,2048]{2,1,0:T(8,128)(2,1)} %broadcast_in_dim.2), calls=%async_computation | async-start | bytes 524288 | tf_op jit(solution)/shard_map/all_to_all | solution.py:45
  16.9 0.1 constant_dynamic-slice_fusion.1
  17.1 0.7 subtract_convert_fusion.low_ref
  17.8 0.7 pad_convert_fusion.high_ref
  18.5 6.8 %fusion.1 = f32[512,1024]{1,0:T(8,128)} fusion(f32[512,896]{1,0:T(8,128)S(1)} %copy-done, f32[896,1024]{1,0:T(8,128)} %refs_13_.1), kind=kOutput, calls=%fused_computation.22 | convolution fusion | flops 2818572288 | bytes 7602176 | tf_op jit(solution)/shard_map/dot_general | solution.py:318
  25.3 3.9 %all-to-all-done = bf16[8,8,2048]{2,1,0:T(8,128)(2,1)S(1)} async-done(((bf16[8,8,2048]{2,1,0:T(8,128)(2,1)}), bf16[8,8,2048]{2,1,0:T(8,128)(2,1)S(1)}, u32[]{:S(2)}, u32[]{:S(2)}) %all-to-all-start) | async-done | bytes 262176 | tf_op jit(solution)/shard_map/all_to_all | solution.py:45
  29.2 2.4 %constant_dynamic-slice_fusion = f32[512,512]{1,0:T(8,128)} fusion(f32[512,1024]{1,0:T(8,128)} %fusion.1, s32[]{:T(128)S(6)} %select_n.54), kind=kLoop, calls=%fused_computation.16 | loop fusion | bytes 2097156 | tf_op jit(solution)/shard_map/dynamic_slice | solution.py:324
  31.5 0.6 collective-permute-start.6
  32.1 2.7 %collective-permute-start.3 = (bf16[64,2048]{1,0:T(8,128)(2,1)S(1)}, bf16[64,2048]{1,0:T(8,128)(2,1)S(1)}, u32[]{:S(2)}, u32[]{:S(2)}) collective-permute-start(bf16[64,2048]{1,0:T(8,128)(2,1)S(1)} %bitcast.36), channel_id=1, source_target_pairs={{0,192},{8,56},{16,208},{24,40},{32,224},{40,24},{48,240},{56,8},{... | collective-permute-start | bytes 786440 | tf_op jit(solution)/shard_map/ppermute | solution.py:33
  34.9 0.6 stack.45.pos_ref
  35.5 4.3 %weights.1.refs_6_.refs_2_ = bf16[2,512,2048]{2,1,0:T(8,128)(2,1)} custom-call(s32[5]{0:T(128)} %stack.45.pos_ref, bf16[112,8192]{1,0:T(8,128)(2,1)} %bitcast.32, bf16[112,8192]{1,0:T(8,128)(2,1)} %bitcast.33, bf16[2,2,112,2048]{3,2,1,0:T(8,128)(2,1)} %bitcast.16.far), custom_call_target="tpu_custom_call" | custom-call | tf_op jit(solution)/shard_map/weights/pallas_call | solution.py:66
  39.8 0.6 collective-permute-done.2
  40.4 0.9 collective-permute-start.5
  41.3 0.5 collective-permute-start.4
  41.9 2.6 %collective-permute-start.10 = (bf16[128,2048]{1,0:T(8,128)(2,1)S(1)}, bf16[128,2048]{1,0:T(8,128)(2,1)S(1)}, u32[]{:S(2)}, u32[]{:S(2)}) collective-permute-start(bf16[128,2048]{1,0:T(8,128)(2,1)S(1)} %constant_dynamic-update-slice_fusion.3.refs_1_), channel_id=1, source_target_pairs={{0,48},{8,200},{16,32},{24,216},{32,16},{40,232},{48,0},{56,248},{... | collective-permute-start | bytes 1572872 | tf_op jit(solution)/shard_map/ppermute | solution.py:33
  44.5 2.5 %add_convert_fusion.wh_ref = bf16[512,512]{1,0:T(8,128)(2,1)} fusion(f32[512,512]{1,0:T(8,128)} %collective-permute-done.6, f32[512,1024]{1,0:T(8,128)} %fusion.1, s32[]{:T(128)S(6)} %select_n.53), kind=kLoop, calls=%fused_computation.1 | loop fusion | flops 524288 | bytes 2621444 | tf_op jit(solution)/shard_map/convert_element_type | solution.py:325
  47.0 0.7 collective-permute-start.7
  47.7 0.9 collective-permute-start.9
  48.6 1.9 %collective-permute-start.8 = (bf16[128,2048]{1,0:T(8,128)(2,1)S(1)}, bf16[128,2048]{1,0:T(8,128)(2,1)}, u32[]{:S(2)}, u32[]{:S(2)}) collective-permute-start(bf16[128,2048]{1,0:T(8,128)(2,1)S(1)} %constant_dynamic-update-slice_fusion.refs_0_), channel_id=1, source_target_pairs={{0,48},{8,200},{16,32},{24,216},{32,16},{40,232},{48,0},{56,248},{... | collective-permute-start | bytes 1572872 | tf_op jit(solution)/shard_map/ppermute | solution.py:33
  50.5 2.5 %collective-permute-done.10.refs_5_ = bf16[128,2048]{1,0:T(8,128)(2,1)S(1)} collective-permute-done((bf16[128,2048]{1,0:T(8,128)(2,1)S(1)}, bf16[128,2048]{1,0:T(8,128)(2,1)S(1)}, u32[]{:S(2)}, u32[]{:S(2)}) %collective-permute-start.10) | collective-permute-done | bytes 524320 | tf_op jit(solution)/shard_map/ppermute | solution.py:33
  52.9 2.6 %collective-permute-done.7.refs_2_ = bf16[128,2048]{1,0:T(8,128)(2,1)} collective-permute-done((bf16[128,2048]{1,0:T(8,128)(2,1)S(1)}, bf16[128,2048]{1,0:T(8,128)(2,1)}, u32[]{:S(2)}, u32[]{:S(2)}) %collective-permute-start.7) | collective-permute-done | bytes 524320 | tf_op jit(solution)/shard_map/ppermute | solution.py:33
  55.5 1.9 %collective-permute-start.12 = (bf16[128,2048]{1,0:T(8,128)(2,1)}, bf16[128,2048]{1,0:T(8,128)(2,1)}, u32[]{:S(2)}, u32[]{:S(2)}) collective-permute-start(bf16[128,2048]{1,0:T(8,128)(2,1)} %collective-permute-done.7.refs_2_), channel_id=1, source_target_pairs={{0,48},{8,200},{16,32},{24,216},{32,16},{40,232},{48,0},{56,248},{... | collective-permute-start | bytes 1572872 | tf_op jit(solution)/shard_map/ppermute | solution.py:33
  57.4 3.7 %collective-permute-done.9.refs_4_ = bf16[128,2048]{1,0:T(8,128)(2,1)S(1)} collective-permute-done((bf16[128,2048]{1,0:T(8,128)(2,1)S(1)}, bf16[128,2048]{1,0:T(8,128)(2,1)S(1)}, u32[]{:S(2)}, u32[]{:S(2)}) %collective-permute-start.9) | collective-permute-done | bytes 524320 | tf_op jit(solution)/shard_map/ppermute | solution.py:33
  61.2 0.8 copy-done.9
  62.0 6.8 %products.2 = (f32[512,256]{1,0:T(8,128)}, f32[512,256]{1,0:T(8,128)}) custom-call(s32[5]{0:T(128)} %stack.45.pos_ref, bf16[128,2048]{1,0:T(8,128)(2,1)} %copy-done.3, bf16[128,2048]{1,0:T(8,128)(2,1)} %copy-done.4, bf16[128,2048]{1,0:T(8,128)(2,1)} %collective-permute-done.7.refs_2_, bf16[128,2048]{1,0:T(8,128)(2,1)} %collective-permute-done.8.refs_3_, ...), custom_call_target="tpu_custom_call" | custom-call | flops 1610612736 | bytes 8388608 | tf_op jit(solution)/shard_map/products/pallas_call | solution.py:120
  68.7 3.3 %collective-permute-start.11 = (f32[512,256]{1,0:T(8,128)}, f32[512,256]{1,0:T(8,128)S(1)}, u32[]{:S(2)}, u32[]{:S(2)}) collective-permute-start(f32[512,256]{1,0:T(8,128)} %get-tuple-element.46), channel_id=1, source_target_pairs={{0,8},{8,0},{1,9},{9,1},{2,10},{10,2},{3,11},{11,3},{4,12},{12,4},... | collective-permute-start | bytes 1572872 | tf_op jit(solution)/shard_map/ppermute | solution.py:37
  72.0 4.9 %products.3 = (f32[256,256]{1,0:T(8,128)}, f32[256,256]{1,0:T(8,128)}) custom-call(s32[5]{0:T(128)} %stack.45.pos_ref, bf16[128,2048]{1,0:T(8,128)(2,1)} %collective-permute-done.12.refs_0_, bf16[128,2048]{1,0:T(8,128)(2,1)} %collective-permute-done.13.refs_1_, bf16[2,512,2048]{2,1,0:T(8,128)(2,1)} %weights.1.refs_6_.refs_2_), custom_call_target="tpu_custom_call" | custom-call | flops 536870912 | bytes 8388608 | tf_op jit(solution)/shard_map/products/pallas_call | solution.py:120
  77.0 1.7 %collective-permute-done.14.far_late = f32[256,256]{1,0:T(8,128)S(1)} collective-permute-done((f32[256,256]{1,0:T(8,128)}, f32[256,256]{1,0:T(8,128)S(1)}, u32[]{:S(2)}, u32[]{:S(2)}) %collective-permute-start.14) | collective-permute-done | bytes 262176 | tf_op jit(solution)/shard_map/ppermute | solution.py:37
  78.7 0.7 copy-done.11
  79.4 3.2 %activate.1 = (bf16[32,16,1152]{2,1,0:T(8,128)(2,1)}, bf16[112,512]{1,0:T(8,128)(2,1)}) custom-call(s32[5]{0:T(128)} %stack.45.pos_ref, f32[512,256]{1,0:T(8,128)} %get-tuple-element.45.own_ref, f32[512,256]{1,0:T(8,128)} %copy-done.6, f32[256,256]{1,0:T(8,128)} %get-tuple-element.47.own_late, f32[256,256]{1,0:T(8,128)} %copy-done.11, ...), custom_call_target="tpu_custom_call" | custom-call | tf_op jit(solution)/shard_map/activate/pallas_call | solution.py:166
  82.7 5.3 %all-to-all-start.1 = ((bf16[32,16,1152]{2,1,0:T(8,128)(2,1)}), bf16[32,16,1152]{2,1,0:T(8,128)(2,1)S(1)}, u32[]{:S(2)}, u32[]{:S(2)}) async-start(bf16[32,16,1152]{2,1,0:T(8,128)(2,1)} %get-tuple-element.53), calls=%async_computation.1 | async-start | bytes 2359296 | tf_op jit(solution)/shard_map/all_to_all | solution.py:45
  87.9 0.1 collective-permute-start.16
  88.0 1.5 collective-permute-start.15
  89.5 3.0 %collective-permute-done.16.refs_2_ = bf16[112,512]{1,0:T(8,128)(2,1)S(1)} collective-permute-done((bf16[112,512]{1,0:T(8,128)(2,1)S(1)}, bf16[112,512]{1,0:T(8,128)(2,1)S(1)}, u32[]{:S(2)}, u32[]{:S(2)}) %collective-permute-start.16) | collective-permute-done | bytes 114720 | tf_op jit(solution)/shard_map/ppermute | solution.py:41
  92.5 1.5 collective-permute-start.18
  94.0 2.4 %collective-permute-done.18.refs_4_ = bf16[112,512]{1,0:T(8,128)(2,1)S(1)} collective-permute-done((bf16[112,512]{1,0:T(8,128)(2,1)S(1)}, bf16[112,512]{1,0:T(8,128)(2,1)S(1)}, u32[]{:S(2)}, u32[]{:S(2)}) %collective-permute-start.18) | collective-permute-done | bytes 114720 | tf_op jit(solution)/shard_map/ppermute | solution.py:41
  96.4 2.7 %collective-permute-start.20 = (bf16[112,512]{1,0:T(8,128)(2,1)S(1)}, bf16[112,512]{1,0:T(8,128)(2,1)S(1)}, u32[]{:S(2)}, u32[]{:S(2)}) collective-permute-start(bf16[112,512]{1,0:T(8,128)(2,1)S(1)} %collective-permute-done.18.refs_4_), channel_id=1, source_target_pairs={{0,7},{1,0},{2,1},{3,2},{4,3},{5,4},{6,5},{7,6},{8,15},{9,8},{10,9... | collective-permute-start | bytes 344072 | tf_op jit(solution)/shard_map/ppermute | solution.py:41
  99.9 0.6 fusion.first_ref
  100.4 0.5 collective-permute-done.20.refs_6_
  100.9 3.4 %collective-permute-done.19.refs_5_ = bf16[112,512]{1,0:T(8,128)(2,1)S(1)} collective-permute-done((bf16[112,512]{1,0:T(8,128)(2,1)S(1)}, bf16[112,512]{1,0:T(8,128)(2,1)S(1)}, u32[]{:S(2)}, u32[]{:S(2)}) %collective-permute-start.19) | collective-permute-done | bytes 114720 | tf_op jit(solution)/shard_map/ppermute | solution.py:41
  104.4 2.3 %all-to-all-done.1.arrived_ref = bf16[32,16,1152]{2,1,0:T(8,128)(2,1)S(1)} async-done(((bf16[32,16,1152]{2,1,0:T(8,128)(2,1)}), bf16[32,16,1152]{2,1,0:T(8,128)(2,1)S(1)}, u32[]{:S(2)}, u32[]{:S(2)}) %all-to-all-start.1) | async-done | bytes 1179680 | tf_op jit(solution)/shard_map/all_to_all | solution.py:45
  106.6 1.0 copy-done.1
  107.7 2.1 %choose.1 = (bf16[8,16,896]{2,1,0:T(8,128)(2,1)}, f32[16,1024]{1,0:T(8,128)}) custom-call(s32[8]{0:T(128)} %fusion.first_ref, bf16[32,16,1152]{2,1,0:T(8,128)(2,1)} %copy-done.1), custom_call_target="tpu_custom_call" | custom-call | tf_op jit(solution)/shard_map/choose/pallas_call | solution.py:194
  109.8 3.4 %all-to-all-start.2 = ((bf16[8,16,896]{2,1,0:T(8,128)(2,1)}), bf16[8,16,896]{2,1,0:T(8,128)(2,1)S(1)}, u32[]{:S(2)}, u32[]{:S(2)}) async-start(bf16[8,16,896]{2,1,0:T(8,128)(2,1)} %get-tuple-element.57), calls=%async_computation.2 | async-start | bytes 458752 | tf_op jit(solution)/shard_map/all_to_all | solution.py:45
  113.2 2.6 %collective-permute-start.22 = (bf16[48,512]{1,0:T(8,128)(2,1)S(1)}, bf16[48,512]{1,0:T(8,128)(2,1)S(1)}, u32[]{:S(2)}, u32[]{:S(2)}) collective-permute-start(bf16[48,512]{1,0:T(8,128)(2,1)S(1)} %slice.15), channel_id=1, source_target_pairs={{0,7},{1,0},{2,1},{3,2},{4,3},{5,4},{6,5},{7,6},{8,15},{9,8},{10,9... | collective-permute-start | bytes 147464 | tf_op jit(solution)/shard_map/ppermute | solution.py:41
  115.9 0.6 pad_add_fusion.refs_0_
  116.5 2.6 %collective-permute-done.22.refs_8_ = bf16[48,512]{1,0:T(8,128)(2,1)S(1)} collective-permute-done((bf16[48,512]{1,0:T(8,128)(2,1)S(1)}, bf16[48,512]{1,0:T(8,128)(2,1)S(1)}, u32[]{:S(2)}, u32[]{:S(2)}) %collective-permute-start.22) | collective-permute-done | bytes 49184 | tf_op jit(solution)/shard_map/ppermute | solution.py:41
  119.1 3.0 %collective-permute-done.21.refs_7_ = bf16[64,512]{1,0:T(8,128)(2,1)S(1)} collective-permute-done((bf16[64,512]{1,0:T(8,128)(2,1)S(1)}, bf16[64,512]{1,0:T(8,128)(2,1)S(1)}, u32[]{:S(2)}, u32[]{:S(2)}) %collective-permute-start.21) | collective-permute-done | bytes 65568 | tf_op jit(solution)/shard_map/ppermute | solution.py:41
  122.1 0.5 all-to-all-done.2.refs_1_
  122.6 0.7 copy-done.5
  123.3 2.0 %assemble.1 = (bf16[16,16,1024]{2,1,0:T(8,128)(2,1)}, bf16[32,512]{1,0:T(8,128)(2,1)}) custom-call(s32[2]{0:T(128)} %pad_add_fusion.refs_0_, bf16[8,16,896]{2,1,0:T(8,128)(2,1)} %copy-done.5), custom_call_target="tpu_custom_call" | custom-call | tf_op jit(solution)/shard_map/assemble/pallas_call | solution.py:229
  125.3 12.1 %all_to_all.20 = bf16[16,16,1024]{2,1,0:T(8,128)(2,1)S(1)} all-to-all(bf16[16,16,1024]{2,1,0:T(8,128)(2,1)} %get-tuple-element.61), channel_id=1, replica_groups=mesh['cal'=2,'gr_0'=2,'gr_1'=4,'gr_2'=2,'gc'=8] {'cal','gr_0','gr_1'}, dimensions={0} | all-to-all | bytes 1048576 | tf_op jit(solution)/shard_map/all_to_all | solution.py:45
  137.4 6.4 %collective-permute-start.23 = (bf16[256,1024]{1,0:T(8,128)(2,1)S(1)}, bf16[256,1024]{1,0:T(8,128)(2,1)S(1)}, u32[]{:S(2)}, u32[]{:S(2)}) collective-permute-start(bf16[256,1024]{1,0:T(8,128)(2,1)S(1)} %bitcast.34), channel_id=1, source_target_pairs={{0,8},{8,0},{1,9},{9,1},{2,10},{10,2},{3,11},{11,3},{4,12},{12,4},... | collective-permute-start | bytes 1572872 | tf_op jit(solution)/shard_map/ppermute | solution.py:37
  144.4 0.9 collective-permute-done.23.refs_10_
  145.4 0.7 copy-done.7
  146.1 6.7 %slab.1 = (f32[896,1024]{1,0:T(8,128)}, f32[16,1024]{1,0:T(8,128)}) custom-call(s32[5]{0:T(128)} %stack.45.pos_ref, s32[1]{0:T(128)S(6)} %copy.13.count_ref, bf16[112,512]{1,0:T(8,128)(2,1)} %get-tuple-element.52.refs_0_, bf16[112,512]{1,0:T(8,128)(2,1)} %copy-done.15, bf16[112,512]{1,0:T(8,128)(2,1)} %copy-done.14, bf16[112,512]{1,0:T(8,128)(2,1)} %copy-done.17, ...), custom_call_target="tpu_custom_call" | custom-call | tf_op jit(solution)/shard_map/slab/pallas_call | solution.py:273
  (62 shorter events, 0.3 us)
Async XLA Ops:
  0.6 16.3 %copy-start = (f32[512,896]{1,0:T(8,128)S(1)}, f32[512,896]{1,0:T(8,128)}, u32[]{:S(2)}) copy-start(f32[512,896]{1,0:T(8,128)} %param.11) | copy-start | bytes 5505028
  1.5 4.0 %collective-permute-start = (bf16[4,2048]{1,0:T(4,128)(2,1)S(1)}, bf16[4,2048]{1,0:T(4,128)(2,1)S(1)}, u32[]{:S(2)}, u32[]{:S(2)}) collective-permute-start(bf16[4,2048]{1,0:T(4,128)(2,1)S(1)} %constant_dynamic-slice_fusion.2), channel_id=1, source_target_pairs={{0,8},{8,0},{1,9},{9,1},{2,10},{10,2},{3,11},{11,3},{4,12},{12,4},... | collective-permute-start | bytes 49160 | tf_op jit(solution)/shard_map/ppermute | solution.py:37
  10.1 19.1 %collective-permute-start.1 = (bf16[4,112,2048]{2,1,0:T(8,128)(2,1)}, bf16[4,112,2048]{2,1,0:T(8,128)(2,1)}, u32[]{:S(2)}, u32[]{:S(2)}) collective-permute-start(bf16[4,112,2048]{2,1,0:T(8,128)(2,1)} %pad_maximum_fusion), channel_id=1, source_target_pairs={{0,8},{8,0},{1,9},{9,1},{2,10},{10,2},{3,11},{11,3},{4,12},{12,4},... | collective-permute-start | bytes 5505032 | tf_op jit(solution)/shard_map/ppermute | solution.py:37
  10.5 18.7 %all-to-all-start = ((bf16[8,8,2048]{2,1,0:T(8,128)(2,1)}), bf16[8,8,2048]{2,1,0:T(8,128)(2,1)S(1)}, u32[]{:S(2)}, u32[]{:S(2)}) async-start(bf16[8,8,2048]{2,1,0:T(8,128)(2,1)} %broadcast_in_dim.2), calls=%async_computation | async-start | bytes 524288 | tf_op jit(solution)/shard_map/all_to_all | solution.py:45
  31.5 12.9 %collective-permute-start.6 = (f32[512,512]{1,0:T(8,128)}, f32[512,512]{1,0:T(8,128)}, u32[]{:S(2)}, u32[]{:S(2)}) collective-permute-start(f32[512,512]{1,0:T(8,128)} %constant_dynamic-slice_fusion), channel_id=1, source_target_pairs={{0,8},{8,0},{1,9},{9,1},{2,10},{10,2},{3,11},{11,3},{4,12},{12,4},... | collective-permute-start | bytes 3145736 | tf_op jit(solution)/shard_map/ppermute | solution.py:37
  32.1 7.6 %collective-permute-start.3 = (bf16[64,2048]{1,0:T(8,128)(2,1)S(1)}, bf16[64,2048]{1,0:T(8,128)(2,1)S(1)}, u32[]{:S(2)}, u32[]{:S(2)}) collective-permute-start(bf16[64,2048]{1,0:T(8,128)(2,1)S(1)} %bitcast.36), channel_id=1, source_target_pairs={{0,192},{8,56},{16,208},{24,40},{32,224},{40,24},{48,240},{56,8},{... | collective-permute-start | bytes 786440 | tf_op jit(solution)/shard_map/ppermute | solution.py:33
  34.9 5.5 %collective-permute-start.2 = (bf16[64,2048]{1,0:T(8,128)(2,1)S(1)}, bf16[64,2048]{1,0:T(8,128)(2,1)S(1)}, u32[]{:S(2)}, u32[]{:S(2)}) collective-permute-start(bf16[64,2048]{1,0:T(8,128)(2,1)S(1)} %bitcast.37), channel_id=1, source_target_pairs={{0,128},{8,24},{16,144},{24,8},{32,160},{40,56},{48,176},{56,40},{... | collective-permute-start | bytes 786440 | tf_op jit(solution)/shard_map/ppermute | solution.py:33
  40.4 6.5 %collective-permute-start.5 = (bf16[32,2048]{1,0:T(8,128)(2,1)S(1)}, bf16[32,2048]{1,0:T(8,128)(2,1)S(1)}, u32[]{:S(2)}, u32[]{:S(2)}) collective-permute-start(bf16[32,2048]{1,0:T(8,128)(2,1)S(1)} %slice.13), channel_id=1, source_target_pairs={{0,128},{8,24},{16,144},{24,8},{32,160},{40,56},{48,176},{56,40},{... | collective-permute-start | bytes 393224 | tf_op jit(solution)/shard_map/ppermute | solution.py:33
  41.3 5.6 %collective-permute-start.4 = (bf16[32,2048]{1,0:T(8,128)(2,1)S(1)}, bf16[32,2048]{1,0:T(8,128)(2,1)S(1)}, u32[]{:S(2)}, u32[]{:S(2)}) collective-permute-start(bf16[32,2048]{1,0:T(8,128)(2,1)S(1)} %slice.12), channel_id=1, source_target_pairs={{0,192},{8,56},{16,208},{24,40},{32,224},{40,24},{48,240},{56,8},{... | collective-permute-start | bytes 393224 | tf_op jit(solution)/shard_map/ppermute | solution.py:33
  41.9 20.1 %copy-start.4 = (bf16[128,2048]{1,0:T(8,128)(2,1)}, bf16[128,2048]{1,0:T(8,128)(2,1)S(1)}, u32[]{:S(2)}) copy-start(bf16[128,2048]{1,0:T(8,128)(2,1)S(1)} %constant_dynamic-update-slice_fusion.3.refs_1_) | copy-start | bytes 1572868
  41.9 11.0 %collective-permute-start.10 = (bf16[128,2048]{1,0:T(8,128)(2,1)S(1)}, bf16[128,2048]{1,0:T(8,128)(2,1)S(1)}, u32[]{:S(2)}, u32[]{:S(2)}) collective-permute-start(bf16[128,2048]{1,0:T(8,128)(2,1)S(1)} %constant_dynamic-update-slice_fusion.3.refs_1_), channel_id=1, source_target_pairs={{0,48},{8,200},{16,32},{24,216},{32,16},{40,232},{48,0},{56,248},{... | collective-permute-start | bytes 1572872 | tf_op jit(solution)/shard_map/ppermute | solution.py:33
  47.0 15.0 %copy-start.3 = (bf16[128,2048]{1,0:T(8,128)(2,1)}, bf16[128,2048]{1,0:T(8,128)(2,1)S(1)}, u32[]{:S(2)}) copy-start(bf16[128,2048]{1,0:T(8,128)(2,1)S(1)} %constant_dynamic-update-slice_fusion.refs_0_) | copy-start | bytes 1572868
  47.0 8.5 %collective-permute-start.7 = (bf16[128,2048]{1,0:T(8,128)(2,1)S(1)}, bf16[128,2048]{1,0:T(8,128)(2,1)}, u32[]{:S(2)}, u32[]{:S(2)}) collective-permute-start(bf16[128,2048]{1,0:T(8,128)(2,1)S(1)} %constant_dynamic-update-slice_fusion.refs_0_), channel_id=1, source_target_pairs={{0,16},{8,136},{16,0},{24,152},{32,48},{40,168},{48,32},{56,184},{... | collective-permute-start | bytes 1572872 | tf_op jit(solution)/shard_map/ppermute | solution.py:33
  47.7 13.4 %collective-permute-start.9 = (bf16[128,2048]{1,0:T(8,128)(2,1)S(1)}, bf16[128,2048]{1,0:T(8,128)(2,1)S(1)}, u32[]{:S(2)}, u32[]{:S(2)}) collective-permute-start(bf16[128,2048]{1,0:T(8,128)(2,1)S(1)} %constant_dynamic-update-slice_fusion.3.refs_1_), channel_id=1, source_target_pairs={{0,16},{8,136},{16,0},{24,152},{32,48},{40,168},{48,32},{56,184},{... | collective-permute-start | bytes 1572872 | tf_op jit(solution)/shard_map/ppermute | solution.py:33
  48.6 13.4 %collective-permute-start.8 = (bf16[128,2048]{1,0:T(8,128)(2,1)S(1)}, bf16[128,2048]{1,0:T(8,128)(2,1)}, u32[]{:S(2)}, u32[]{:S(2)}) collective-permute-start(bf16[128,2048]{1,0:T(8,128)(2,1)S(1)} %constant_dynamic-update-slice_fusion.refs_0_), channel_id=1, source_target_pairs={{0,48},{8,200},{16,32},{24,216},{32,16},{40,232},{48,0},{56,248},{... | collective-permute-start | bytes 1572872 | tf_op jit(solution)/shard_map/ppermute | solution.py:33
  52.9 9.1 %copy-start.8 = (bf16[128,2048]{1,0:T(8,128)(2,1)}, bf16[128,2048]{1,0:T(8,128)(2,1)S(1)}, u32[]{:S(2)}) copy-start(bf16[128,2048]{1,0:T(8,128)(2,1)S(1)} %collective-permute-done.10.refs_5_) | copy-start | bytes 1572868
  52.9 19.1 %collective-permute-start.13 = (bf16[128,2048]{1,0:T(8,128)(2,1)S(1)}, bf16[128,2048]{1,0:T(8,128)(2,1)}, u32[]{:S(2)}, u32[]{:S(2)}) collective-permute-start(bf16[128,2048]{1,0:T(8,128)(2,1)S(1)} %collective-permute-done.10.refs_5_), channel_id=1, source_target_pairs={{0,16},{8,136},{16,0},{24,152},{32,48},{40,168},{48,32},{56,184},{... | collective-permute-start | bytes 1572872 | tf_op jit(solution)/shard_map/ppermute | solution.py:33
  55.5 16.5 %collective-permute-start.12 = (bf16[128,2048]{1,0:T(8,128)(2,1)}, bf16[128,2048]{1,0:T(8,128)(2,1)}, u32[]{:S(2)}, u32[]{:S(2)}) collective-permute-start(bf16[128,2048]{1,0:T(8,128)(2,1)} %collective-permute-done.7.refs_2_), channel_id=1, source_target_pairs={{0,48},{8,200},{16,32},{24,216},{32,16},{40,232},{48,0},{56,248},{... | collective-permute-start | bytes 1572872 | tf_op jit(solution)/shard_map/ppermute | solution.py:33
  61.2 0.8 copy-start.9
  68.7 8.3 %collective-permute-start.11 = (f32[512,256]{1,0:T(8,128)}, f32[512,256]{1,0:T(8,128)S(1)}, u32[]{:S(2)}, u32[]{:S(2)}) collective-permute-start(f32[512,256]{1,0:T(8,128)} %get-tuple-element.46), channel_id=1, source_target_pairs={{0,8},{8,0},{1,9},{9,1},{2,10},{10,2},{3,11},{11,3},{4,12},{12,4},... | collective-permute-start | bytes 1572872 | tf_op jit(solution)/shard_map/ppermute | solution.py:37
  77.0 1.7 %collective-permute-start.14 = (f32[256,256]{1,0:T(8,128)}, f32[256,256]{1,0:T(8,128)S(1)}, u32[]{:S(2)}, u32[]{:S(2)}) collective-permute-start(f32[256,256]{1,0:T(8,128)} %get-tuple-element.48), channel_id=1, source_target_pairs={{0,8},{8,0},{1,9},{9,1},{2,10},{10,2},{3,11},{11,3},{4,12},{12,4},... | collective-permute-start | bytes 786440 | tf_op jit(solution)/shard_map/ppermute | solution.py:37
  77.0 1.7 %copy-start.6 = (f32[512,256]{1,0:T(8,128)}, f32[512,256]{1,0:T(8,128)S(1)}, u32[]{:S(2)}) copy-start(f32[512,256]{1,0:T(8,128)S(1)} %collective-permute-done.11.far_ref) | copy-start | bytes 1572868
  78.7 0.7 copy-start.11
  82.7 5.3 %copy-start.13 = (bf16[112,512]{1,0:T(8,128)(2,1)S(1)}, bf16[112,512]{1,0:T(8,128)(2,1)}, u32[]{:S(2)}) copy-start(bf16[112,512]{1,0:T(8,128)(2,1)} %get-tuple-element.52.refs_0_) | copy-start | bytes 344068
  82.7 24.0 %all-to-all-start.1 = ((bf16[32,16,1152]{2,1,0:T(8,128)(2,1)}), bf16[32,16,1152]{2,1,0:T(8,128)(2,1)S(1)}, u32[]{:S(2)}, u32[]{:S(2)}) async-start(bf16[32,16,1152]{2,1,0:T(8,128)(2,1)} %get-tuple-element.53), calls=%async_computation.1 | async-start | bytes 2359296 | tf_op jit(solution)/shard_map/all_to_all | solution.py:45
  87.9 4.5 %collective-permute-start.16 = (bf16[112,512]{1,0:T(8,128)(2,1)S(1)}, bf16[112,512]{1,0:T(8,128)(2,1)S(1)}, u32[]{:S(2)}, u32[]{:S(2)}) collective-permute-start(bf16[112,512]{1,0:T(8,128)(2,1)S(1)} %copy-done.13), channel_id=1, source_target_pairs={{0,7},{1,0},{2,1},{3,2},{4,3},{5,4},{6,5},{7,6},{8,15},{9,8},{10,9... | collective-permute-start | bytes 344072 | tf_op jit(solution)/shard_map/ppermute | solution.py:41
  88.0 6.0 %collective-permute-start.15 = (bf16[112,512]{1,0:T(8,128)(2,1)S(1)}, bf16[112,512]{1,0:T(8,128)(2,1)S(1)}, u32[]{:S(2)}, u32[]{:S(2)}) collective-permute-start(bf16[112,512]{1,0:T(8,128)(2,1)S(1)} %copy-done.13), channel_id=1, source_target_pairs={{0,1},{1,2},{2,3},{3,4},{4,5},{5,6},{6,7},{7,0},{8,9},{9,10},{10,1... | collective-permute-start | bytes 344072 | tf_op jit(solution)/shard_map/ppermute | solution.py:41
  92.5 52.8 %copy-start.14 = (bf16[112,512]{1,0:T(8,128)(2,1)}, bf16[112,512]{1,0:T(8,128)(2,1)S(1)}, u32[]{:S(2)}) copy-start(bf16[112,512]{1,0:T(8,128)(2,1)S(1)} %collective-permute-done.16.refs_2_) | copy-start | bytes 344068
  92.5 3.9 %collective-permute-start.18 = (bf16[112,512]{1,0:T(8,128)(2,1)S(1)}, bf16[112,512]{1,0:T(8,128)(2,1)S(1)}, u32[]{:S(2)}, u32[]{:S(2)}) collective-permute-start(bf16[112,512]{1,0:T(8,128)(2,1)S(1)} %collective-permute-done.16.refs_2_), channel_id=1, source_target_pairs={{0,7},{1,0},{2,1},{3,2},{4,3},{5,4},{6,5},{7,6},{8,15},{9,8},{10,9... | collective-permute-start | bytes 344072 | tf_op jit(solution)/shard_map/ppermute | solution.py:41
  94.0 5.1 %copy-start.15 = (bf16[112,512]{1,0:T(8,128)(2,1)}, bf16[112,512]{1,0:T(8,128)(2,1)S(1)}, u32[]{:S(2)}) copy-start(bf16[112,512]{1,0:T(8,128)(2,1)S(1)} %collective-permute-done.15.refs_1_) | copy-start | bytes 344068
  94.0 5.2 %collective-permute-start.17 = (bf16[112,512]{1,0:T(8,128)(2,1)S(1)}, bf16[112,512]{1,0:T(8,128)(2,1)S(1)}, u32[]{:S(2)}, u32[]{:S(2)}) collective-permute-start(bf16[112,512]{1,0:T(8,128)(2,1)S(1)} %collective-permute-done.15.refs_1_), channel_id=1, source_target_pairs={{0,1},{1,2},{2,3},{3,4},{4,5},{5,6},{6,7},{7,0},{8,9},{9,10},{10,1... | collective-permute-start | bytes 344072 | tf_op jit(solution)/shard_map/ppermute | solution.py:41
  96.4 4.5 %copy-start.16 = (bf16[112,512]{1,0:T(8,128)(2,1)}, bf16[112,512]{1,0:T(8,128)(2,1)S(1)}, u32[]{:S(2)}) copy-start(bf16[112,512]{1,0:T(8,128)(2,1)S(1)} %collective-permute-done.18.refs_4_) | copy-start | bytes 344068
  96.4 4.5 %collective-permute-start.20 = (bf16[112,512]{1,0:T(8,128)(2,1)S(1)}, bf16[112,512]{1,0:T(8,128)(2,1)S(1)}, u32[]{:S(2)}, u32[]{:S(2)}) collective-permute-start(bf16[112,512]{1,0:T(8,128)(2,1)S(1)} %collective-permute-done.18.refs_4_), channel_id=1, source_target_pairs={{0,7},{1,0},{2,1},{3,2},{4,3},{5,4},{6,5},{7,6},{8,15},{9,8},{10,9... | collective-permute-start | bytes 344072 | tf_op jit(solution)/shard_map/ppermute | solution.py:41
  99.1 46.2 %copy-start.17 = (bf16[112,512]{1,0:T(8,128)(2,1)}, bf16[112,512]{1,0:T(8,128)(2,1)S(1)}, u32[]{:S(2)}) copy-start(bf16[112,512]{1,0:T(8,128)(2,1)S(1)} %collective-permute-done.17.refs_3_) | copy-start | bytes 344068
  99.1 5.2 %collective-permute-start.19 = (bf16[112,512]{1,0:T(8,128)(2,1)S(1)}, bf16[112,512]{1,0:T(8,128)(2,1)S(1)}, u32[]{:S(2)}, u32[]{:S(2)}) collective-permute-start(bf16[112,512]{1,0:T(8,128)(2,1)S(1)} %collective-permute-done.17.refs_3_), channel_id=1, source_target_pairs={{0,1},{1,2},{2,3},{3,4},{4,5},{5,6},{6,7},{7,0},{8,9},{9,10},{10,1... | collective-permute-start | bytes 344072 | tf_op jit(solution)/shard_map/ppermute | solution.py:41
  100.9 44.4 %copy-start.12 = (bf16[112,512]{1,0:T(8,128)(2,1)}, bf16[112,512]{1,0:T(8,128)(2,1)S(1)}, u32[]{:S(2)}) copy-start(bf16[112,512]{1,0:T(8,128)(2,1)S(1)} %collective-permute-done.20.refs_6_) | copy-start | bytes 344068
  104.4 40.9 %copy-start.10 = (bf16[112,512]{1,0:T(8,128)(2,1)}, bf16[112,512]{1,0:T(8,128)(2,1)S(1)}, u32[]{:S(2)}) copy-start(bf16[112,512]{1,0:T(8,128)(2,1)S(1)} %collective-permute-done.19.refs_5_) | copy-start | bytes 344068
  106.6 1.0 copy-start.1
  109.8 12.9 %all-to-all-start.2 = ((bf16[8,16,896]{2,1,0:T(8,128)(2,1)}), bf16[8,16,896]{2,1,0:T(8,128)(2,1)S(1)}, u32[]{:S(2)}, u32[]{:S(2)}) async-start(bf16[8,16,896]{2,1,0:T(8,128)(2,1)} %get-tuple-element.57), calls=%async_computation.2 | async-start | bytes 458752 | tf_op jit(solution)/shard_map/all_to_all | solution.py:45
  113.2 5.9 %collective-permute-start.22 = (bf16[48,512]{1,0:T(8,128)(2,1)S(1)}, bf16[48,512]{1,0:T(8,128)(2,1)S(1)}, u32[]{:S(2)}, u32[]{:S(2)}) collective-permute-start(bf16[48,512]{1,0:T(8,128)(2,1)S(1)} %slice.15), channel_id=1, source_target_pairs={{0,7},{1,0},{2,1},{3,2},{4,3},{5,4},{6,5},{7,6},{8,15},{9,8},{10,9... | collective-permute-start | bytes 147464 | tf_op jit(solution)/shard_map/ppermute | solution.py:41
  115.9 6.2 %collective-permute-start.21 = (bf16[64,512]{1,0:T(8,128)(2,1)S(1)}, bf16[64,512]{1,0:T(8,128)(2,1)S(1)}, u32[]{:S(2)}, u32[]{:S(2)}) collective-permute-start(bf16[64,512]{1,0:T(8,128)(2,1)S(1)} %slice.14), channel_id=1, source_target_pairs={{0,1},{1,2},{2,3},{3,4},{4,5},{5,6},{6,7},{7,0},{8,9},{9,10},{10,1... | collective-permute-start | bytes 196616 | tf_op jit(solution)/shard_map/ppermute | solution.py:41
  119.1 26.2 %copy-start.19 = (bf16[48,512]{1,0:T(8,128)(2,1)}, bf16[48,512]{1,0:T(8,128)(2,1)S(1)}, u32[]{:S(2)}) copy-start(bf16[48,512]{1,0:T(8,128)(2,1)S(1)} %collective-permute-done.22.refs_8_) | copy-start | bytes 147460
  122.1 23.2 %copy-start.18 = (bf16[64,512]{1,0:T(8,128)(2,1)}, bf16[64,512]{1,0:T(8,128)(2,1)S(1)}, u32[]{:S(2)}) copy-start(bf16[64,512]{1,0:T(8,128)(2,1)S(1)} %collective-permute-done.21.refs_7_) | copy-start | bytes 196612
  122.6 0.7 copy-start.5
  137.4 7.9 %copy-start.2 = (bf16[16,16,1024]{2,1,0:T(8,128)(2,1)}, bf16[16,16,1024]{2,1,0:T(8,128)(2,1)S(1)}, u32[]{:S(2)}) copy-start(bf16[16,16,1024]{2,1,0:T(8,128)(2,1)S(1)} %all_to_all.20) | copy-start | bytes 1572868
  137.4 7.9 %collective-permute-start.23 = (bf16[256,1024]{1,0:T(8,128)(2,1)S(1)}, bf16[256,1024]{1,0:T(8,128)(2,1)S(1)}, u32[]{:S(2)}, u32[]{:S(2)}) collective-permute-start(bf16[256,1024]{1,0:T(8,128)(2,1)S(1)} %bitcast.34), channel_id=1, source_target_pairs={{0,8},{8,0},{1,9},{9,1},{2,10},{10,2},{3,11},{11,3},{4,12},{12,4},... | collective-permute-start | bytes 1572872 | tf_op jit(solution)/shard_map/ppermute | solution.py:37
  145.3 0.8 copy-start.7
where the time goes:
time: 154 us; the launch traced here: 153 us
  starting transfers between devices  49.4 us (32%)
  waiting for transfers between devices  34.6 us (22%)
  Pallas kernels  30 us (19%)
  blocking collectives  12.1 us (8%)
  local copies, waits for them, and re-layouts  11 us (7%)
  matrix products  6.84 us (4%)
  other arithmetic  6.63 us (4%)
  between operations  2.37 us (2%)
    all_to_all x3, starting transfers between devices, exchange(): return lax.all_to_all(array, axes, split_axis=0, concat_axis=0, tiled=True)  15.1 us
    ppermute x8, waiting for transfers between devices, shift_z(): return lax.ppermute(array, 'gc', [(i, (i + d) % 8) for i in range(8)])  15 us
    ppermute x6, starting transfers between devices, core_swap(): return lax.ppermute(array, 'gr_2', [(0, 1), (1, 0)])  13.8 us
    all_to_all x1, blocking collectives, exchange(): return lax.all_to_all(array, axes, split_axis=0, concat_axis=0, tiled=True)  12.1 us
    ppermute x10, starting transfers between devices, plane_permute(): return lax.ppermute(array, CAL_GR, pairs)  12 us
    pallas_call x2, Pallas kernels, product_call(): pl.pallas_call(kernel, grid_spec=pltpu.PrefetchScalarGridSpec(num_scalar_...  11.7 us
    ppermute x10, waiting for transfers between devices, plane_permute(): return lax.ppermute(array, CAL_GR, pairs)  9.48 us
    ppermute x8, starting transfers between devices, shift_z(): return lax.ppermute(array, 'gc', [(i, (i + d) % 8) for i in range(8)])  8.46 us
  transfers between devices with their start and end apart: 27, of which 16 were waited for; matrix products, arithmetic and copies ran while one was open for 8% of the time, Pallas kernels for 10%

commit v1 on v0

v1 whole, which is shorter than its diff:
```python
import jax
import jax.numpy as jnp
from jax import lax
from jax.experimental import pallas as pl
from jax.experimental.pallas import tpu as pltpu
from jax.sharding import Mesh
from jax.sharding import PartitionSpec as P

GR_GC = ("gr_0", "gr_1", "gr_2", "gc")
PLANE = ("cal", "gr_0", "gr_1")
CAL_GR = ("cal", "gr_0", "gr_1", "gr_2")
CAL_GR_GC = ("cal", "gr_0", "gr_1", "gr_2", "gc")


F32 = jnp.float32
BF16 = jnp.bfloat16
NT = (((1,), (1,)), ((), ()))
VMEM = pl.BlockSpec(memory_space=pltpu.VMEM)
SMEM = pl.BlockSpec(memory_space=pltpu.SMEM)


def plane_index(x, y, c):
    return (((x & 1) * 2 + (x >> 1)) * 4 + y) * 2 + c


def plane_permute(array, on_x_of_core, k):
    pairs = []
    for x in range(4):
        for y in range(4):
            for c in range(2):
                to = (x ^ k, y) if c == on_x_of_core else (x, y ^ k)
                pairs.append((plane_index(x, y, c), plane_index(*to, c)))
    return lax.ppermute(array, CAL_GR, pairs)


def core_swap(array):
    return lax.ppermute(array, "gr_2", [(0, 1), (1, 0)])


def shift_z(array, d):
    return lax.ppermute(array, "gc", [(i, (i + d) % 8) for i in range(8)])


def exchange(array, axes):
    return lax.all_to_all(array, axes, split_axis=0, concat_axis=0, tiled=True)


def split_bf16(a):
    high = a.astype(BF16)
    return high, (a - high.astype(F32)).astype(BF16)


GROUPS = ((0, 0), (0, 1), (1, 0), (1, 1), (3, 0), (3, 1), (2, 0), (2, 1))


def weights_kernel(pos_ref, gate, up, far, out_ref):
    n = gate.shape[0]
    for i, part in enumerate((gate[...], up[...], far[0, 0], far[0, 1])):
        out_ref[0, i * 128 : i * 128 + n, :] = part
        out_ref[0, i * 128 + n : (i + 1) * 128, :] = jnp.zeros((128 - n, part.shape[1]), BF16)


def weights_call(pos, gate_t, up_t, far_w):
    n, depth = far_w.shape[2:]
    columns = pl.BlockSpec((n, depth), lambda f, pos: (0, (f ^ pos[0]) * 2 + pos[3]))
    return pl.pallas_call(
        weights_kernel,
        grid_spec=pltpu.PrefetchScalarGridSpec(
            num_scalar_prefetch=1,
            grid=(2,),
            in_specs=[columns, columns, pl.BlockSpec((1, 2, n, depth), lambda f, pos: (f ^ pos[0], 0, 0, 0))],
            out_specs=pl.BlockSpec((1, 512, depth), lambda f, pos: (f, 0, 0)),
        ),
        out_shape=jax.ShapeDtypeStruct((2, 512, depth), BF16),
        name="weights",
    )(pos, gate_t, up_t, far_w)


def products(tokens, weights, f):
    w = weights[f] if isinstance(f, int) else lax.dynamic_index_in_dim(weights, f, 0, keepdims=False)
    return [lax.dot_general(tokens, half, NT, preferred_element_type=F32) for half in (w[:256], w[256:])]


def activate(pos_ref, *refs):
    own, far = refs[:8], refs[8:10]
    high_ref, low_ref, wh_ref, out_ref, ht_ref, sum_ref = refs[10:]
    c = pos_ref[3]
    xh, y = pos_ref[1], pos_ref[2]
    sum_ref[...] = jnp.zeros_like(sum_ref)
    for i, (m, g) in enumerate(GROUPS):
        theirs = far[0][i * 128 : (i + 1) * 128, :] if i < 6 else far[1][(i - 6) * 128 : (i - 5) * 128, :]
        for core, part in ((c, own[i][...]), (1 - c, theirs)):
            for j in range(2):
                block = jnp.where(
                    core == 0,
                    (xh ^ j) * 4 + (y ^ m),
                    (xh ^ (m >> 1)) * 4 + (y ^ (g + 2 * j)),
                )
                at = pl.ds(pl.multiple_of(block * 64, 64), 64)
                sum_ref[at, :] += part[j * 64 : (j + 1) * 64]
    both = sum_ref[...]
    gate, up = both[:, :128], both[:, 128:]
    hidden = gate / (1.0 + jnp.exp(-gate)) * up
    low = hidden.astype(BF16)
    for q in range(32):
        chunk = (q & 1) * 16 + (q >> 1)
        out_ref[q, :, :128] = low[chunk * 16 : (chunk + 1) * 16, :]
    n = ht_ref.shape[0]
    for half in range(2):
        at = pl.ds(pl.multiple_of((half ^ c) * 256, 256), 256)
        ht_ref[:, at] = hidden[half * 256 : (half + 1) * 256, :].T[:n].astype(BF16)
    part = lax.dot_general(high_ref[...], low, NT, preferred_element_type=F32)
    part += lax.dot_general(low_ref[...], low, NT, preferred_element_type=F32)
    part = part.astype(BF16)
    for q in range(32):
        out_ref[q, :, 128:640] = part[q * 16 : (q + 1) * 16, :]
        out_ref[q, :, 640:] = wh_ref[q * 16 : (q + 1) * 16, :]


def activate_call(pos, own, far, error, wh, n):
    return pl.pallas_call(
        activate,
        out_shape=(
            jax.ShapeDtypeStruct((32, 16, 640 + wh.shape[1]), BF16),
            jax.ShapeDtypeStruct((n, 512), BF16),
        ),
        in_specs=[SMEM] + [VMEM] * 13,
        out_specs=(VMEM, VMEM),
        scratch_shapes=[pltpu.VMEM((512, 256), F32)],
        name="activate",
    )(pos, *own, *far, *error, wh)


def choose(first_ref, arrived_ref, out_ref):
    total = jnp.sum(arrived_ref[:, :, 128:].astype(F32), axis=0).astype(BF16)
    for k in range(8):
        for p in range(3):
            out_ref[k, :, p * 128 : (p + 1) * 128] = arrived_ref[first_ref[k] + p, :, :128]
        out_ref[k, :, 384:] = total


def choose_call(first, arrived):
    return pl.pallas_call(
        choose,
        grid_spec=pltpu.PrefetchScalarGridSpec(
            num_scalar_prefetch=1,
            grid=(1,),
            in_specs=[pl.BlockSpec((32, 16, 640), lambda i, first: (0, 0, 0))],
            out_specs=pl.BlockSpec((8, 16, 896), lambda i, first: (0, 0, 0)),
        ),
        out_shape=jax.ShapeDtypeStruct((8, 16, 896), BF16),
        name="choose",
    )(first, arrived)


def assemble(n, shift_ref, y_ref, chunk_ref, total_ref, line_ref):
    for p in range(3):
        for z in range(8):
            line_ref[:, pl.ds((p * 8 + z) * n, n)] = y_ref[z, :, p * 128 : p * 128 + n].astype(F32)
    width = chunk_ref.shape[2]
    d, c = shift_ref[0], shift_ref[1]
    base = pl.multiple_of((d // 128) * 128, 128)
    near = line_ref[:, pl.ds(base, width + 128)]
    turned = pltpu.roll(near, width + 128 - (d - base), 1)
    chunk = turned[:, :width].astype(BF16)
    for k in range(chunk_ref.shape[0]):
        chunk_ref[k] = chunk
    high, low = split_bf16(jnp.sum(y_ref[:, :, 384:].astype(F32), axis=0))
    for half in range(2):
        at = pl.ds(pl.multiple_of((half ^ c) * 256, 256), 256)
        total_ref[:16, at] = high[:, half * 256 : (half + 1) * 256]
        total_ref[16:, at] = low[:, half * 256 : (half + 1) * 256]


def assemble_call(pieces, shift, width, n):
    def kernel(*refs):
        assemble(n, *refs)

    return pl.pallas_call(
        kernel,
        out_shape=(
            jax.ShapeDtypeStruct((16, 16, width), BF16),
            jax.ShapeDtypeStruct((32, 512), BF16),
        ),
        in_specs=[SMEM, VMEM],
        out_specs=(VMEM, VMEM),
        scratch_shapes=[pltpu.VMEM((16, 24 * n), F32)],
        name="assemble",
    )(shift, pieces)


def panel_kernel(pos_ref, *refs):
    panel_ref = refs[-1]
    z = pos_ref[4]
    n = refs[0].shape[0]
    for piece, d, r0 in zip(refs[:9], (0, -1, 1, -2, 2, -3, 3, -4, 4), (0,) * 8 + (64,)):
        at = pl.multiple_of(((z + d + 8) % 8) * n + r0, 16)
        panel_ref[pl.ds(at, piece.shape[0]), :] = piece[...]


def panel_call(pos, pieces):
    rows = 8 * pieces[0].shape[0]
    return pl.pallas_call(
        panel_kernel,
        out_shape=jax.ShapeDtypeStruct((rows, 512), BF16),
        in_specs=[SMEM] + [VMEM] * len(pieces),
        out_specs=VMEM,
        name="panel",
    )(pos, *pieces)


def on_device(tokens, gate_weight, up_weight, hessian_slab, weight_error, slab_offset, token_count):
    xl, xh, y, c, z = (lax.axis_index(a) for a in CAL_GR_GC)
    pos = jnp.stack([xl, xh, y, c, z]).astype(jnp.int32)
    n = gate_weight.shape[1]
    width = hessian_slab.shape[1]
    quarter = tokens.shape[1] // 2

    mine = lax.dynamic_slice_in_dim(tokens, c * quarter, quarter, 1)
    theirs = core_swap(lax.dynamic_slice_in_dim(tokens, (1 - c) * quarter, quarter, 1))
    piece = jnp.concatenate([jnp.where(c == 0, mine, theirs), jnp.where(c == 0, theirs, mine)], 0)
    copies = jnp.broadcast_to(piece[None], (8, *piece.shape))
    copies, gate_weight, up_weight, weight_error = lax.optimization_barrier(
        (copies, gate_weight, up_weight, weight_error)
    )
    b0 = exchange(copies, "gc").reshape(64, quarter)
    gate_t, up_t = gate_weight.T, up_weight.T
    far_w = core_swap(
        jnp.stack(
            [
                lax.dynamic_slice_in_dim(w, (2 * f + 1 - c) * quarter, quarter, 1)
                for f in range(2)
                for w in (gate_t, up_t)
            ]
        )
    )

    error = jnp.pad(lax.dynamic_slice_in_dim(weight_error, z * n, n, 1), ((0, 0), (0, 128 - n)))
    half = width // 2
    wh_own, wh_sent = (
        jnp.dot(
            weight_error,
            lax.dynamic_slice_in_dim(hessian_slab, core * half, half, 1),
            precision=lax.Precision.HIGH,
            preferred_element_type=F32,
        )
        for core in (c, 1 - c)
    )
    b0, wh_own, wh_sent, far_w, high, low = lax.optimization_barrier(
        (b0, wh_own, wh_sent, far_w, *split_bf16(error))
    )

    b1 = plane_permute(b0, 0, 1)
    b3 = plane_permute(b0, 0, 3)
    wh_far = core_swap(wh_sent)
    wh = (wh_own + wh_far).astype(BF16)
    weights = weights_call(pos, gate_t, up_t, far_w.reshape(2, 2, n, quarter))
    b1, b3, weights = lax.optimization_barrier((b1, b3, weights))
    b2a = plane_permute(b1[:32], 0, 3)
    b2b = plane_permute(b3[32:], 0, 1)
    b2a, b2b, wh = lax.optimization_barrier((b2a, b2b, wh))
    sb = jnp.concatenate([b1, b3], 0)
    s3b = plane_permute(sb, 1, 3)
    s1b = plane_permute(sb, 1, 1)
    sa = jnp.concatenate([b0, b2a, b2b], 0)
    s1a = plane_permute(sa, 1, 1)
    s3a = plane_permute(sa, 1, 3)
    s2b = plane_permute(s3b, 1, 1)
    s2a = plane_permute(s1a, 1, 3)
    own, far = [], []
    for buffer, f in zip((sa, sb, s1a, s1b, s3a, s3b, s2a, s2b), (0, 1 - c, c, 1, c, 1, 0, 1 - c)):
        mine, theirs = products(buffer, weights, f)
        own.append(mine)
        far.append(theirs)
    far = [core_swap(jnp.concatenate(part, 0)) for part in (far[:6], far[6:])]
    sent, hidden_t = activate_call(pos, own, far, (high, low), wh, n)

    f1, g1 = shift_z(hidden_t, 1), shift_z(hidden_t, -1)
    f2, g2 = shift_z(f1, 1), shift_z(g1, -1)
    arrived = exchange(sent, CAL_GR)
    arrived, f2, g2 = lax.optimization_barrier((arrived, f2, g2))
    f3, g3 = shift_z(f2, 1), shift_z(g2, -1)
    panel_width = 8 * n
    starts = slab_offset[0] + jnp.arange(8, dtype=jnp.int32) * width
    pieces = exchange(choose_call(jnp.minimum(starts // panel_width, 29), arrived), "gc")
    sums = jnp.sum(arrived[:, :, 640:].reshape(16, 2, 16, half).astype(F32), axis=0)
    wh = jnp.concatenate([sums[0], sums[1]], 1)
    pieces, f3, g3, wh = lax.optimization_barrier((pieces, f3, g3, wh))
    f4, g4 = shift_z(f3[:64], 1), shift_z(g3[64:], -1)
    start = slab_offset[0] + z * width
    shift = start - jnp.minimum(start // panel_width, 29) * panel_width
    chunk, total = assemble_call(pieces, jnp.stack([shift, c]).astype(jnp.int32), width, n)
    near = exchange(chunk, PLANE).reshape(256, width)
    panel_t = panel_call(pos, (hidden_t, f1, g1, f2, g2, f3, g3, f4, g4))
    near, panel_t = lax.optimization_barrier((near, panel_t))
    window = jnp.concatenate([near, core_swap(near)], 0)
    scale = 1.0 / token_count[0].astype(F32)
    gram = jnp.dot(panel_t, window, preferred_element_type=F32)
    added = jnp.dot(total, window, preferred_element_type=F32)
    return (hessian_slab + gram * scale, wh + (added[:16] + added[16:]) * scale)


def solution(mesh):
    split = Mesh(
        mesh.devices.reshape(mesh.shape["cal"], 2, 4, 2, mesh.shape["gc"]),
        ("cal", "gr_0", "gr_1", "gr_2", "gc"),
    )

    return jax.shard_map(
        on_device,
        mesh=split,
        in_specs=(
            P(GR_GC, "cal"),
            P(None, CAL_GR_GC),
            P(None, CAL_GR_GC),
            P(CAL_GR, "gc"),
            P(None, CAL_GR),
            P(),
            P(),
        ),
        out_specs=(P(CAL_GR, "gc"), P(CAL_GR, "gc")),
        check_vma=False,
    )
```

time: 154 us -> 159 us (1.032)
  matrix products: 6.84 us -> 28.3 us
  Pallas kernels: 30 us -> 14.7 us
  blocking collectives: 12.1 us -> 0 us
  local copies, waits for them, and re-layouts: 11 us -> 15.8 us
  waiting for transfers between devices: 34.6 us -> 38.2 us
  starting transfers between devices: 49.4 us -> 51.8 us
    dot_general x1 -> x20, matrix products: 6.84 us -> 28.3 us  [the longest x16 16.7 us: products(): lax.dot_general(tokens, half, NT, preferred_element_type=F32)]
    all_to_all x3 -> x4, waiting for transfers between devices: 6.68 us -> 23.1 us  [exchange(): return lax.all_to_all(array, axes, split_axis=0, concat_axis=0, tiled=True)]
    pallas_call x4 -> x2, Pallas kernels: 20.5 us -> 4.79 us  [the longest x1 2.54 us: choose_call(): pl.pallas_call(choose, grid_spec=pltpu.PrefetchScalarGridSpec(num_scalar_...]
    all_to_all x1 -> x0, blocking collectives: 12.1 us -> none  [exchange(): return lax.all_to_all(array, axes, split_axis=0, concat_axis=0, tiled=True)]
    ppermute x8, waiting for transfers between devices: 15 us -> 7.61 us  [shift_z(): return lax.ppermute(array, 'gc', [(i, (i + d) % 8) for i in range(8)])]
    ppermute x10, waiting for transfers between devices: 9.48 us -> 5.75 us  [plane_permute(): return lax.ppermute(array, CAL_GR, pairs)]
    all_to_all x3 -> x4, starting transfers between devices: 15.1 us -> 18.4 us  [exchange(): return lax.all_to_all(array, axes, split_axis=0, concat_axis=0, tiled=True)]
    unnamed x43 -> x34, local copies, waits for them, and re-layouts: 4.05 us -> 6.69 us
  transfers between devices with their start and end apart: 27 -> 28, of which waited for: 16 -> 12; matrix products, arithmetic and copies ran while one was open for 8% -> 21% of each run, Pallas kernels for 10% -> 6%
where the time goes in v1:
time: 159 us; the launch traced here: 158 us
  starting transfers between devices  51.8 us (33%)
  waiting for transfers between devices  38.2 us (24%)
  matrix products  28.3 us (18%)
  local copies, waits for them, and re-layouts  15.8 us (10%)
  Pallas kernels  14.7 us (9%)
  other arithmetic  7.09 us (4%)
  between operations  2.35 us (1%)
    all_to_all x4, waiting for transfers between devices, exchange(): return lax.all_to_all(array, axes, split_axis=0, concat_axis=0, tiled=True)  23.1 us
    all_to_all x4, starting transfers between devices, exchange(): return lax.all_to_all(array, axes, split_axis=0, concat_axis=0, tiled=True)  18.4 us
    dot_general x16, matrix products, products(): lax.dot_general(tokens, half, NT, preferred_element_type=F32)  16.7 us
    ppermute x6, starting transfers between devices, core_swap(): return lax.ppermute(array, 'gr_2', [(0, 1), (1, 0)])  15 us
    ppermute x10, starting transfers between devices, plane_permute(): return lax.ppermute(array, CAL_GR, pairs)  10 us
    ppermute x8, starting transfers between devices, shift_z(): return lax.ppermute(array, 'gc', [(i, (i + d) % 8) for i in range(8)])  8.39 us
    ppermute x8, waiting for transfers between devices, shift_z(): return lax.ppermute(array, 'gc', [(i, (i + d) % 8) for i in range(8)])  7.61 us
    unnamed x34, local copies, waits for them, and re-layouts  6.69 us
  transfers between devices with their start and end apart: 28, of which 12 were waited for; matrix products, arithmetic and copies ran while one was open for 21% of the time, Pallas kernels for 6%

profile of v1, /device:TPU:1, one launch (start us, length us, event | category | flops | bytes accessed | tf_op | source)
XLA Modules:
  0.0 158.2 jit_solution(61593680938547910)
XLA Ops:
  0.7 0.9 constant_dynamic-slice_fusion.1
  1.5 3.2 %collective-permute-start = (bf16[4,2048]{1,0:T(4,128)(2,1)S(1)}, bf16[4,2048]{1,0:T(4,128)(2,1)S(1)}, u32[]{:S(2)}, u32[]{:S(2)}) collective-permute-start(bf16[4,2048]{1,0:T(4,128)(2,1)S(1)} %constant_dynamic-slice_fusion.1), channel_id=1, source_target_pairs={{0,8},{8,0},{1,9},{9,1},{2,10},{10,2},{3,11},{11,3},{4,12},{12,4},... | collective-permute-start | bytes 49160 | tf_op jit(solution)/shard_map/ppermute | solution.py:37
  4.7 0.8 collective-permute-done
  5.6 0.7 broadcast_select_fusion.1
  6.3 0.7 broadcast_in_dim.2
  7.0 1.6 dynamic-slice_bitcast_fusion.14
  8.6 1.5 pad_maximum_fusion
  10.4 6.5 %all-to-all-start = ((bf16[8,8,2048]{2,1,0:T(8,128)(2,1)}), bf16[8,8,2048]{2,1,0:T(8,128)(2,1)S(1)}, u32[]{:S(2)}, u32[]{:S(2)}) async-start(bf16[8,8,2048]{2,1,0:T(8,128)(2,1)} %broadcast_in_dim.2), calls=%async_computation | async-start | bytes 524288 | tf_op jit(solution)/shard_map/all_to_all | solution.py:45
  17.0 4.4 %fusion = f32[512,512]{1,0:T(8,128)} fusion(f32[512,896]{1,0:T(8,128)S(1)} %copy-done, f32[896,1024]{1,0:T(8,128)} %param.10, s32[]{:T(128)S(6)} %select_n.62), kind=kOutput, calls=%fused_computation.2 | convolution fusion | flops 1409286144 | bytes 4718596 | tf_op jit(solution)/shard_map/dot_general | solution.py:241
  21.5 0.7 subtract_convert_fusion.refs_11_
  22.9 1.9 %fusion.2 = f32[512,512]{1,0:T(8,128)S(1)} fusion(f32[512,896]{1,0:T(8,128)S(1)} %copy-done, f32[896,1024]{1,0:T(8,128)S(1)} %copy-done.2, s32[]{:T(128)S(6)} %select_n.61), kind=kOutput, calls=%fused_computation.4 | convolution fusion | flops 1409286144 | bytes 4718596 | tf_op jit(solution)/shard_map/dot_general | solution.py:241
  24.8 4.4 %all-to-all-done = bf16[8,8,2048]{2,1,0:T(8,128)(2,1)S(1)} async-done(((bf16[8,8,2048]{2,1,0:T(8,128)(2,1)}), bf16[8,8,2048]{2,1,0:T(8,128)(2,1)S(1)}, u32[]{:S(2)}, u32[]{:S(2)}) %all-to-all-start) | async-done | bytes 262176 | tf_op jit(solution)/shard_map/all_to_all | solution.py:45
  29.1 2.7 %collective-permute-start.3 = (bf16[64,2048]{1,0:T(8,128)(2,1)S(1)}, bf16[64,2048]{1,0:T(8,128)(2,1)S(1)}, u32[]{:S(2)}, u32[]{:S(2)}) collective-permute-start(bf16[64,2048]{1,0:T(8,128)(2,1)S(1)} %bitcast.100), channel_id=1, source_target_pairs={{0,192},{8,56},{16,208},{24,40},{32,224},{40,24},{48,240},{56,8},{... | collective-permute-start | bytes 786440 | tf_op jit(solution)/shard_map/ppermute | solution.py:33
  32.5 4.2 %weights.1 = bf16[2,512,2048]{2,1,0:T(8,128)(2,1)} custom-call(s32[5]{0:T(128)} %stack.47.pos_ref, bf16[112,8192]{1,0:T(8,128)(2,1)} %bitcast.95, bf16[112,8192]{1,0:T(8,128)(2,1)} %bitcast.96, bf16[2,2,112,2048]{3,2,1,0:T(8,128)(2,1)} %bitcast.18.far), custom_call_target="tpu_custom_call" | custom-call | tf_op jit(solution)/shard_map/weights/pallas_call | solution.py:66
  36.7 0.7 copy-done.8
  37.5 1.0 constant_dynamic-update-slice_fusion.4
  38.5 1.0 constant_dynamic-update-slice_fusion.3
  39.4 2.5 %collective-permute-start.10 = (bf16[128,2048]{1,0:T(8,128)(2,1)S(1)}, bf16[128,2048]{1,0:T(8,128)(2,1)}, u32[]{:S(2)}, u32[]{:S(2)}) collective-permute-start(bf16[128,2048]{1,0:T(8,128)(2,1)S(1)} %constant_dynamic-update-slice_fusion.3), channel_id=1, source_target_pairs={{0,48},{8,200},{16,32},{24,216},{32,16},{40,232},{48,0},{56,248},{... | collective-permute-start | bytes 1572872 | tf_op jit(solution)/shard_map/ppermute | solution.py:33
  41.9 2.1 %collective-permute-start.6 = (f32[512,512]{1,0:T(8,128)}, f32[512,512]{1,0:T(8,128)}, u32[]{:S(2)}, u32[]{:S(2)}) collective-permute-start(f32[512,512]{1,0:T(8,128)} %fusion), channel_id=1, source_target_pairs={{0,8},{8,0},{1,9},{9,1},{2,10},{10,2},{3,11},{11,3},{4,12},{12,4},... | collective-permute-start | bytes 3145736 | tf_op jit(solution)/shard_map/ppermute | solution.py:37
  44.0 0.8 collective-permute-start.8
  44.8 1.4 constant_dynamic-update-slice_fusion.2
  46.2 0.9 slice.91
  47.1 0.9 slice.92
  48.8 2.4 %fusion.26.refs_1_ = f32[128,256]{1,0:T(8,128)} fusion(bf16[128,2048]{1,0:T(8,128)(2,1)S(1)} %constant_dynamic-update-slice_fusion.3, bf16[2,512,2048]{2,1,0:T(8,128)(2,1)} %weights.1, s32[]{:T(128)S(6)} %select_n.66), kind=kOutput, calls=%fused_computation.40 | convolution fusion | flops 134217728 | bytes 1703940 | tf_op jit(solution)/shard_map/dot_general | solution.py:81
  51.7 2.5 %fusion.9.refs_5_ = f32[128,256]{1,0:T(8,128)} fusion(bf16[128,2048]{1,0:T(8,128)(2,1)} %collective-permute-done.10, bf16[2,512,2048]{2,1,0:T(8,128)(2,1)} %weights.1), kind=kOutput, calls=%fused_computation.22 | convolution fusion | flops 134217728 | bytes 1703936 | tf_op jit(solution)/shard_map/dot_general | solution.py:81
  54.2 1.1 fusion.11.refs_3_
  55.3 2.2 %add_convert_fusion.refs_12_ = bf16[512,512]{1,0:T(8,128)(2,1)} fusion(f32[512,512]{1,0:T(8,128)S(1)} %fusion.2, f32[512,512]{1,0:T(8,128)} %collective-permute-done.6), kind=kLoop, calls=%fused_computation.30 | loop fusion | flops 524288 | bytes 2621440 | tf_op jit(solution)/shard_map/convert_element_type | solution.py:256
  57.6 1.1 fusion.15.refs_0_
  58.7 1.2 collective-permute-start.9
  61.4 1.1 fusion.25.refs_7_
  62.6 5.7 %collective-permute-done.7 = bf16[128,2048]{1,0:T(8,128)(2,1)S(1)} collective-permute-done((bf16[128,2048]{1,0:T(8,128)(2,1)S(1)}, bf16[128,2048]{1,0:T(8,128)(2,1)S(1)}, u32[]{:S(2)}, u32[]{:S(2)}) %collective-permute-start.7) | collective-permute-done | bytes 524320 | tf_op jit(solution)/shard_map/ppermute | solution.py:33
  68.3 1.5 collective-permute-start.11
  71.2 1.5 convolution_dynamic-update-slice_fusion
  72.8 3.0 %collective-permute-start.13 = (f32[768,256]{1,0:T(8,128)S(1)}, f32[768,256]{1,0:T(8,128)S(1)}, u32[]{:S(2)}, u32[]{:S(2)}) collective-permute-start(f32[768,256]{1,0:T(8,128)S(1)} %convolution_dynamic-update-slice_fusion), channel_id=1, source_target_pairs={{0,8},{8,0},{1,9},{9,1},{2,10},{10,2},{3,11},{11,3},{4,12},{12,4},... | collective-permute-start | bytes 2359304 | tf_op jit(solution)/shard_map/ppermute | solution.py:37
  75.8 1.1 fusion.27.refs_4_
  76.9 1.2 fusion.28.refs_2_
  78.6 4.1 %collective-permute-start.14 = (f32[256,256]{1,0:T(8,128)S(1)}, f32[256,256]{1,0:T(8,128)S(1)}, u32[]{:S(2)}, u32[]{:S(2)}) collective-permute-start(f32[256,256]{1,0:T(8,128)S(1)} %pad_maximum_fusion.1), channel_id=1, source_target_pairs={{0,8},{8,0},{1,9},{9,1},{2,10},{10,2},{3,11},{11,3},{4,12},{12,4},... | collective-permute-start | bytes 786440 | tf_op jit(solution)/shard_map/ppermute | solution.py:37
  82.7 1.1 fusion.13.refs_6_
  83.9 0.7 copy-done.9
  84.6 0.9 copy-done.7
  85.5 3.7 %activate.1 = (bf16[32,16,1152]{2,1,0:T(8,128)(2,1)}, bf16[112,512]{1,0:T(8,128)(2,1)}) custom-call(s32[5]{0:T(128)} %stack.47.pos_ref, f32[128,256]{1,0:T(8,128)} %fusion.15.refs_0_, f32[128,256]{1,0:T(8,128)} %fusion.26.refs_1_, f32[128,256]{1,0:T(8,128)} %fusion.28.refs_2_, f32[128,256]{1,0:T(8,128)} %fusion.11.refs_3_, f32[128,256]{1,0:T(8,128)} %fusion.27.refs_4_, ...), custom_call_target="tpu_custom_call" | custom-call | tf_op jit(solution)/shard_map/activate/pallas_call | solution.py:121
  89.2 4.6 %all-to-all-start.1 = ((bf16[32,16,1152]{2,1,0:T(8,128)(2,1)}), bf16[32,16,1152]{2,1,0:T(8,128)(2,1)S(1)}, u32[]{:S(2)}, u32[]{:S(2)}) async-start(bf16[32,16,1152]{2,1,0:T(8,128)(2,1)} %get-tuple-element.47), calls=%async_computation.1 | async-start | bytes 2359296 | tf_op jit(solution)/shard_map/all_to_all | solution.py:45
  93.9 1.5 collective-permute-start.15
  96.0 2.5 %collective-permute-done.17.refs_2_ = bf16[112,512]{1,0:T(8,128)(2,1)S(1)} collective-permute-done((bf16[112,512]{1,0:T(8,128)(2,1)}, bf16[112,512]{1,0:T(8,128)(2,1)S(1)}, u32[]{:S(2)}, u32[]{:S(2)}) %collective-permute-start.17) | collective-permute-done | bytes 114720 | tf_op jit(solution)/shard_map/ppermute | solution.py:41
  98.6 1.5 collective-permute-start.18
  101.3 1.2 collective-permute-done.18.refs_4_
  102.5 2.7 %collective-permute-done.16.refs_3_ = bf16[112,512]{1,0:T(8,128)(2,1)} collective-permute-done((bf16[112,512]{1,0:T(8,128)(2,1)S(1)}, bf16[112,512]{1,0:T(8,128)(2,1)}, u32[]{:S(2)}, u32[]{:S(2)}) %collective-permute-start.16) | collective-permute-done | bytes 114720 | tf_op jit(solution)/shard_map/ppermute | solution.py:41
  105.2 7.3 %all-to-all-done.1.arrived_ref = bf16[32,16,1152]{2,1,0:T(8,128)(2,1)S(1)} async-done(((bf16[32,16,1152]{2,1,0:T(8,128)(2,1)}), bf16[32,16,1152]{2,1,0:T(8,128)(2,1)S(1)}, u32[]{:S(2)}, u32[]{:S(2)}) %all-to-all-start.1) | async-done | bytes 1179680 | tf_op jit(solution)/shard_map/all_to_all | solution.py:45
  112.8 2.4 %collective-permute-start.20 = (bf16[112,512]{1,0:T(8,128)(2,1)}, bf16[112,512]{1,0:T(8,128)(2,1)}, u32[]{:S(2)}, u32[]{:S(2)}) collective-permute-start(bf16[112,512]{1,0:T(8,128)(2,1)} %collective-permute-done.18.refs_4_), channel_id=1, source_target_pairs={{0,7},{1,0},{2,1},{3,2},{4,3},{5,4},{6,5},{7,6},{8,15},{9,8},{10,9... | collective-permute-start | bytes 344072 | tf_op jit(solution)/shard_map/ppermute | solution.py:41
  115.3 2.5 %choose.1 = bf16[8,16,896]{2,1,0:T(8,128)(2,1)} custom-call(s32[8]{0:T(128)} %fusion.42.first_ref, bf16[32,16,1152]{2,1,0:T(8,128)(2,1)} %copy-done.3), custom_call_target="tpu_custom_call" | custom-call | tf_op jit(solution)/shard_map/choose/pallas_call | solution.py:143
  117.8 3.6 %all-to-all-start.2 = ((bf16[8,16,896]{2,1,0:T(8,128)(2,1)}), bf16[8,16,896]{2,1,0:T(8,128)(2,1)S(1)}, u32[]{:S(2)}, u32[]{:S(2)}) async-start(bf16[8,16,896]{2,1,0:T(8,128)(2,1)} %choose.1), calls=%async_computation.2 | async-start | bytes 458752 | tf_op jit(solution)/shard_map/all_to_all | solution.py:45
  121.6 10.7 %all-to-all-done.2.refs_1_ = bf16[8,16,896]{2,1,0:T(8,128)(2,1)S(1)} async-done(((bf16[8,16,896]{2,1,0:T(8,128)(2,1)}), bf16[8,16,896]{2,1,0:T(8,128)(2,1)S(1)}, u32[]{:S(2)}, u32[]{:S(2)}) %all-to-all-start.2) | async-done | bytes 229408 | tf_op jit(solution)/shard_map/all_to_all | solution.py:45
  132.2 0.7 copy-done.6
  132.9 2.0 %assemble.1 = (bf16[16,16,1024]{2,1,0:T(8,128)(2,1)}, bf16[32,512]{1,0:T(8,128)(2,1)}) custom-call(s32[2]{0:T(128)} %pad_add_fusion.refs_0_, bf16[8,16,896]{2,1,0:T(8,128)(2,1)} %copy-done.6), custom_call_target="tpu_custom_call" | custom-call | tf_op jit(solution)/shard_map/assemble/pallas_call | solution.py:179
  134.9 3.7 %all-to-all-start.3 = ((bf16[16,16,1024]{2,1,0:T(8,128)(2,1)}), bf16[16,16,1024]{2,1,0:T(8,128)(2,1)S(1)}, u32[]{:S(2)}, u32[]{:S(2)}) async-start(bf16[16,16,1024]{2,1,0:T(8,128)(2,1)} %get-tuple-element.53), calls=%async_computation.3 | async-start | bytes 1048576 | tf_op jit(solution)/shard_map/all_to_all | solution.py:45
  138.6 0.8 slice.112
  139.5 0.8 slice.113
  140.3 2.6 %collective-permute-start.22 = (bf16[48,512]{1,0:T(8,128)(2,1)S(1)}, bf16[48,512]{1,0:T(8,128)(2,1)S(1)}, u32[]{:S(2)}, u32[]{:S(2)}) collective-permute-start(bf16[48,512]{1,0:T(8,128)(2,1)S(1)} %slice.113), channel_id=1, source_target_pairs={{0,7},{1,0},{2,1},{3,2},{4,3},{5,4},{6,5},{7,6},{8,15},{9,8},{10,9... | collective-permute-start | bytes 147464 | tf_op jit(solution)/shard_map/ppermute | solution.py:41
  142.9 1.2 collective-permute-done.22.refs_8_
  145.3 2.3 %panel.1 = bf16[896,512]{1,0:T(8,128)(2,1)} custom-call(s32[5]{0:T(128)} %stack.47.pos_ref, bf16[112,512]{1,0:T(8,128)(2,1)} %get-tuple-element.48.refs_0_, bf16[112,512]{1,0:T(8,128)(2,1)} %copy-done.11, bf16[112,512]{1,0:T(8,128)(2,1)} %copy-done.10, bf16[112,512]{1,0:T(8,128)(2,1)} %collective-permute-done.16.refs_3_, ...), custom_call_target="tpu_custom_call" | custom-call | tf_op jit(solution)/shard_map/panel/pallas_call | solution.py:203
  147.6 0.8 all-to-all-done.3
  148.4 2.2 %collective-permute-start.23 = (bf16[256,1024]{1,0:T(8,128)(2,1)S(1)}, bf16[256,1024]{1,0:T(8,128)(2,1)S(1)}, u32[]{:S(2)}, u32[]{:S(2)}) collective-permute-start(bf16[256,1024]{1,0:T(8,128)(2,1)S(1)} %bitcast.97), channel_id=1, source_target_pairs={{0,8},{8,0},{1,9},{9,1},{2,10},{10,2},{3,11},{11,3},{4,12},{12,4},... | collective-permute-start | bytes 1572872 | tf_op jit(solution)/shard_map/ppermute | solution.py:37
  151.4 0.8 collective-permute-done.23
  152.5 5.0 %multiply_add_fusion = f32[896,1024]{1,0:T(8,128)} fusion(f32[896,1024]{1,0:T(8,128)} %param.10, bf16[896,512]{1,0:T(8,128)(2,1)S(1)} %copy-done.4, bf16[512,1024]{1,0:T(8,128)(2,1)S(1)} %constant_dynamic-update-slice_fusion.5, f32[]{:T(128)} %bitcast.31), kind=kOutput, calls=%fused_computation | convolution fusion | flops 941359104 | bytes 9306116 | tf_op jit(solution)/shard_map/dot_general | solution.py:298
  (77 shorter events, 10.7 us)
Async XLA Ops:
  0.6 16.3 %copy-start = (f32[512,896]{1,0:T(8,128)S(1)}, f32[512,896]{1,0:T(8,128)}, u32[]{:S(2)}) copy-start(f32[512,896]{1,0:T(8,128)} %param.11) | copy-start | bytes 5505028
  1.5 4.0 %collective-permute-start = (bf16[4,2048]{1,0:T(4,128)(2,1)S(1)}, bf16[4,2048]{1,0:T(4,128)(2,1)S(1)}, u32[]{:S(2)}, u32[]{:S(2)}) collective-permute-start(bf16[4,2048]{1,0:T(4,128)(2,1)S(1)} %constant_dynamic-slice_fusion.1), channel_id=1, source_target_pairs={{0,8},{8,0},{1,9},{9,1},{2,10},{10,2},{3,11},{11,3},{4,12},{12,4},... | collective-permute-start | bytes 49160 | tf_op jit(solution)/shard_map/ppermute | solution.py:37
  10.1 19.1 %collective-permute-start.1 = (bf16[4,112,2048]{2,1,0:T(8,128)(2,1)}, bf16[4,112,2048]{2,1,0:T(8,128)(2,1)}, u32[]{:S(2)}, u32[]{:S(2)}) collective-permute-start(bf16[4,112,2048]{2,1,0:T(8,128)(2,1)} %pad_maximum_fusion), channel_id=1, source_target_pairs={{0,8},{8,0},{1,9},{9,1},{2,10},{10,2},{3,11},{11,3},{4,12},{12,4},... | collective-permute-start | bytes 5505032 | tf_op jit(solution)/shard_map/ppermute | solution.py:37
  10.4 18.7 %all-to-all-start = ((bf16[8,8,2048]{2,1,0:T(8,128)(2,1)}), bf16[8,8,2048]{2,1,0:T(8,128)(2,1)S(1)}, u32[]{:S(2)}, u32[]{:S(2)}) async-start(bf16[8,8,2048]{2,1,0:T(8,128)(2,1)} %broadcast_in_dim.2), calls=%async_computation | async-start | bytes 524288 | tf_op jit(solution)/shard_map/all_to_all | solution.py:45
  16.9 6.0 %copy-start.2 = (f32[896,1024]{1,0:T(8,128)S(1)}, f32[896,1024]{1,0:T(8,128)}, u32[]{:S(2)}) copy-start(f32[896,1024]{1,0:T(8,128)} %param.10) | copy-start | bytes 11010052
  29.1 7.6 %copy-start.5 = (bf16[8,8,2048]{2,1,0:T(8,128)(2,1)}, bf16[8,8,2048]{2,1,0:T(8,128)(2,1)S(1)}, u32[]{:S(2)}) copy-start(bf16[8,8,2048]{2,1,0:T(8,128)(2,1)S(1)} %all-to-all-done) | copy-start | bytes 786436
  29.1 7.6 %collective-permute-start.3 = (bf16[64,2048]{1,0:T(8,128)(2,1)S(1)}, bf16[64,2048]{1,0:T(8,128)(2,1)S(1)}, u32[]{:S(2)}, u32[]{:S(2)}) collective-permute-start(bf16[64,2048]{1,0:T(8,128)(2,1)S(1)} %bitcast.100), channel_id=1, source_target_pairs={{0,192},{8,56},{16,208},{24,40},{32,224},{40,24},{48,240},{56,8},{... | collective-permute-start | bytes 786440 | tf_op jit(solution)/shard_map/ppermute | solution.py:33
  31.9 5.6 %collective-permute-start.2 = (bf16[64,2048]{1,0:T(8,128)(2,1)S(1)}, bf16[64,2048]{1,0:T(8,128)(2,1)}, u32[]{:S(2)}, u32[]{:S(2)}) collective-permute-start(bf16[64,2048]{1,0:T(8,128)(2,1)S(1)} %bitcast.101), channel_id=1, source_target_pairs={{0,128},{8,24},{16,144},{24,8},{32,160},{40,56},{48,176},{56,40},{... | collective-permute-start | bytes 786440 | tf_op jit(solution)/shard_map/ppermute | solution.py:33
  36.7 0.7 copy-start.8
  39.4 11.7 %collective-permute-start.10 = (bf16[128,2048]{1,0:T(8,128)(2,1)S(1)}, bf16[128,2048]{1,0:T(8,128)(2,1)}, u32[]{:S(2)}, u32[]{:S(2)}) collective-permute-start(bf16[128,2048]{1,0:T(8,128)(2,1)S(1)} %constant_dynamic-update-slice_fusion.3), channel_id=1, source_target_pairs={{0,48},{8,200},{16,32},{24,216},{32,16},{40,232},{48,0},{56,248},{... | collective-permute-start | bytes 1572872 | tf_op jit(solution)/shard_map/ppermute | solution.py:33
  41.9 13.4 %collective-permute-start.6 = (f32[512,512]{1,0:T(8,128)}, f32[512,512]{1,0:T(8,128)}, u32[]{:S(2)}, u32[]{:S(2)}) collective-permute-start(f32[512,512]{1,0:T(8,128)} %fusion), channel_id=1, source_target_pairs={{0,8},{8,0},{1,9},{9,1},{2,10},{10,2},{3,11},{11,3},{4,12},{12,4},... | collective-permute-start | bytes 3145736 | tf_op jit(solution)/shard_map/ppermute | solution.py:37
  44.0 10.2 %copy-start.1 = (bf16[2,512,2048]{2,1,0:T(8,128)(2,1)S(1)}, bf16[2,512,2048]{2,1,0:T(8,128)(2,1)}, u32[]{:S(2)}) copy-start(bf16[2,512,2048]{2,1,0:T(8,128)(2,1)} %weights.1) | copy-start | bytes 12582916
  44.0 10.2 %collective-permute-start.8 = (bf16[128,2048]{1,0:T(8,128)(2,1)S(1)}, bf16[128,2048]{1,0:T(8,128)(2,1)S(1)}, u32[]{:S(2)}, u32[]{:S(2)}) collective-permute-start(bf16[128,2048]{1,0:T(8,128)(2,1)S(1)} %constant_dynamic-update-slice_fusion.3), channel_id=1, source_target_pairs={{0,16},{8,136},{16,0},{24,152},{32,48},{40,168},{48,32},{56,184},{... | collective-permute-start | bytes 1572872 | tf_op jit(solution)/shard_map/ppermute | solution.py:33
  48.1 9.5 %collective-permute-start.5 = (bf16[32,2048]{1,0:T(8,128)(2,1)S(1)}, bf16[32,2048]{1,0:T(8,128)(2,1)S(1)}, u32[]{:S(2)}, u32[]{:S(2)}) collective-permute-start(bf16[32,2048]{1,0:T(8,128)(2,1)S(1)} %slice.92), channel_id=1, source_target_pairs={{0,128},{8,24},{16,144},{24,8},{32,160},{40,56},{48,176},{56,40},{... | collective-permute-start | bytes 393224 | tf_op jit(solution)/shard_map/ppermute | solution.py:33
  48.2 9.4 %collective-permute-start.4 = (bf16[32,2048]{1,0:T(8,128)(2,1)S(1)}, bf16[32,2048]{1,0:T(8,128)(2,1)S(1)}, u32[]{:S(2)}, u32[]{:S(2)}) collective-permute-start(bf16[32,2048]{1,0:T(8,128)(2,1)S(1)} %slice.91), channel_id=1, source_target_pairs={{0,192},{8,56},{16,208},{24,40},{32,224},{40,24},{48,240},{56,8},{... | collective-permute-start | bytes 393224 | tf_op jit(solution)/shard_map/ppermute | solution.py:33
  51.1 9.8 %collective-permute-start.12 = (bf16[128,2048]{1,0:T(8,128)(2,1)}, bf16[128,2048]{1,0:T(8,128)(2,1)S(1)}, u32[]{:S(2)}, u32[]{:S(2)}) collective-permute-start(bf16[128,2048]{1,0:T(8,128)(2,1)} %collective-permute-done.10), channel_id=1, source_target_pairs={{0,16},{8,136},{16,0},{24,152},{32,48},{40,168},{48,32},{56,184},{... | collective-permute-start | bytes 1572872 | tf_op jit(solution)/shard_map/ppermute | solution.py:33
  58.7 12.0 %collective-permute-start.9 = (bf16[128,2048]{1,0:T(8,128)(2,1)S(1)}, bf16[128,2048]{1,0:T(8,128)(2,1)S(1)}, u32[]{:S(2)}, u32[]{:S(2)}) collective-permute-start(bf16[128,2048]{1,0:T(8,128)(2,1)S(1)} %constant_dynamic-update-slice_fusion), channel_id=1, source_target_pairs={{0,48},{8,200},{16,32},{24,216},{32,16},{40,232},{48,0},{56,248},{... | collective-permute-start | bytes 1572872 | tf_op jit(solution)/shard_map/ppermute | solution.py:33
  59.9 8.3 %collective-permute-start.7 = (bf16[128,2048]{1,0:T(8,128)(2,1)S(1)}, bf16[128,2048]{1,0:T(8,128)(2,1)S(1)}, u32[]{:S(2)}, u32[]{:S(2)}) collective-permute-start(bf16[128,2048]{1,0:T(8,128)(2,1)S(1)} %constant_dynamic-update-slice_fusion), channel_id=1, source_target_pairs={{0,16},{8,136},{16,0},{24,152},{32,48},{40,168},{48,32},{56,184},{... | collective-permute-start | bytes 1572872 | tf_op jit(solution)/shard_map/ppermute | solution.py:33
  68.3 9.8 %collective-permute-start.11 = (bf16[128,2048]{1,0:T(8,128)(2,1)S(1)}, bf16[128,2048]{1,0:T(8,128)(2,1)S(1)}, u32[]{:S(2)}, u32[]{:S(2)}) collective-permute-start(bf16[128,2048]{1,0:T(8,128)(2,1)S(1)} %collective-permute-done.7), channel_id=1, source_target_pairs={{0,48},{8,200},{16,32},{24,216},{32,16},{40,232},{48,0},{56,248},{... | collective-permute-start | bytes 1572872 | tf_op jit(solution)/shard_map/ppermute | solution.py:33
  72.8 11.1 %collective-permute-start.13 = (f32[768,256]{1,0:T(8,128)S(1)}, f32[768,256]{1,0:T(8,128)S(1)}, u32[]{:S(2)}, u32[]{:S(2)}) collective-permute-start(f32[768,256]{1,0:T(8,128)S(1)} %convolution_dynamic-update-slice_fusion), channel_id=1, source_target_pairs={{0,8},{8,0},{1,9},{9,1},{2,10},{10,2},{3,11},{11,3},{4,12},{12,4},... | collective-permute-start | bytes 2359304 | tf_op jit(solution)/shard_map/ppermute | solution.py:37
  78.6 5.3 %collective-permute-start.14 = (f32[256,256]{1,0:T(8,128)S(1)}, f32[256,256]{1,0:T(8,128)S(1)}, u32[]{:S(2)}, u32[]{:S(2)}) collective-permute-start(f32[256,256]{1,0:T(8,128)S(1)} %pad_maximum_fusion.1), channel_id=1, source_target_pairs={{0,8},{8,0},{1,9},{9,1},{2,10},{10,2},{3,11},{11,3},{4,12},{12,4},... | collective-permute-start | bytes 786440 | tf_op jit(solution)/shard_map/ppermute | solution.py:37
  83.9 0.7 copy-start.9
  84.6 0.9 copy-start.7
  89.2 23.3 %all-to-all-start.1 = ((bf16[32,16,1152]{2,1,0:T(8,128)(2,1)}), bf16[32,16,1152]{2,1,0:T(8,128)(2,1)S(1)}, u32[]{:S(2)}, u32[]{:S(2)}) async-start(bf16[32,16,1152]{2,1,0:T(8,128)(2,1)} %get-tuple-element.47), calls=%async_computation.1 | async-start | bytes 2359296 | tf_op jit(solution)/shard_map/all_to_all | solution.py:45
  93.8 4.8 %collective-permute-start.17 = (bf16[112,512]{1,0:T(8,128)(2,1)}, bf16[112,512]{1,0:T(8,128)(2,1)S(1)}, u32[]{:S(2)}, u32[]{:S(2)}) collective-permute-start(bf16[112,512]{1,0:T(8,128)(2,1)} %get-tuple-element.48.refs_0_), channel_id=1, source_target_pairs={{0,7},{1,0},{2,1},{3,2},{4,3},{5,4},{6,5},{7,6},{8,15},{9,8},{10,9... | collective-permute-start | bytes 344072 | tf_op jit(solution)/shard_map/ppermute | solution.py:41
  93.9 6.2 %collective-permute-start.15 = (bf16[112,512]{1,0:T(8,128)(2,1)}, bf16[112,512]{1,0:T(8,128)(2,1)S(1)}, u32[]{:S(2)}, u32[]{:S(2)}) collective-permute-start(bf16[112,512]{1,0:T(8,128)(2,1)} %get-tuple-element.48.refs_0_), channel_id=1, source_target_pairs={{0,1},{1,2},{2,3},{3,4},{4,5},{5,6},{6,7},{7,0},{8,9},{9,10},{10,1... | collective-permute-start | bytes 344072 | tf_op jit(solution)/shard_map/ppermute | solution.py:41
  98.6 14.2 %copy-start.10 = (bf16[112,512]{1,0:T(8,128)(2,1)}, bf16[112,512]{1,0:T(8,128)(2,1)S(1)}, u32[]{:S(2)}) copy-start(bf16[112,512]{1,0:T(8,128)(2,1)S(1)} %collective-permute-done.17.refs_2_) | copy-start | bytes 344068
  98.6 3.9 %collective-permute-start.18 = (bf16[112,512]{1,0:T(8,128)(2,1)S(1)}, bf16[112,512]{1,0:T(8,128)(2,1)}, u32[]{:S(2)}, u32[]{:S(2)}) collective-permute-start(bf16[112,512]{1,0:T(8,128)(2,1)S(1)} %collective-permute-done.17.refs_2_), channel_id=1, source_target_pairs={{0,7},{1,0},{2,1},{3,2},{4,3},{5,4},{6,5},{7,6},{8,15},{9,8},{10,9... | collective-permute-start | bytes 344072 | tf_op jit(solution)/shard_map/ppermute | solution.py:41
  100.1 12.7 %copy-start.11 = (bf16[112,512]{1,0:T(8,128)(2,1)}, bf16[112,512]{1,0:T(8,128)(2,1)S(1)}, u32[]{:S(2)}) copy-start(bf16[112,512]{1,0:T(8,128)(2,1)S(1)} %collective-permute-done.15.refs_1_) | copy-start | bytes 344068
  100.1 5.1 %collective-permute-start.16 = (bf16[112,512]{1,0:T(8,128)(2,1)S(1)}, bf16[112,512]{1,0:T(8,128)(2,1)}, u32[]{:S(2)}, u32[]{:S(2)}) collective-permute-start(bf16[112,512]{1,0:T(8,128)(2,1)S(1)} %collective-permute-done.15.refs_1_), channel_id=1, source_target_pairs={{0,1},{1,2},{2,3},{3,4},{4,5},{5,6},{6,7},{7,0},{8,9},{9,10},{10,1... | collective-permute-start | bytes 344072 | tf_op jit(solution)/shard_map/ppermute | solution.py:41
  112.5 2.7 %copy-start.3 = (bf16[32,16,1152]{2,1,0:T(8,128)(2,1)}, bf16[32,16,1152]{2,1,0:T(8,128)(2,1)S(1)}, u32[]{:S(2)}) copy-start(bf16[32,16,1152]{2,1,0:T(8,128)(2,1)S(1)} %all-to-all-done.1.arrived_ref) | copy-start | bytes 3538948
  112.5 9.0 %collective-permute-start.19 = (bf16[112,512]{1,0:T(8,128)(2,1)}, bf16[112,512]{1,0:T(8,128)(2,1)}, u32[]{:S(2)}, u32[]{:S(2)}) collective-permute-start(bf16[112,512]{1,0:T(8,128)(2,1)} %collective-permute-done.16.refs_3_), channel_id=1, source_target_pairs={{0,1},{1,2},{2,3},{3,4},{4,5},{5,6},{6,7},{7,0},{8,9},{9,10},{10,1... | collective-permute-start | bytes 344072 | tf_op jit(solution)/shard_map/ppermute | solution.py:41
  112.8 8.8 %collective-permute-start.20 = (bf16[112,512]{1,0:T(8,128)(2,1)}, bf16[112,512]{1,0:T(8,128)(2,1)}, u32[]{:S(2)}, u32[]{:S(2)}) collective-permute-start(bf16[112,512]{1,0:T(8,128)(2,1)} %collective-permute-done.18.refs_4_), channel_id=1, source_target_pairs={{0,7},{1,0},{2,1},{3,2},{4,3},{5,4},{6,5},{7,6},{8,15},{9,8},{10,9... | collective-permute-start | bytes 344072 | tf_op jit(solution)/shard_map/ppermute | solution.py:41
  117.8 14.4 %all-to-all-start.2 = ((bf16[8,16,896]{2,1,0:T(8,128)(2,1)}), bf16[8,16,896]{2,1,0:T(8,128)(2,1)S(1)}, u32[]{:S(2)}, u32[]{:S(2)}) async-start(bf16[8,16,896]{2,1,0:T(8,128)(2,1)} %choose.1), calls=%async_computation.2 | async-start | bytes 458752 | tf_op jit(solution)/shard_map/all_to_all | solution.py:45
  132.2 0.7 copy-start.6
  134.9 17.3 %copy-start.14 = (bf16[32,512]{1,0:T(8,128)(2,1)S(1)}, bf16[32,512]{1,0:T(8,128)(2,1)}, u32[]{:S(2)}) copy-start(bf16[32,512]{1,0:T(8,128)(2,1)} %get-tuple-element.59) | copy-start | bytes 98308
  134.9 13.5 %all-to-all-start.3 = ((bf16[16,16,1024]{2,1,0:T(8,128)(2,1)}), bf16[16,16,1024]{2,1,0:T(8,128)(2,1)S(1)}, u32[]{:S(2)}, u32[]{:S(2)}) async-start(bf16[16,16,1024]{2,1,0:T(8,128)(2,1)} %get-tuple-element.53), calls=%async_computation.3 | async-start | bytes 1048576 | tf_op jit(solution)/shard_map/all_to_all | solution.py:45
  139.4 4.7 %collective-permute-start.21 = (bf16[64,512]{1,0:T(8,128)(2,1)S(1)}, bf16[64,512]{1,0:T(8,128)(2,1)S(1)}, u32[]{:S(2)}, u32[]{:S(2)}) collective-permute-start(bf16[64,512]{1,0:T(8,128)(2,1)S(1)} %slice.112), channel_id=1, source_target_pairs={{0,1},{1,2},{2,3},{3,4},{4,5},{5,6},{6,7},{7,0},{8,9},{9,10},{10,1... | collective-permute-start | bytes 196616 | tf_op jit(solution)/shard_map/ppermute | solution.py:41
  140.3 3.8 %collective-permute-start.22 = (bf16[48,512]{1,0:T(8,128)(2,1)S(1)}, bf16[48,512]{1,0:T(8,128)(2,1)S(1)}, u32[]{:S(2)}, u32[]{:S(2)}) collective-permute-start(bf16[48,512]{1,0:T(8,128)(2,1)S(1)} %slice.113), channel_id=1, source_target_pairs={{0,7},{1,0},{2,1},{3,2},{4,3},{5,4},{6,5},{7,6},{8,15},{9,8},{10,9... | collective-permute-start | bytes 147464 | tf_op jit(solution)/shard_map/ppermute | solution.py:41
  144.1 0.6 copy-start.13
  144.7 0.6 copy-start.12
  147.6 4.9 %copy-start.4 = (bf16[896,512]{1,0:T(8,128)(2,1)S(1)}, bf16[896,512]{1,0:T(8,128)(2,1)}, u32[]{:S(2)}) copy-start(bf16[896,512]{1,0:T(8,128)(2,1)} %panel.1) | copy-start | bytes 2752516
  148.4 3.8 %collective-permute-start.23 = (bf16[256,1024]{1,0:T(8,128)(2,1)S(1)}, bf16[256,1024]{1,0:T(8,128)(2,1)S(1)}, u32[]{:S(2)}, u32[]{:S(2)}) collective-permute-start(bf16[256,1024]{1,0:T(8,128)(2,1)S(1)} %bitcast.97), channel_id=1, source_target_pairs={{0,8},{8,0},{1,9},{9,1},{2,10},{10,2},{3,11},{11,3},{4,12},{12,4},... | collective-permute-start | bytes 1572872 | tf_op jit(solution)/shard_map/ppermute | solution.py:37

commit v2 on v1

--- a/solution.py
+++ b/solution.py
@@ -189,24 +189,53 @@
     )(shift, pieces)
 
 
-def panel_kernel(pos_ref, *refs):
-    panel_ref = refs[-1]
+def slab_kernel(pos_ref, count_ref, *refs):
+    pieces = refs[:9]
+    near, far, total_ref, wh_ref, slab_ref, new_ref, grad_ref, panel_ref = refs[9:]
     z = pos_ref[4]
-    n = refs[0].shape[0]
-    for piece, d, r0 in zip(refs[:9], (0, -1, 1, -2, 2, -3, 3, -4, 4), (0,) * 8 + (64,)):
-        at = pl.multiple_of(((z + d + 8) % 8) * n + r0, 16)
-        panel_ref[pl.ds(at, piece.shape[0]), :] = piece[...]
-
-
-def panel_call(pos, pieces):
-    rows = 8 * pieces[0].shape[0]
-    return pl.pallas_call(
-        panel_kernel,
-        out_shape=jax.ShapeDtypeStruct((rows, 512), BF16),
-        in_specs=[SMEM] + [VMEM] * len(pieces),
-        out_specs=VMEM,
-        name="panel",
-    )(pos, *pieces)
+    n = pieces[0].shape[0]
+
+    @pl.when(pl.program_id(0) == 0)
+    def _():
+        for piece, d, r0 in zip(pieces, (0, -1, 1, -2, 2, -3, 3, -4, 4), (0,) * 8 + (64,)):
+            at = pl.multiple_of(((z + d + 8) % 8) * n + r0, 16)
+            panel_ref[pl.ds(at, piece.shape[0]), :] = piece[...]
+
+    scale = 1.0 / jnp.full((1, 1), count_ref[0].astype(F32), F32)
+    gram = jnp.dot(panel_ref[:, :256], near[...], preferred_element_type=F32)
+    gram += jnp.dot(panel_ref[:, 256:], far[...], preferred_element_type=F32)
+    new_ref[...] = slab_ref[...] + gram * scale
+    added = jnp.dot(total_ref[:, :256], near[...], preferred_element_type=F32)
+    added += jnp.dot(total_ref[:, 256:], far[...], preferred_element_type=F32)
+    grad_ref[...] = wh_ref[...] + (added[:16] + added[16:]) * scale
+
+
+def slab_call(pos, count, pieces, near, far, total, wh, slab):
+    rows, width = slab.shape
+    step = 512
+
+    def fixed(a):
+        return pl.BlockSpec(a.shape, lambda k, *_: (0,) * a.ndim)
+
+    def columns(r):
+        return pl.BlockSpec((r, step), lambda k, *_: (0, k))
+
+    return pl.pallas_call(
+        slab_kernel,
+        grid_spec=pltpu.PrefetchScalarGridSpec(
+            num_scalar_prefetch=2,
+            grid=(width // step,),
+            in_specs=[fixed(p) for p in pieces]
+            + [columns(256), columns(256), fixed(total), columns(16), columns(rows)],
+            out_specs=(columns(rows), columns(16)),
+            scratch_shapes=[pltpu.VMEM((rows, 512), BF16)],
+        ),
+        out_shape=(
+            jax.ShapeDtypeStruct((rows, width), F32),
+            jax.ShapeDtypeStruct((16, width), F32),
+        ),
+        name="slab",
+    )(pos, count, *pieces, near, far, total, wh, slab)
 
 
 def on_device(tokens, gate_weight, up_weight, hessian_slab, weight_error, slab_offset, token_count):
@@ -252,27 +281,25 @@
 
     b1 = plane_permute(b0, 0, 1)
     b3 = plane_permute(b0, 0, 3)
-    wh_far = core_swap(wh_sent)
-    wh = (wh_own + wh_far).astype(BF16)
+    b2 = plane_permute(b0, 0, 2)
     weights = weights_call(pos, gate_t, up_t, far_w.reshape(2, 2, n, quarter))
-    b1, b3, weights = lax.optimization_barrier((b1, b3, weights))
-    b2a = plane_permute(b1[:32], 0, 3)
-    b2b = plane_permute(b3[32:], 0, 1)
-    b2a, b2b, wh = lax.optimization_barrier((b2a, b2b, wh))
     sb = jnp.concatenate([b1, b3], 0)
     s3b = plane_permute(sb, 1, 3)
     s1b = plane_permute(sb, 1, 1)
-    sa = jnp.concatenate([b0, b2a, b2b], 0)
+    sa = jnp.concatenate([b0, b2], 0)
     s1a = plane_permute(sa, 1, 1)
     s3a = plane_permute(sa, 1, 3)
     s2b = plane_permute(s3b, 1, 1)
     s2a = plane_permute(s1a, 1, 3)
+    wh_far = core_swap(wh_sent)
+    wh = (wh_own + wh_far).astype(BF16)
     own, far = [], []
     for buffer, f in zip((sa, sb, s1a, s1b, s3a, s3b, s2a, s2b), (0, 1 - c, c, 1, c, 1, 0, 1 - c)):
         mine, theirs = products(buffer, weights, f)
         own.append(mine)
         far.append(theirs)
-    far = [core_swap(jnp.concatenate(part, 0)) for part in (far[:6], far[6:])]
+    far = [jnp.concatenate(part, 0) for part in (far[:6], far[6:])]
+    far = [core_swap(part) for part in far]
     sent, hidden_t = activate_call(pos, own, far, (high, low), wh, n)
 
     f1, g1 = shift_z(hidden_t, 1), shift_z(hidden_t, -1)
@@ -282,7 +309,8 @@
     f3, g3 = shift_z(f2, 1), shift_z(g2, -1)
     panel_width = 8 * n
     starts = slab_offset[0] + jnp.arange(8, dtype=jnp.int32) * width
-    pieces = exchange(choose_call(jnp.minimum(starts // panel_width, 29), arrived), "gc")
+    wanted = choose_call(jnp.minimum(starts // panel_width, 29), arrived)
+    pieces = exchange(wanted, "gc")
     sums = jnp.sum(arrived[:, :, 640:].reshape(16, 2, 16, half).astype(F32), axis=0)
     wh = jnp.concatenate([sums[0], sums[1]], 1)
     pieces, f3, g3, wh = lax.optimization_barrier((pieces, f3, g3, wh))
@@ -291,13 +319,9 @@
     shift = start - jnp.minimum(start // panel_width, 29) * panel_width
     chunk, total = assemble_call(pieces, jnp.stack([shift, c]).astype(jnp.int32), width, n)
     near = exchange(chunk, PLANE).reshape(256, width)
-    panel_t = panel_call(pos, (hidden_t, f1, g1, f2, g2, f3, g3, f4, g4))
-    near, panel_t = lax.optimization_barrier((near, panel_t))
-    window = jnp.concatenate([near, core_swap(near)], 0)
-    scale = 1.0 / token_count[0].astype(F32)
-    gram = jnp.dot(panel_t, window, preferred_element_type=F32)
-    added = jnp.dot(total, window, preferred_element_type=F32)
-    return (hessian_slab + gram * scale, wh + (added[:16] + added[16:]) * scale)
+    return slab_call(
+        pos, token_count, (hidden_t, f1, g1, f2, g2, f3, g3, f4, g4), near, core_swap(near), total, wh, hessian_slab
+    )
 
 
 def solution(mesh):

time: 159 us -> 154 us (0.969)
  blocking collectives: 0 us -> 13.6 us
  starting transfers between devices: 51.8 us -> 44.4 us
  matrix products: 28.3 us -> 22.1 us
  waiting for transfers between devices: 38.2 us -> 34.1 us
  local copies, waits for them, and re-layouts: 15.8 us -> 12 us
  Pallas kernels: 14.7 us -> 17.7 us
    all_to_all x0 -> x1, blocking collectives: none -> 13.6 us  [exchange(): return lax.all_to_all(array, axes, split_axis=0, concat_axis=0, tiled=True)]
    ppermute x6, starting transfers between devices: 15 us -> 9.57 us  [core_swap(): return lax.ppermute(array, 'gr_2', [(0, 1), (1, 0)])]
    dot_general x2 -> x0, matrix products: 5.3 us -> none  [the longest x1 5.02 us: on_device(): gram = jnp.dot(panel_t, window, preferred_element_type=F32)]
    pallas_call x1, Pallas kernels: 2.25 us -> 5.31 us  [slab_call(): pl.pallas_call(slab_kernel, grid_spec=pltpu.PrefetchScalarGridSpec(num_sc...]
    unnamed x34 -> x26, local copies, waits for them, and re-layouts: 6.69 us -> 3.95 us
    all_to_all x4 -> x3, starting transfers between devices: 18.4 us -> 15.9 us  [exchange(): return lax.all_to_all(array, axes, split_axis=0, concat_axis=0, tiled=True)]
    ppermute x10 -> x9, waiting for transfers between devices: 5.75 us -> 3.56 us  [plane_permute(): return lax.ppermute(array, CAL_GR, pairs)]
    slice x2 -> x0, local copies, waits for them, and re-layouts: 1.83 us -> none  [the longest x1 0.92 us: on_device(): b2b = plane_permute(b3[32:], 0, 1)]
  transfers between devices with their start and end apart: 28 -> 26, of which waited for: 12 -> 10; matrix products, arithmetic and copies ran while one was open for 21% -> 22% of each run, Pallas kernels for 6% -> 4%
where the time goes in v2:
time: 154 us; the launch traced here: 153 us
  starting transfers between devices  44.4 us (29%)
  waiting for transfers between devices  34.1 us (22%)
  matrix products  22.1 us (14%)
  Pallas kernels  17.7 us (11%)
  blocking collectives  13.6 us (9%)
  local copies, waits for them, and re-layouts  12 us (8%)
  other arithmetic  7 us (5%)
  between operations  2.43 us (2%)
    all_to_all x3, waiting for transfers between devices, exchange(): return lax.all_to_all(array, axes, split_axis=0, concat_axis=0, tiled=True)  22.5 us
    all_to_all x3, starting transfers between devices, exchange(): return lax.all_to_all(array, axes, split_axis=0, concat_axis=0, tiled=True)  15.9 us
    dot_general x16, matrix products, products(): lax.dot_general(tokens, half, NT, preferred_element_type=F32)  15.8 us
    all_to_all x1, blocking collectives, exchange(): return lax.all_to_all(array, axes, split_axis=0, concat_axis=0, tiled=True)  13.6 us
    ppermute x9, starting transfers between devices, plane_permute(): return lax.ppermute(array, CAL_GR, pairs)  10.6 us
    ppermute x6, starting transfers between devices, core_swap(): return lax.ppermute(array, 'gr_2', [(0, 1), (1, 0)])  9.57 us
    ppermute x8, starting transfers between devices, shift_z(): return lax.ppermute(array, 'gc', [(i, (i + d) % 8) for i in range(8)])  8.39 us
    ppermute x8, waiting for transfers between devices, shift_z(): return lax.ppermute(array, 'gc', [(i, (i + d) % 8) for i in range(8)])  7.16 us
  transfers between devices with their start and end apart: 26, of which 10 were waited for; matrix products, arithmetic and copies ran while one was open for 22% of the time, Pallas kernels for 4%

profile of v2, /device:TPU:1, one launch (start us, length us, event | category | flops | bytes accessed | tf_op | source)
XLA Modules:
  0.0 153.4 jit_solution(1463332152906331326)
XLA Ops:
  0.7 0.9 constant_dynamic-slice_fusion.1
  1.5 3.2 %collective-permute-start = (bf16[4,2048]{1,0:T(4,128)(2,1)S(1)}, bf16[4,2048]{1,0:T(4,128)(2,1)S(1)}, u32[]{:S(2)}, u32[]{:S(2)}) collective-permute-start(bf16[4,2048]{1,0:T(4,128)(2,1)S(1)} %constant_dynamic-slice_fusion.1), channel_id=1, source_target_pairs={{0,8},{8,0},{1,9},{9,1},{2,10},{10,2},{3,11},{11,3},{4,12},{12,4},... | collective-permute-start | bytes 49160 | tf_op jit(solution)/shard_map/ppermute | solution.py:37
  4.7 0.8 collective-permute-done
  5.6 0.7 broadcast_select_fusion.1
  6.3 0.7 broadcast_in_dim.2
  7.0 1.6 %dynamic-slice_bitcast_fusion.14 = (bf16[1,112,2048]{2,1,0:T(8,128)(2,1)S(1)}, bf16[1,112,2048]{2,1,0:T(8,128)(2,1)S(1)}, bf16[1,112,2048]{2,1,0:T(8,128)(2,1)S(1)}, bf16[1,112,2048]{2,1,0:T(8,128)(2,1)S(1)}) fusion(bf16[8192,112]{0,1:T(8,128)(2,1)} %param.9, s32[]{:T(128)S(6)} %select_n.61, s32[]{:T(128)S(6)} %select_n.62, bf16[8192,112]{0,1:T(8,128)(2,1)} %param.8), kind=kLoop, calls=%fused_computation.33 | loop fusion | bytes 3670024 | tf_op jit(solution)/shard_map/stack | solution.py:258
  8.6 1.5 pad_maximum_fusion
  10.4 6.5 %all-to-all-start = ((bf16[8,8,2048]{2,1,0:T(8,128)(2,1)}), bf16[8,8,2048]{2,1,0:T(8,128)(2,1)S(1)}, u32[]{:S(2)}, u32[]{:S(2)}) async-start(bf16[8,8,2048]{2,1,0:T(8,128)(2,1)} %broadcast_in_dim.2), calls=%async_computation | async-start | bytes 524288 | tf_op jit(solution)/shard_map/all_to_all | solution.py:45
  17.0 4.4 %fusion = f32[512,512]{1,0:T(8,128)} fusion(f32[512,896]{1,0:T(8,128)S(1)} %copy-done, f32[896,1024]{1,0:T(8,128)} %refs_13_.1, s32[]{:T(128)S(6)} %select_n.60), kind=kOutput, calls=%fused_computation.1 | convolution fusion | flops 1409286144 | bytes 4718596 | tf_op jit(solution)/shard_map/dot_general | solution.py:270
  21.5 0.7 subtract_convert_fusion.refs_11_
  22.2 0.7 pad_convert_fusion.refs_10_
  22.8 1.9 %fusion.2 = f32[512,512]{1,0:T(8,128)S(1)} fusion(f32[512,896]{1,0:T(8,128)S(1)} %copy-done, f32[896,1024]{1,0:T(8,128)S(1)} %copy-done.2, s32[]{:T(128)S(6)} %select_n.59), kind=kOutput, calls=%fused_computation.3 | convolution fusion | flops 1409286144 | bytes 4718596 | tf_op jit(solution)/shard_map/dot_general | solution.py:270
  24.8 4.4 %all-to-all-done = bf16[8,8,2048]{2,1,0:T(8,128)(2,1)S(1)} async-done(((bf16[8,8,2048]{2,1,0:T(8,128)(2,1)}), bf16[8,8,2048]{2,1,0:T(8,128)(2,1)S(1)}, u32[]{:S(2)}, u32[]{:S(2)}) %all-to-all-start) | async-done | bytes 262176 | tf_op jit(solution)/shard_map/all_to_all | solution.py:45
  29.1 2.9 %collective-permute-start.2 = (bf16[64,2048]{1,0:T(8,128)(2,1)S(1)}, bf16[64,2048]{1,0:T(8,128)(2,1)S(1)}, u32[]{:S(2)}, u32[]{:S(2)}) collective-permute-start(bf16[64,2048]{1,0:T(8,128)(2,1)S(1)} %bitcast.91), channel_id=1, source_target_pairs={{0,64},{8,40},{16,80},{24,56},{32,96},{40,8},{48,112},{56,24},{128... | collective-permute-start | bytes 786440 | tf_op jit(solution)/shard_map/ppermute | solution.py:33
  32.0 0.7 stack.45.pos_ref
  32.7 0.8 collective-permute-start.4
  33.5 0.7 constant_dynamic-update-slice_fusion.1
  34.2 1.1 collective-permute-start.13
  35.3 4.3 %weights.1 = bf16[2,512,2048]{2,1,0:T(8,128)(2,1)} custom-call(s32[5]{0:T(128)} %stack.45.pos_ref, bf16[112,8192]{1,0:T(8,128)(2,1)} %bitcast.86, bf16[112,8192]{1,0:T(8,128)(2,1)} %bitcast.87, bf16[2,2,112,2048]{3,2,1,0:T(8,128)(2,1)} %bitcast.16.far), custom_call_target="tpu_custom_call" | custom-call | tf_op jit(solution)/shard_map/weights/pallas_call | solution.py:66
  39.5 0.7 constant_dynamic-update-slice_fusion
  40.3 1.8 %collective-permute-start.7 = (bf16[128,2048]{1,0:T(8,128)(2,1)}, bf16[128,2048]{1,0:T(8,128)(2,1)S(1)}, u32[]{:S(2)}, u32[]{:S(2)}) collective-permute-start(bf16[128,2048]{1,0:T(8,128)(2,1)} %constant_dynamic-update-slice_fusion), channel_id=1, source_target_pairs={{0,48},{8,200},{16,32},{24,216},{32,16},{40,232},{48,0},{56,248},{... | collective-permute-start | bytes 1572872 | tf_op jit(solution)/shard_map/ppermute | solution.py:33
  42.1 1.1 collective-permute-start.5
  43.2 1.0 constant_dynamic-update-slice_fusion.3
  44.2 1.0 constant_dynamic-update-slice_fusion.2
  45.2 0.9 collective-permute-start.8
  46.1 2.5 %fusion.5.refs_0_ = f32[128,256]{1,0:T(8,128)} fusion(bf16[128,2048]{1,0:T(8,128)(2,1)} %constant_dynamic-update-slice_fusion, bf16[2,512,2048]{2,1,0:T(8,128)(2,1)} %weights.1), kind=kOutput, calls=%fused_computation.22 | convolution fusion | flops 134217728 | bytes 1703936 | tf_op jit(solution)/shard_map/dot_general | solution.py:81
  48.7 1.9 %convolution_dynamic-update-slice_fusion.5 = f32[768,256]{1,0:T(8,128)S(1)} fusion(bf16[128,2048]{1,0:T(8,128)(2,1)} %constant_dynamic-update-slice_fusion, bf16[2,512,2048]{2,1,0:T(8,128)(2,1)} %weights.1), kind=kOutput, calls=%fused_computation.10 | convolution fusion | flops 134217728 | bytes 1703936 | tf_op jit(solution)/shard_map/dot_general | solution.py:81
  50.5 1.1 fusion.10.refs_1_
  52.7 3.5 %collective-permute-done.6 = bf16[128,2048]{1,0:T(8,128)(2,1)S(1)} collective-permute-done((bf16[128,2048]{1,0:T(8,128)(2,1)S(1)}, bf16[128,2048]{1,0:T(8,128)(2,1)S(1)}, u32[]{:S(2)}, u32[]{:S(2)}) %collective-permute-start.6) | collective-permute-done | bytes 524320 | tf_op jit(solution)/shard_map/ppermute | solution.py:33
  57.7 2.1 %collective-permute-start.11 = (f32[768,256]{1,0:T(8,128)S(1)}, f32[768,256]{1,0:T(8,128)}, u32[]{:S(2)}, u32[]{:S(2)}) collective-permute-start(f32[768,256]{1,0:T(8,128)S(1)} %convolution_dynamic-update-slice_fusion), channel_id=1, source_target_pairs={{0,8},{8,0},{1,9},{9,1},{2,10},{10,2},{3,11},{11,3},{4,12},{12,4},... | collective-permute-start | bytes 2359304 | tf_op jit(solution)/shard_map/ppermute | solution.py:37
  59.9 1.8 %collective-permute-start.9 = (bf16[128,2048]{1,0:T(8,128)(2,1)S(1)}, bf16[128,2048]{1,0:T(8,128)(2,1)S(1)}, u32[]{:S(2)}, u32[]{:S(2)}) collective-permute-start(bf16[128,2048]{1,0:T(8,128)(2,1)S(1)} %collective-permute-done.5), channel_id=1, source_target_pairs={{0,48},{8,200},{16,32},{24,216},{32,16},{40,232},{48,0},{56,248},{... | collective-permute-start | bytes 1572872 | tf_op jit(solution)/shard_map/ppermute | solution.py:33
  61.7 1.1 collective-permute-start.10
  62.8 1.1 fusion.11.refs_4_
  64.0 1.1 fusion.6.refs_5_
  65.1 1.1 fusion.7.refs_3_
  66.3 1.1 fusion.12.refs_2_
  67.4 2.2 %add_convert_fusion.refs_12_ = bf16[512,512]{1,0:T(8,128)(2,1)} fusion(f32[512,512]{1,0:T(8,128)S(1)} %fusion.2, f32[512,512]{1,0:T(8,128)} %collective-permute-done.13), kind=kLoop, calls=%fused_computation.20 | loop fusion | flops 524288 | bytes 2621440 | tf_op jit(solution)/shard_map/convert_element_type | solution.py:295
  70.6 0.9 collective-permute-start.12
  71.5 1.1 fusion.9.refs_7_
  72.6 1.1 fusion.4.refs_6_
  73.8 0.7 copy-done.7
  74.5 3.7 %activate.1 = (bf16[32,16,1152]{2,1,0:T(8,128)(2,1)}, bf16[112,512]{1,0:T(8,128)(2,1)}) custom-call(s32[5]{0:T(128)} %stack.45.pos_ref, f32[128,256]{1,0:T(8,128)} %fusion.5.refs_0_, f32[128,256]{1,0:T(8,128)} %fusion.10.refs_1_, f32[128,256]{1,0:T(8,128)} %fusion.12.refs_2_, f32[128,256]{1,0:T(8,128)} %fusion.7.refs_3_, f32[128,256]{1,0:T(8,128)} %fusion.11.refs_4_, ...), custom_call_target="tpu_custom_call" | custom-call | tf_op jit(solution)/shard_map/activate/pallas_call | solution.py:121
  78.1 6.1 %all-to-all-start.1 = ((bf16[32,16,1152]{2,1,0:T(8,128)(2,1)}), bf16[32,16,1152]{2,1,0:T(8,128)(2,1)S(1)}, u32[]{:S(2)}, u32[]{:S(2)}) async-start(bf16[32,16,1152]{2,1,0:T(8,128)(2,1)} %get-tuple-element.34), calls=%async_computation.1 | async-start | bytes 2359296 | tf_op jit(solution)/shard_map/all_to_all | solution.py:45
  84.3 1.5 collective-permute-start.14
  86.4 2.5 %collective-permute-done.15.refs_2_ = bf16[112,512]{1,0:T(8,128)(2,1)S(1)} collective-permute-done((bf16[112,512]{1,0:T(8,128)(2,1)}, bf16[112,512]{1,0:T(8,128)(2,1)S(1)}, u32[]{:S(2)}, u32[]{:S(2)}) %collective-permute-start.15) | collective-permute-done | bytes 114720 | tf_op jit(solution)/shard_map/ppermute | solution.py:41
  89.0 1.5 collective-permute-start.17
  90.5 0.6 pad_add_fusion.refs_0_
  91.1 0.6 fusion.24.first_ref
  91.7 1.2 collective-permute-done.17.refs_4_
  92.9 2.7 %collective-permute-done.16.refs_3_ = bf16[112,512]{1,0:T(8,128)(2,1)} collective-permute-done((bf16[112,512]{1,0:T(8,128)(2,1)S(1)}, bf16[112,512]{1,0:T(8,128)(2,1)}, u32[]{:S(2)}, u32[]{:S(2)}) %collective-permute-start.16) | collective-permute-done | bytes 114720 | tf_op jit(solution)/shard_map/ppermute | solution.py:41
  95.6 7.3 %all-to-all-done.1.arrived_ref = bf16[32,16,1152]{2,1,0:T(8,128)(2,1)S(1)} async-done(((bf16[32,16,1152]{2,1,0:T(8,128)(2,1)}), bf16[32,16,1152]{2,1,0:T(8,128)(2,1)S(1)}, u32[]{:S(2)}, u32[]{:S(2)}) %all-to-all-start.1) | async-done | bytes 1179680 | tf_op jit(solution)/shard_map/all_to_all | solution.py:45
  103.2 2.4 %collective-permute-start.19 = (bf16[112,512]{1,0:T(8,128)(2,1)}, bf16[112,512]{1,0:T(8,128)(2,1)}, u32[]{:S(2)}, u32[]{:S(2)}) collective-permute-start(bf16[112,512]{1,0:T(8,128)(2,1)} %collective-permute-done.17.refs_4_), channel_id=1, source_target_pairs={{0,7},{1,0},{2,1},{3,2},{4,3},{5,4},{6,5},{7,6},{8,15},{9,8},{10,9... | collective-permute-start | bytes 344072 | tf_op jit(solution)/shard_map/ppermute | solution.py:41
  105.7 2.5 %choose.1 = bf16[8,16,896]{2,1,0:T(8,128)(2,1)} custom-call(s32[8]{0:T(128)} %fusion.24.first_ref, bf16[32,16,1152]{2,1,0:T(8,128)(2,1)} %copy-done.3), custom_call_target="tpu_custom_call" | custom-call | tf_op jit(solution)/shard_map/choose/pallas_call | solution.py:143
  108.2 3.4 %all-to-all-start.2 = ((bf16[8,16,896]{2,1,0:T(8,128)(2,1)}), bf16[8,16,896]{2,1,0:T(8,128)(2,1)S(1)}, u32[]{:S(2)}, u32[]{:S(2)}) async-start(bf16[8,16,896]{2,1,0:T(8,128)(2,1)} %choose.1), calls=%async_computation.2 | async-start | bytes 458752 | tf_op jit(solution)/shard_map/all_to_all | solution.py:45
  111.7 0.6 pad_maximum_fusion.2.refs_12_
  112.3 10.9 %all-to-all-done.2.refs_1_ = bf16[8,16,896]{2,1,0:T(8,128)(2,1)S(1)} async-done(((bf16[8,16,896]{2,1,0:T(8,128)(2,1)}), bf16[8,16,896]{2,1,0:T(8,128)(2,1)S(1)}, u32[]{:S(2)}, u32[]{:S(2)}) %all-to-all-start.2) | async-done | bytes 229408 | tf_op jit(solution)/shard_map/all_to_all | solution.py:45
  123.2 0.7 copy-done.5
  123.9 2.0 %assemble.1 = (bf16[16,16,1024]{2,1,0:T(8,128)(2,1)}, bf16[32,512]{1,0:T(8,128)(2,1)}) custom-call(s32[2]{0:T(128)} %pad_add_fusion.refs_0_, bf16[8,16,896]{2,1,0:T(8,128)(2,1)} %copy-done.5), custom_call_target="tpu_custom_call" | custom-call | tf_op jit(solution)/shard_map/assemble/pallas_call | solution.py:179
  125.9 13.6 %all_to_all.20 = bf16[16,16,1024]{2,1,0:T(8,128)(2,1)S(1)} all-to-all(bf16[16,16,1024]{2,1,0:T(8,128)(2,1)} %get-tuple-element.41), channel_id=1, replica_groups=mesh['cal'=2,'gr_0'=2,'gr_1'=4,'gr_2'=2,'gc'=8] {'cal','gr_0','gr_1'}, dimensions={0} | all-to-all | bytes 1048576 | tf_op jit(solution)/shard_map/all_to_all | solution.py:45
  139.5 1.9 %collective-permute-start.22 = (bf16[256,1024]{1,0:T(8,128)(2,1)S(1)}, bf16[256,1024]{1,0:T(8,128)(2,1)S(1)}, u32[]{:S(2)}, u32[]{:S(2)}) collective-permute-start(bf16[256,1024]{1,0:T(8,128)(2,1)S(1)} %bitcast.88), channel_id=1, source_target_pairs={{0,8},{8,0},{1,9},{9,1},{2,10},{10,2},{3,11},{11,3},{4,12},{12,4},... | collective-permute-start | bytes 1572872 | tf_op jit(solution)/shard_map/ppermute | solution.py:37
  141.4 0.8 slice.98
  142.3 0.8 slice.99
  143.1 2.7 %collective-permute-start.21 = (bf16[48,512]{1,0:T(8,128)(2,1)S(1)}, bf16[48,512]{1,0:T(8,128)(2,1)S(1)}, u32[]{:S(2)}, u32[]{:S(2)}) collective-permute-start(bf16[48,512]{1,0:T(8,128)(2,1)S(1)} %slice.99), channel_id=1, source_target_pairs={{0,7},{1,0},{2,1},{3,2},{4,3},{5,4},{6,5},{7,6},{8,15},{9,8},{10,9... | collective-permute-start | bytes 147464 | tf_op jit(solution)/shard_map/ppermute | solution.py:41
  147.9 5.3 %slab.1 = (f32[896,1024]{1,0:T(8,128)}, f32[16,1024]{1,0:T(8,128)}) custom-call(s32[5]{0:T(128)} %stack.45.pos_ref, s32[1]{0:T(128)S(6)} %copy.17.count_ref, bf16[112,512]{1,0:T(8,128)(2,1)} %get-tuple-element.33.refs_0_, bf16[112,512]{1,0:T(8,128)(2,1)} %copy-done.9, bf16[112,512]{1,0:T(8,128)(2,1)} %copy-done.8, ...), custom_call_target="tpu_custom_call" | custom-call | tf_op jit(solution)/shard_map/slab/pallas_call | solution.py:223
  (60 shorter events, 6.1 us)
Async XLA Ops:
  0.6 16.3 %copy-start = (f32[512,896]{1,0:T(8,128)S(1)}, f32[512,896]{1,0:T(8,128)}, u32[]{:S(2)}) copy-start(f32[512,896]{1,0:T(8,128)} %param.11) | copy-start | bytes 5505028
  1.5 4.0 %collective-permute-start = (bf16[4,2048]{1,0:T(4,128)(2,1)S(1)}, bf16[4,2048]{1,0:T(4,128)(2,1)S(1)}, u32[]{:S(2)}, u32[]{:S(2)}) collective-permute-start(bf16[4,2048]{1,0:T(4,128)(2,1)S(1)} %constant_dynamic-slice_fusion.1), channel_id=1, source_target_pairs={{0,8},{8,0},{1,9},{9,1},{2,10},{10,2},{3,11},{11,3},{4,12},{12,4},... | collective-permute-start | bytes 49160 | tf_op jit(solution)/shard_map/ppermute | solution.py:37
  10.1 19.1 %collective-permute-start.1 = (bf16[4,112,2048]{2,1,0:T(8,128)(2,1)}, bf16[4,112,2048]{2,1,0:T(8,128)(2,1)}, u32[]{:S(2)}, u32[]{:S(2)}) collective-permute-start(bf16[4,112,2048]{2,1,0:T(8,128)(2,1)} %pad_maximum_fusion), channel_id=1, source_target_pairs={{0,8},{8,0},{1,9},{9,1},{2,10},{10,2},{3,11},{11,3},{4,12},{12,4},... | collective-permute-start | bytes 5505032 | tf_op jit(solution)/shard_map/ppermute | solution.py:37
  10.4 18.7 %all-to-all-start = ((bf16[8,8,2048]{2,1,0:T(8,128)(2,1)}), bf16[8,8,2048]{2,1,0:T(8,128)(2,1)S(1)}, u32[]{:S(2)}, u32[]{:S(2)}) async-start(bf16[8,8,2048]{2,1,0:T(8,128)(2,1)} %broadcast_in_dim.2), calls=%async_computation | async-start | bytes 524288 | tf_op jit(solution)/shard_map/all_to_all | solution.py:45
  16.9 6.0 %copy-start.2 = (f32[896,1024]{1,0:T(8,128)S(1)}, f32[896,1024]{1,0:T(8,128)}, u32[]{:S(2)}) copy-start(f32[896,1024]{1,0:T(8,128)} %refs_13_.1) | copy-start | bytes 11010052
  29.1 10.4 %collective-permute-start.2 = (bf16[64,2048]{1,0:T(8,128)(2,1)S(1)}, bf16[64,2048]{1,0:T(8,128)(2,1)S(1)}, u32[]{:S(2)}, u32[]{:S(2)}) collective-permute-start(bf16[64,2048]{1,0:T(8,128)(2,1)S(1)} %bitcast.91), channel_id=1, source_target_pairs={{0,64},{8,40},{16,80},{24,56},{32,96},{40,8},{48,112},{56,24},{128... | collective-permute-start | bytes 786440 | tf_op jit(solution)/shard_map/ppermute | solution.py:33
  32.7 11.5 %collective-permute-start.4 = (bf16[64,2048]{1,0:T(8,128)(2,1)S(1)}, bf16[64,2048]{1,0:T(8,128)(2,1)}, u32[]{:S(2)}, u32[]{:S(2)}) collective-permute-start(bf16[64,2048]{1,0:T(8,128)(2,1)S(1)} %bitcast.92), channel_id=1, source_target_pairs={{0,192},{8,56},{16,208},{24,40},{32,224},{40,24},{48,240},{56,8},{... | collective-permute-start | bytes 786440 | tf_op jit(solution)/shard_map/ppermute | solution.py:33
  33.5 9.7 %collective-permute-start.3 = (bf16[64,2048]{1,0:T(8,128)(2,1)S(1)}, bf16[64,2048]{1,0:T(8,128)(2,1)}, u32[]{:S(2)}, u32[]{:S(2)}) collective-permute-start(bf16[64,2048]{1,0:T(8,128)(2,1)S(1)} %bitcast.93), channel_id=1, source_target_pairs={{0,128},{8,24},{16,144},{24,8},{32,160},{40,56},{48,176},{56,40},{... | collective-permute-start | bytes 786440 | tf_op jit(solution)/shard_map/ppermute | solution.py:33
  34.2 33.2 %collective-permute-start.13 = (f32[512,512]{1,0:T(8,128)}, f32[512,512]{1,0:T(8,128)}, u32[]{:S(2)}, u32[]{:S(2)}) collective-permute-start(f32[512,512]{1,0:T(8,128)} %fusion), channel_id=1, source_target_pairs={{0,8},{8,0},{1,9},{9,1},{2,10},{10,2},{3,11},{11,3},{4,12},{12,4},... | collective-permute-start | bytes 3145736 | tf_op jit(solution)/shard_map/ppermute | solution.py:37
  39.5 11.0 %copy-start.1 = (bf16[2,512,2048]{2,1,0:T(8,128)(2,1)S(1)}, bf16[2,512,2048]{2,1,0:T(8,128)(2,1)}, u32[]{:S(2)}) copy-start(bf16[2,512,2048]{2,1,0:T(8,128)(2,1)} %weights.1) | copy-start | bytes 12582916
  40.3 16.5 %collective-permute-start.7 = (bf16[128,2048]{1,0:T(8,128)(2,1)}, bf16[128,2048]{1,0:T(8,128)(2,1)S(1)}, u32[]{:S(2)}, u32[]{:S(2)}) collective-permute-start(bf16[128,2048]{1,0:T(8,128)(2,1)} %constant_dynamic-update-slice_fusion), channel_id=1, source_target_pairs={{0,48},{8,200},{16,32},{24,216},{32,16},{40,232},{48,0},{56,248},{... | collective-permute-start | bytes 1572872 | tf_op jit(solution)/shard_map/ppermute | solution.py:33
  42.1 10.1 %collective-permute-start.5 = (bf16[128,2048]{1,0:T(8,128)(2,1)}, bf16[128,2048]{1,0:T(8,128)(2,1)S(1)}, u32[]{:S(2)}, u32[]{:S(2)}) collective-permute-start(bf16[128,2048]{1,0:T(8,128)(2,1)} %constant_dynamic-update-slice_fusion), channel_id=1, source_target_pairs={{0,16},{8,136},{16,0},{24,152},{32,48},{40,168},{48,32},{56,184},{... | collective-permute-start | bytes 1572872 | tf_op jit(solution)/shard_map/ppermute | solution.py:33
  45.2 12.1 %collective-permute-start.8 = (bf16[128,2048]{1,0:T(8,128)(2,1)S(1)}, bf16[128,2048]{1,0:T(8,128)(2,1)S(1)}, u32[]{:S(2)}, u32[]{:S(2)}) collective-permute-start(bf16[128,2048]{1,0:T(8,128)(2,1)S(1)} %constant_dynamic-update-slice_fusion.2), channel_id=1, source_target_pairs={{0,48},{8,200},{16,32},{24,216},{32,16},{40,232},{48,0},{56,248},{... | collective-permute-start | bytes 1572872 | tf_op jit(solution)/shard_map/ppermute | solution.py:33
  46.1 10.1 %collective-permute-start.6 = (bf16[128,2048]{1,0:T(8,128)(2,1)S(1)}, bf16[128,2048]{1,0:T(8,128)(2,1)S(1)}, u32[]{:S(2)}, u32[]{:S(2)}) collective-permute-start(bf16[128,2048]{1,0:T(8,128)(2,1)S(1)} %constant_dynamic-update-slice_fusion.2), channel_id=1, source_target_pairs={{0,16},{8,136},{16,0},{24,152},{32,48},{40,168},{48,32},{56,184},{... | collective-permute-start | bytes 1572872 | tf_op jit(solution)/shard_map/ppermute | solution.py:33
  57.7 16.0 %collective-permute-start.11 = (f32[768,256]{1,0:T(8,128)S(1)}, f32[768,256]{1,0:T(8,128)}, u32[]{:S(2)}, u32[]{:S(2)}) collective-permute-start(f32[768,256]{1,0:T(8,128)S(1)} %convolution_dynamic-update-slice_fusion), channel_id=1, source_target_pairs={{0,8},{8,0},{1,9},{9,1},{2,10},{10,2},{3,11},{11,3},{4,12},{12,4},... | collective-permute-start | bytes 2359304 | tf_op jit(solution)/shard_map/ppermute | solution.py:37
  59.9 9.7 %collective-permute-start.9 = (bf16[128,2048]{1,0:T(8,128)(2,1)S(1)}, bf16[128,2048]{1,0:T(8,128)(2,1)S(1)}, u32[]{:S(2)}, u32[]{:S(2)}) collective-permute-start(bf16[128,2048]{1,0:T(8,128)(2,1)S(1)} %collective-permute-done.5), channel_id=1, source_target_pairs={{0,48},{8,200},{16,32},{24,216},{32,16},{40,232},{48,0},{56,248},{... | collective-permute-start | bytes 1572872 | tf_op jit(solution)/shard_map/ppermute | solution.py:33
  61.7 8.4 %collective-permute-start.10 = (bf16[128,2048]{1,0:T(8,128)(2,1)S(1)}, bf16[128,2048]{1,0:T(8,128)(2,1)S(1)}, u32[]{:S(2)}, u32[]{:S(2)}) collective-permute-start(bf16[128,2048]{1,0:T(8,128)(2,1)S(1)} %collective-permute-done.8), channel_id=1, source_target_pairs={{0,16},{8,136},{16,0},{24,152},{32,48},{40,168},{48,32},{56,184},{... | collective-permute-start | bytes 1572872 | tf_op jit(solution)/shard_map/ppermute | solution.py:33
  70.6 3.1 %collective-permute-start.12 = (f32[256,256]{1,0:T(8,128)S(1)}, f32[256,256]{1,0:T(8,128)S(1)}, u32[]{:S(2)}, u32[]{:S(2)}) collective-permute-start(f32[256,256]{1,0:T(8,128)S(1)} %pad_maximum_fusion.1), channel_id=1, source_target_pairs={{0,8},{8,0},{1,9},{9,1},{2,10},{10,2},{3,11},{11,3},{4,12},{12,4},... | collective-permute-start | bytes 786440 | tf_op jit(solution)/shard_map/ppermute | solution.py:37
  73.8 0.7 copy-start.7
  78.1 24.8 %all-to-all-start.1 = ((bf16[32,16,1152]{2,1,0:T(8,128)(2,1)}), bf16[32,16,1152]{2,1,0:T(8,128)(2,1)S(1)}, u32[]{:S(2)}, u32[]{:S(2)}) async-start(bf16[32,16,1152]{2,1,0:T(8,128)(2,1)} %get-tuple-element.34), calls=%async_computation.1 | async-start | bytes 2359296 | tf_op jit(solution)/shard_map/all_to_all | solution.py:45
  84.2 4.8 %collective-permute-start.15 = (bf16[112,512]{1,0:T(8,128)(2,1)}, bf16[112,512]{1,0:T(8,128)(2,1)S(1)}, u32[]{:S(2)}, u32[]{:S(2)}) collective-permute-start(bf16[112,512]{1,0:T(8,128)(2,1)} %get-tuple-element.33.refs_0_), channel_id=1, source_target_pairs={{0,7},{1,0},{2,1},{3,2},{4,3},{5,4},{6,5},{7,6},{8,15},{9,8},{10,9... | collective-permute-start | bytes 344072 | tf_op jit(solution)/shard_map/ppermute | solution.py:41
  84.3 6.2 %collective-permute-start.14 = (bf16[112,512]{1,0:T(8,128)(2,1)}, bf16[112,512]{1,0:T(8,128)(2,1)S(1)}, u32[]{:S(2)}, u32[]{:S(2)}) collective-permute-start(bf16[112,512]{1,0:T(8,128)(2,1)} %get-tuple-element.33.refs_0_), channel_id=1, source_target_pairs={{0,1},{1,2},{2,3},{3,4},{4,5},{5,6},{6,7},{7,0},{8,9},{9,10},{10,1... | collective-permute-start | bytes 344072 | tf_op jit(solution)/shard_map/ppermute | solution.py:41
  89.0 14.2 %copy-start.8 = (bf16[112,512]{1,0:T(8,128)(2,1)}, bf16[112,512]{1,0:T(8,128)(2,1)S(1)}, u32[]{:S(2)}) copy-start(bf16[112,512]{1,0:T(8,128)(2,1)S(1)} %collective-permute-done.15.refs_2_) | copy-start | bytes 344068
  89.0 3.9 %collective-permute-start.17 = (bf16[112,512]{1,0:T(8,128)(2,1)S(1)}, bf16[112,512]{1,0:T(8,128)(2,1)}, u32[]{:S(2)}, u32[]{:S(2)}) collective-permute-start(bf16[112,512]{1,0:T(8,128)(2,1)S(1)} %collective-permute-done.15.refs_2_), channel_id=1, source_target_pairs={{0,7},{1,0},{2,1},{3,2},{4,3},{5,4},{6,5},{7,6},{8,15},{9,8},{10,9... | collective-permute-start | bytes 344072 | tf_op jit(solution)/shard_map/ppermute | solution.py:41
  90.5 12.7 %copy-start.9 = (bf16[112,512]{1,0:T(8,128)(2,1)}, bf16[112,512]{1,0:T(8,128)(2,1)S(1)}, u32[]{:S(2)}) copy-start(bf16[112,512]{1,0:T(8,128)(2,1)S(1)} %collective-permute-done.14.refs_1_) | copy-start | bytes 344068
  90.5 5.1 %collective-permute-start.16 = (bf16[112,512]{1,0:T(8,128)(2,1)S(1)}, bf16[112,512]{1,0:T(8,128)(2,1)}, u32[]{:S(2)}, u32[]{:S(2)}) collective-permute-start(bf16[112,512]{1,0:T(8,128)(2,1)S(1)} %collective-permute-done.14.refs_1_), channel_id=1, source_target_pairs={{0,1},{1,2},{2,3},{3,4},{4,5},{5,6},{6,7},{7,0},{8,9},{9,10},{10,1... | collective-permute-start | bytes 344072 | tf_op jit(solution)/shard_map/ppermute | solution.py:41
  102.9 2.7 %copy-start.3 = (bf16[32,16,1152]{2,1,0:T(8,128)(2,1)}, bf16[32,16,1152]{2,1,0:T(8,128)(2,1)S(1)}, u32[]{:S(2)}) copy-start(bf16[32,16,1152]{2,1,0:T(8,128)(2,1)S(1)} %all-to-all-done.1.arrived_ref) | copy-start | bytes 3538948
  102.9 9.4 %collective-permute-start.18 = (bf16[112,512]{1,0:T(8,128)(2,1)}, bf16[112,512]{1,0:T(8,128)(2,1)}, u32[]{:S(2)}, u32[]{:S(2)}) collective-permute-start(bf16[112,512]{1,0:T(8,128)(2,1)} %collective-permute-done.16.refs_3_), channel_id=1, source_target_pairs={{0,1},{1,2},{2,3},{3,4},{4,5},{5,6},{6,7},{7,0},{8,9},{9,10},{10,1... | collective-permute-start | bytes 344072 | tf_op jit(solution)/shard_map/ppermute | solution.py:41
  103.2 9.1 %collective-permute-start.19 = (bf16[112,512]{1,0:T(8,128)(2,1)}, bf16[112,512]{1,0:T(8,128)(2,1)}, u32[]{:S(2)}, u32[]{:S(2)}) collective-permute-start(bf16[112,512]{1,0:T(8,128)(2,1)} %collective-permute-done.17.refs_4_), channel_id=1, source_target_pairs={{0,7},{1,0},{2,1},{3,2},{4,3},{5,4},{6,5},{7,6},{8,15},{9,8},{10,9... | collective-permute-start | bytes 344072 | tf_op jit(solution)/shard_map/ppermute | solution.py:41
  108.2 15.0 %all-to-all-start.2 = ((bf16[8,16,896]{2,1,0:T(8,128)(2,1)}), bf16[8,16,896]{2,1,0:T(8,128)(2,1)S(1)}, u32[]{:S(2)}, u32[]{:S(2)}) async-start(bf16[8,16,896]{2,1,0:T(8,128)(2,1)} %choose.1), calls=%async_computation.2 | async-start | bytes 458752 | tf_op jit(solution)/shard_map/all_to_all | solution.py:45
  123.2 0.7 copy-start.5
  139.5 7.6 %copy-start.4 = (bf16[16,16,1024]{2,1,0:T(8,128)(2,1)}, bf16[16,16,1024]{2,1,0:T(8,128)(2,1)S(1)}, u32[]{:S(2)}) copy-start(bf16[16,16,1024]{2,1,0:T(8,128)(2,1)S(1)} %all_to_all.20) | copy-start | bytes 1572868
  139.5 7.6 %collective-permute-start.22 = (bf16[256,1024]{1,0:T(8,128)(2,1)S(1)}, bf16[256,1024]{1,0:T(8,128)(2,1)S(1)}, u32[]{:S(2)}, u32[]{:S(2)}) collective-permute-start(bf16[256,1024]{1,0:T(8,128)(2,1)S(1)} %bitcast.88), channel_id=1, source_target_pairs={{0,8},{8,0},{1,9},{9,1},{2,10},{10,2},{3,11},{11,3},{4,12},{12,4},... | collective-permute-start | bytes 1572872 | tf_op jit(solution)/shard_map/ppermute | solution.py:37
  142.3 4.8 %collective-permute-start.20 = (bf16[64,512]{1,0:T(8,128)(2,1)S(1)}, bf16[64,512]{1,0:T(8,128)(2,1)S(1)}, u32[]{:S(2)}, u32[]{:S(2)}) collective-permute-start(bf16[64,512]{1,0:T(8,128)(2,1)S(1)} %slice.98), channel_id=1, source_target_pairs={{0,1},{1,2},{2,3},{3,4},{4,5},{5,6},{6,7},{7,0},{8,9},{9,10},{10,1... | collective-permute-start | bytes 196616 | tf_op jit(solution)/shard_map/ppermute | solution.py:41
  143.1 3.9 %collective-permute-start.21 = (bf16[48,512]{1,0:T(8,128)(2,1)S(1)}, bf16[48,512]{1,0:T(8,128)(2,1)S(1)}, u32[]{:S(2)}, u32[]{:S(2)}) collective-permute-start(bf16[48,512]{1,0:T(8,128)(2,1)S(1)} %slice.99), channel_id=1, source_target_pairs={{0,7},{1,0},{2,1},{3,2},{4,3},{5,4},{6,5},{7,6},{8,15},{9,8},{10,9... | collective-permute-start | bytes 147464 | tf_op jit(solution)/shard_map/ppermute | solution.py:41
  146.9 0.6 copy-start.11
  147.1 0.6 copy-start.10
  147.1 0.8 copy-start.6

commit v3 on v2

--- a/solution.py
+++ b/solution.py
@@ -82,14 +82,14 @@
 
 
 def activate(pos_ref, *refs):
-    own, far = refs[:8], refs[8:10]
-    high_ref, low_ref, wh_ref, out_ref, ht_ref, sum_ref = refs[10:]
+    own, far = refs[:2], refs[2:4]
+    high_ref, low_ref, wh_ref, out_ref, ht_ref, sum_ref = refs[4:]
     c = pos_ref[3]
     xh, y = pos_ref[1], pos_ref[2]
     sum_ref[...] = jnp.zeros_like(sum_ref)
     for i, (m, g) in enumerate(GROUPS):
-        theirs = far[0][i * 128 : (i + 1) * 128, :] if i < 6 else far[1][(i - 6) * 128 : (i - 5) * 128, :]
-        for core, part in ((c, own[i][...]), (1 - c, theirs)):
+        late, at = i // 6, slice(i % 6 * 128, i % 6 * 128 + 128)
+        for core, part in ((c, own[late][at, :]), (1 - c, far[late][at, :])):
             for j in range(2):
                 block = jnp.where(
                     core == 0,
@@ -124,7 +124,7 @@
             jax.ShapeDtypeStruct((32, 16, 640 + wh.shape[1]), BF16),
             jax.ShapeDtypeStruct((n, 512), BF16),
         ),
-        in_specs=[SMEM] + [VMEM] * 13,
+        in_specs=[SMEM] + [VMEM] * 7,
         out_specs=(VMEM, VMEM),
         scratch_shapes=[pltpu.VMEM((512, 256), F32)],
         name="activate",
@@ -190,15 +190,15 @@
 
 
 def slab_kernel(pos_ref, count_ref, *refs):
-    pieces = refs[:9]
-    near, far, total_ref, wh_ref, slab_ref, new_ref, grad_ref, panel_ref = refs[9:]
+    pieces = refs[:8]
+    near, far, total_ref, wh_ref, slab_ref, new_ref, grad_ref, panel_ref = refs[8:]
     z = pos_ref[4]
     n = pieces[0].shape[0]
 
     @pl.when(pl.program_id(0) == 0)
     def _():
-        for piece, d, r0 in zip(pieces, (0, -1, 1, -2, 2, -3, 3, -4, 4), (0,) * 8 + (64,)):
-            at = pl.multiple_of(((z + d + 8) % 8) * n + r0, 16)
+        for piece, d in zip(pieces, (0, -1, 1, -2, 2, -3, 3, 4)):
+            at = pl.multiple_of(((z + d + 8) % 8) * n, 16)
             panel_ref[pl.ds(at, piece.shape[0]), :] = piece[...]
 
     scale = 1.0 / jnp.full((1, 1), count_ref[0].astype(F32), F32)
@@ -281,12 +281,13 @@
 
     b1 = plane_permute(b0, 0, 1)
     b3 = plane_permute(b0, 0, 3)
-    b2 = plane_permute(b0, 0, 2)
+    b2a = plane_permute(b1[:32], 0, 3)
+    b2b = plane_permute(b3[32:], 0, 1)
     weights = weights_call(pos, gate_t, up_t, far_w.reshape(2, 2, n, quarter))
     sb = jnp.concatenate([b1, b3], 0)
     s3b = plane_permute(sb, 1, 3)
     s1b = plane_permute(sb, 1, 1)
-    sa = jnp.concatenate([b0, b2], 0)
+    sa = jnp.concatenate([b0, b2a, b2b], 0)
     s1a = plane_permute(sa, 1, 1)
     s3a = plane_permute(sa, 1, 3)
     s2b = plane_permute(s3b, 1, 1)
@@ -298,7 +299,7 @@
         mine, theirs = products(buffer, weights, f)
         own.append(mine)
         far.append(theirs)
-    far = [jnp.concatenate(part, 0) for part in (far[:6], far[6:])]
+    own, far = ([jnp.concatenate(part, 0) for part in (all_of[:6], all_of[6:])] for all_of in (own, far))
     far = [core_swap(part) for part in far]
     sent, hidden_t = activate_call(pos, own, far, (high, low), wh, n)
 
@@ -313,14 +314,15 @@
     pieces = exchange(wanted, "gc")
     sums = jnp.sum(arrived[:, :, 640:].reshape(16, 2, 16, half).astype(F32), axis=0)
     wh = jnp.concatenate([sums[0], sums[1]], 1)
-    pieces, f3, g3, wh = lax.optimization_barrier((pieces, f3, g3, wh))
+    pieces, wh = lax.optimization_barrier((pieces, wh))
     f4, g4 = shift_z(f3[:64], 1), shift_z(g3[64:], -1)
+    h4 = jnp.concatenate([f4, g4], 0)
     start = slab_offset[0] + z * width
     shift = start - jnp.minimum(start // panel_width, 29) * panel_width
     chunk, total = assemble_call(pieces, jnp.stack([shift, c]).astype(jnp.int32), width, n)
     near = exchange(chunk, PLANE).reshape(256, width)
     return slab_call(
-        pos, token_count, (hidden_t, f1, g1, f2, g2, f3, g3, f4, g4), near, core_swap(near), total, wh, hessian_slab
+        pos, token_count, (hidden_t, f1, g1, f2, g2, f3, g3, h4), near, core_swap(near), total, wh, hessian_slab
     )
 
 

time: 154 us -> 161 us (1.045)
  waiting for transfers between devices: 34.1 us -> 42.7 us
  matrix products: 22.1 us -> 16.9 us
    ppermute x9 -> x10, waiting for transfers between devices: 3.56 us -> 9.33 us  [plane_permute(): return lax.ppermute(array, CAL_GR, pairs)]
    dot_general x16, matrix products: 15.8 us -> 10.6 us  [products(): lax.dot_general(tokens, half, NT, preferred_element_type=F32)]
    ppermute x8, waiting for transfers between devices: 7.16 us -> 10.2 us  [shift_z(): return lax.ppermute(array, 'gc', [(i, (i + d) % 8) for i in range(8)])]
    ppermute x9 -> x10, starting transfers between devices: 10.6 us -> 12.2 us  [plane_permute(): return lax.ppermute(array, CAL_GR, pairs)]
    slice x2, local copies, waits for them, and re-layouts: 1.65 us -> 0.01 us  [on_device(): f4, g4 = (shift_z(f3[:64], 1), shift_z(g3[64:], -1))]
    unnamed x26 -> x31, local copies, waits for them, and re-layouts: 3.95 us -> 5.25 us
  transfers between devices with their start and end apart: 26 -> 27, of which waited for: 10 -> 13; matrix products, arithmetic and copies ran while one was open for 22% -> 18% of each run, Pallas kernels for 4% -> 3%
where the time goes in v3:
time: 161 us; the launch traced here: 160 us
  starting transfers between devices  45.3 us (28%)
  waiting for transfers between devices  42.7 us (27%)
  Pallas kernels  17.6 us (11%)
  matrix products  16.9 us (10%)
  blocking collectives  13.7 us (9%)
  local copies, waits for them, and re-layouts  12.5 us (8%)
  other arithmetic  8.6 us (5%)
  between operations  2.56 us (2%)
    all_to_all x3, waiting for transfers between devices, exchange(): return lax.all_to_all(array, axes, split_axis=0, concat_axis=0, tiled=True)  22.3 us
    all_to_all x3, starting transfers between devices, exchange(): return lax.all_to_all(array, axes, split_axis=0, concat_axis=0, tiled=True)  15.1 us
    all_to_all x1, blocking collectives, exchange(): return lax.all_to_all(array, axes, split_axis=0, concat_axis=0, tiled=True)  13.7 us
    ppermute x10, starting transfers between devices, plane_permute(): return lax.ppermute(array, CAL_GR, pairs)  12.2 us
    dot_general x16, matrix products, products(): lax.dot_general(tokens, half, NT, preferred_element_type=F32)  10.6 us
    ppermute x8, waiting for transfers between devices, shift_z(): return lax.ppermute(array, 'gc', [(i, (i + d) % 8) for i in range(8)])  10.2 us
    ppermute x6, starting transfers between devices, core_swap(): return lax.ppermute(array, 'gr_2', [(0, 1), (1, 0)])  9.46 us
    ppermute x10, waiting for transfers between devices, plane_permute(): return lax.ppermute(array, CAL_GR, pairs)  9.33 us
  transfers between devices with their start and end apart: 27, of which 13 were waited for; matrix products, arithmetic and copies ran while one was open for 18% of the time, Pallas kernels for 3%

profile of v3, /device:TPU:1, one launch (start us, length us, event | category | flops | bytes accessed | tf_op | source)
XLA Modules:
  0.0 159.8 jit_solution(3423602605090739958)
XLA Ops:
  0.7 0.9 constant_dynamic-slice_fusion.1
  1.5 3.2 %collective-permute-start = (bf16[4,2048]{1,0:T(4,128)(2,1)S(1)}, bf16[4,2048]{1,0:T(4,128)(2,1)S(1)}, u32[]{:S(2)}, u32[]{:S(2)}) collective-permute-start(bf16[4,2048]{1,0:T(4,128)(2,1)S(1)} %constant_dynamic-slice_fusion.1), channel_id=1, source_target_pairs={{0,8},{8,0},{1,9},{9,1},{2,10},{10,2},{3,11},{11,3},{4,12},{12,4},... | collective-permute-start | bytes 49160 | tf_op jit(solution)/shard_map/ppermute | solution.py:37
  4.7 0.8 collective-permute-done
  5.6 0.7 broadcast_select_fusion.1
  6.3 0.7 broadcast_in_dim.2
  7.1 1.6 dynamic-slice_bitcast_fusion.14
  8.6 1.5 pad_maximum_fusion
  10.4 6.5 %all-to-all-start = ((bf16[8,8,2048]{2,1,0:T(8,128)(2,1)}), bf16[8,8,2048]{2,1,0:T(8,128)(2,1)S(1)}, u32[]{:S(2)}, u32[]{:S(2)}) async-start(bf16[8,8,2048]{2,1,0:T(8,128)(2,1)} %broadcast_in_dim.2), calls=%async_computation | async-start | bytes 524288 | tf_op jit(solution)/shard_map/all_to_all | solution.py:45
  17.1 4.4 %fusion = f32[512,512]{1,0:T(8,128)} fusion(f32[512,896]{1,0:T(8,128)S(1)} %copy-done, f32[896,1024]{1,0:T(8,128)} %refs_12_.1, s32[]{:T(128)S(6)} %select_n.60), kind=kOutput, calls=%fused_computation.1 | convolution fusion | flops 1409286144 | bytes 4718596 | tf_op jit(solution)/shard_map/dot_general | solution.py:270
  21.5 0.7 subtract_convert_fusion.refs_5_
  22.2 0.7 pad_convert_fusion.refs_4_
  22.9 1.9 %fusion.2 = f32[512,512]{1,0:T(8,128)S(1)} fusion(f32[512,896]{1,0:T(8,128)S(1)} %copy-done, f32[896,1024]{1,0:T(8,128)S(1)} %copy-done.2, s32[]{:T(128)S(6)} %select_n.59), kind=kOutput, calls=%fused_computation.3 | convolution fusion | flops 1409286144 | bytes 4718596 | tf_op jit(solution)/shard_map/dot_general | solution.py:270
  24.8 4.3 %all-to-all-done = bf16[8,8,2048]{2,1,0:T(8,128)(2,1)S(1)} async-done(((bf16[8,8,2048]{2,1,0:T(8,128)(2,1)}), bf16[8,8,2048]{2,1,0:T(8,128)(2,1)S(1)}, u32[]{:S(2)}, u32[]{:S(2)}) %all-to-all-start) | async-done | bytes 262176 | tf_op jit(solution)/shard_map/all_to_all | solution.py:45
  29.1 1.3 collective-permute-start.2
  30.4 0.6 stack.45.pos_ref
  31.1 1.9 %collective-permute-start.4 = (bf16[64,2048]{1,0:T(8,128)(2,1)S(1)}, bf16[64,2048]{1,0:T(8,128)(2,1)}, u32[]{:S(2)}, u32[]{:S(2)}) collective-permute-start(bf16[64,2048]{1,0:T(8,128)(2,1)S(1)} %bitcast.92), channel_id=1, source_target_pairs={{0,192},{8,56},{16,208},{24,40},{32,224},{40,24},{48,240},{56,8},{... | collective-permute-start | bytes 786440 | tf_op jit(solution)/shard_map/ppermute | solution.py:33
  33.0 0.7 constant_dynamic-update-slice_fusion.2
  33.7 1.0 collective-permute-start.14
  34.7 4.2 %weights.1 = bf16[2,512,2048]{2,1,0:T(8,128)(2,1)} custom-call(s32[5]{0:T(128)} %stack.45.pos_ref, bf16[112,8192]{1,0:T(8,128)(2,1)} %bitcast.86, bf16[112,8192]{1,0:T(8,128)(2,1)} %bitcast.87, bf16[2,2,112,2048]{3,2,1,0:T(8,128)(2,1)} %bitcast.16.far), custom_call_target="tpu_custom_call" | custom-call | tf_op jit(solution)/shard_map/weights/pallas_call | solution.py:66
  39.0 2.8 %collective-permute-start.3 = (bf16[32,2048]{1,0:T(8,128)(2,1)S(1)}, bf16[32,2048]{1,0:T(8,128)(2,1)S(1)}, u32[]{:S(2)}, u32[]{:S(2)}) collective-permute-start(bf16[32,2048]{1,0:T(8,128)(2,1)S(1)} %slice.108), channel_id=1, source_target_pairs={{0,192},{8,56},{16,208},{24,40},{32,224},{40,24},{48,240},{56,8},{... | collective-permute-start | bytes 393224 | tf_op jit(solution)/shard_map/ppermute | solution.py:33
  41.8 1.0 constant_dynamic-update-slice_fusion.3
  42.8 0.9 collective-permute-start.9
  43.7 0.9 slice.109
  44.8 0.7 constant_dynamic-update-slice_fusion.1
  45.4 4.8 %collective-permute-done.5 = bf16[32,2048]{1,0:T(8,128)(2,1)S(1)} collective-permute-done((bf16[32,2048]{1,0:T(8,128)(2,1)S(1)}, bf16[32,2048]{1,0:T(8,128)(2,1)S(1)}, u32[]{:S(2)}, u32[]{:S(2)}) %collective-permute-start.5) | collective-permute-done | bytes 131104 | tf_op jit(solution)/shard_map/ppermute | solution.py:33
  50.2 0.7 constant_dynamic-update-slice_fusion
  50.9 1.8 %collective-permute-start.8 = (bf16[128,2048]{1,0:T(8,128)(2,1)}, bf16[128,2048]{1,0:T(8,128)(2,1)S(1)}, u32[]{:S(2)}, u32[]{:S(2)}) collective-permute-start(bf16[128,2048]{1,0:T(8,128)(2,1)} %constant_dynamic-update-slice_fusion), channel_id=1, source_target_pairs={{0,48},{8,200},{16,32},{24,216},{32,16},{40,232},{48,0},{56,248},{... | collective-permute-start | bytes 1572872 | tf_op jit(solution)/shard_map/ppermute | solution.py:33
  52.7 0.9 collective-permute-start.6
  53.6 1.9 %convolution_dynamic-update-slice_fusion.5 = f32[768,256]{1,0:T(8,128)S(1)} fusion(bf16[128,2048]{1,0:T(8,128)(2,1)} %constant_dynamic-update-slice_fusion, bf16[2,512,2048]{2,1,0:T(8,128)(2,1)} %weights.1), kind=kOutput, calls=%fused_computation.10 | convolution fusion | flops 134217728 | bytes 1703936 | tf_op jit(solution)/shard_map/dot_general | solution.py:81
  55.5 1.9 %convolution_dynamic-update-slice_fusion.11 = f32[768,256]{1,0:T(8,128)S(1)} fusion(bf16[128,2048]{1,0:T(8,128)(2,1)} %constant_dynamic-update-slice_fusion, bf16[2,512,2048]{2,1,0:T(8,128)(2,1)} %weights.1), kind=kOutput, calls=%fused_computation.16 | convolution fusion | flops 134217728 | bytes 1703936 | tf_op jit(solution)/shard_map/dot_general | solution.py:81
  58.4 0.9 collective-permute-start.11
  59.2 2.0 %collective-permute-done.6 = bf16[128,2048]{1,0:T(8,128)(2,1)S(1)} collective-permute-done((bf16[128,2048]{1,0:T(8,128)(2,1)}, bf16[128,2048]{1,0:T(8,128)(2,1)S(1)}, u32[]{:S(2)}, u32[]{:S(2)}) %collective-permute-start.6) | collective-permute-done | bytes 524320 | tf_op jit(solution)/shard_map/ppermute | solution.py:33
  63.3 2.0 %collective-permute-start.12 = (f32[768,256]{1,0:T(8,128)S(1)}, f32[768,256]{1,0:T(8,128)}, u32[]{:S(2)}, u32[]{:S(2)}) collective-permute-start(f32[768,256]{1,0:T(8,128)S(1)} %convolution_dynamic-update-slice_fusion), channel_id=1, source_target_pairs={{0,8},{8,0},{1,9},{9,1},{2,10},{10,2},{3,11},{11,3},{4,12},{12,4},... | collective-permute-start | bytes 2359304 | tf_op jit(solution)/shard_map/ppermute | solution.py:37
  65.2 1.6 collective-permute-start.10
  68.8 2.5 %add_convert_fusion.refs_6_ = bf16[512,512]{1,0:T(8,128)(2,1)} fusion(f32[512,512]{1,0:T(8,128)S(1)} %fusion.2, f32[512,512]{1,0:T(8,128)} %collective-permute-done.14), kind=kLoop, calls=%fused_computation.26 | loop fusion | flops 524288 | bytes 2621440 | tf_op jit(solution)/shard_map/convert_element_type | solution.py:296
  72.3 2.5 %collective-permute-done.10 = bf16[128,2048]{1,0:T(8,128)(2,1)S(1)} collective-permute-done((bf16[128,2048]{1,0:T(8,128)(2,1)S(1)}, bf16[128,2048]{1,0:T(8,128)(2,1)S(1)}, u32[]{:S(2)}, u32[]{:S(2)}) %collective-permute-start.10) | collective-permute-done | bytes 524320 | tf_op jit(solution)/shard_map/ppermute | solution.py:33
  75.3 1.0 collective-permute-start.13
  76.8 0.7 pad_maximum_fusion.1.refs_1_
  77.6 0.7 copy-done.9
  78.3 3.6 %activate.1 = (bf16[32,16,1152]{2,1,0:T(8,128)(2,1)}, bf16[112,512]{1,0:T(8,128)(2,1)}) custom-call(s32[5]{0:T(128)} %stack.45.pos_ref, f32[768,256]{1,0:T(8,128)} %copy-done.6, f32[256,256]{1,0:T(8,128)} %pad_maximum_fusion.1.refs_1_, f32[768,256]{1,0:T(8,128)} %collective-permute-done.12.refs_2_, f32[256,256]{1,0:T(8,128)} %copy-done.9, ...), custom_call_target="tpu_custom_call" | custom-call | tf_op jit(solution)/shard_map/activate/pallas_call | solution.py:121
  81.8 5.2 %all-to-all-start.1 = ((bf16[32,16,1152]{2,1,0:T(8,128)(2,1)}), bf16[32,16,1152]{2,1,0:T(8,128)(2,1)S(1)}, u32[]{:S(2)}, u32[]{:S(2)}) async-start(bf16[32,16,1152]{2,1,0:T(8,128)(2,1)} %get-tuple-element.32), calls=%async_computation.1 | async-start | bytes 2359296 | tf_op jit(solution)/shard_map/all_to_all | solution.py:45
  87.2 1.5 collective-permute-start.15
  89.3 2.5 %collective-permute-done.16.refs_2_ = bf16[112,512]{1,0:T(8,128)(2,1)S(1)} collective-permute-done((bf16[112,512]{1,0:T(8,128)(2,1)}, bf16[112,512]{1,0:T(8,128)(2,1)S(1)}, u32[]{:S(2)}, u32[]{:S(2)}) %collective-permute-start.16) | collective-permute-done | bytes 114720 | tf_op jit(solution)/shard_map/ppermute | solution.py:41
  91.8 1.5 collective-permute-start.18
  93.3 0.7 pad_add_fusion.refs_0_
  94.5 1.3 collective-permute-done.18.refs_4_
  95.8 0.6 copy-done.13
  96.4 2.1 %collective-permute-done.17.refs_3_ = bf16[112,512]{1,0:T(8,128)(2,1)} collective-permute-done((bf16[112,512]{1,0:T(8,128)(2,1)S(1)}, bf16[112,512]{1,0:T(8,128)(2,1)}, u32[]{:S(2)}, u32[]{:S(2)}) %collective-permute-start.17) | collective-permute-done | bytes 114720 | tf_op jit(solution)/shard_map/ppermute | solution.py:41
  98.5 7.3 %all-to-all-done.1.arrived_ref = bf16[32,16,1152]{2,1,0:T(8,128)(2,1)S(1)} async-done(((bf16[32,16,1152]{2,1,0:T(8,128)(2,1)}), bf16[32,16,1152]{2,1,0:T(8,128)(2,1)S(1)}, u32[]{:S(2)}, u32[]{:S(2)}) %all-to-all-start.1) | async-done | bytes 1179680 | tf_op jit(solution)/shard_map/all_to_all | solution.py:45
  105.8 0.9 copy-done.3
  106.8 2.5 %choose.1 = bf16[8,16,896]{2,1,0:T(8,128)(2,1)} custom-call(s32[8]{0:T(128)} %fusion.18.first_ref, bf16[32,16,1152]{2,1,0:T(8,128)(2,1)} %copy-done.3), custom_call_target="tpu_custom_call" | custom-call | tf_op jit(solution)/shard_map/choose/pallas_call | solution.py:143
  109.3 3.4 %all-to-all-start.2 = ((bf16[8,16,896]{2,1,0:T(8,128)(2,1)}), bf16[8,16,896]{2,1,0:T(8,128)(2,1)S(1)}, u32[]{:S(2)}, u32[]{:S(2)}) async-start(bf16[8,16,896]{2,1,0:T(8,128)(2,1)} %choose.1), calls=%async_computation.2 | async-start | bytes 458752 | tf_op jit(solution)/shard_map/all_to_all | solution.py:45
  112.8 0.6 pad_maximum_fusion.4.refs_11_
  113.4 10.6 %all-to-all-done.2.refs_1_ = bf16[8,16,896]{2,1,0:T(8,128)(2,1)S(1)} async-done(((bf16[8,16,896]{2,1,0:T(8,128)(2,1)}), bf16[8,16,896]{2,1,0:T(8,128)(2,1)S(1)}, u32[]{:S(2)}, u32[]{:S(2)}) %all-to-all-start.2) | async-done | bytes 229408 | tf_op jit(solution)/shard_map/all_to_all | solution.py:45
  124.1 0.7 copy-done.5
  124.8 2.0 %assemble.1 = (bf16[16,16,1024]{2,1,0:T(8,128)(2,1)}, bf16[32,512]{1,0:T(8,128)(2,1)}) custom-call(s32[2]{0:T(128)} %pad_add_fusion.refs_0_, bf16[8,16,896]{2,1,0:T(8,128)(2,1)} %copy-done.5), custom_call_target="tpu_custom_call" | custom-call | tf_op jit(solution)/shard_map/assemble/pallas_call | solution.py:179
  126.7 13.7 %all_to_all.20 = bf16[16,16,1024]{2,1,0:T(8,128)(2,1)S(1)} all-to-all(bf16[16,16,1024]{2,1,0:T(8,128)(2,1)} %get-tuple-element.37), channel_id=1, replica_groups=mesh['cal'=2,'gr_0'=2,'gr_1'=4,'gr_2'=2,'gc'=8] {'cal','gr_0','gr_1'}, dimensions={0} | all-to-all | bytes 1048576 | tf_op jit(solution)/shard_map/all_to_all | solution.py:45
  140.4 1.9 %collective-permute-start.23 = (bf16[256,1024]{1,0:T(8,128)(2,1)S(1)}, bf16[256,1024]{1,0:T(8,128)(2,1)S(1)}, u32[]{:S(2)}, u32[]{:S(2)}) collective-permute-start(bf16[256,1024]{1,0:T(8,128)(2,1)S(1)} %bitcast.88), channel_id=1, source_target_pairs={{0,8},{8,0},{1,9},{9,1},{2,10},{10,2},{3,11},{11,3},{4,12},{12,4},... | collective-permute-start | bytes 1572872 | tf_op jit(solution)/shard_map/ppermute | solution.py:37
  142.4 2.6 %collective-permute-start.20 = (bf16[112,512]{1,0:T(8,128)(2,1)}, bf16[112,512]{1,0:T(8,128)(2,1)S(1)}, u32[]{:S(2)}, u32[]{:S(2)}) collective-permute-start(bf16[112,512]{1,0:T(8,128)(2,1)} %copy-done.13), channel_id=1, source_target_pairs={{0,7},{1,0},{2,1},{3,2},{4,3},{5,4},{6,5},{7,6},{8,15},{9,8},{10,9... | collective-permute-start | bytes 344072 | tf_op jit(solution)/shard_map/ppermute | solution.py:41
  145.0 3.4 %collective-permute-done.19.refs_5_ = bf16[112,512]{1,0:T(8,128)(2,1)S(1)} collective-permute-done((bf16[112,512]{1,0:T(8,128)(2,1)}, bf16[112,512]{1,0:T(8,128)(2,1)S(1)}, u32[]{:S(2)}, u32[]{:S(2)}) %collective-permute-start.19) | collective-permute-done | bytes 114720 | tf_op jit(solution)/shard_map/ppermute | solution.py:41
  148.6 2.7 %collective-permute-start.22 = (bf16[48,512]{1,0:T(8,128)(2,1)S(1)}, bf16[48,512]{1,0:T(8,128)(2,1)S(1)}, u32[]{:S(2)}, u32[]{:S(2)}) collective-permute-start(bf16[48,512]{1,0:T(8,128)(2,1)S(1)} %slice.115), channel_id=1, source_target_pairs={{0,7},{1,0},{2,1},{3,2},{4,3},{5,4},{6,5},{7,6},{8,15},{9,8},{10,9... | collective-permute-start | bytes 147464 | tf_op jit(solution)/shard_map/ppermute | solution.py:41
  152.8 0.7 pad_maximum_fusion.3.refs_7_
  153.5 0.8 copy-done.7
  154.3 5.3 %slab.1 = (f32[896,1024]{1,0:T(8,128)}, f32[16,1024]{1,0:T(8,128)}) custom-call(s32[5]{0:T(128)} %stack.45.pos_ref, s32[1]{0:T(128)S(6)} %copy.23.count_ref, bf16[112,512]{1,0:T(8,128)(2,1)} %get-tuple-element.31.refs_0_, bf16[112,512]{1,0:T(8,128)(2,1)} %copy-done.12, bf16[112,512]{1,0:T(8,128)(2,1)} %copy-done.11, ...), custom_call_target="tpu_custom_call" | custom-call | tf_op jit(solution)/shard_map/slab/pallas_call | solution.py:223
  (71 shorter events, 9.4 us)
Async XLA Ops:
  0.6 16.3 %copy-start = (f32[512,896]{1,0:T(8,128)S(1)}, f32[512,896]{1,0:T(8,128)}, u32[]{:S(2)}) copy-start(f32[512,896]{1,0:T(8,128)} %param.11) | copy-start | bytes 5505028
  1.5 4.0 %collective-permute-start = (bf16[4,2048]{1,0:T(4,128)(2,1)S(1)}, bf16[4,2048]{1,0:T(4,128)(2,1)S(1)}, u32[]{:S(2)}, u32[]{:S(2)}) collective-permute-start(bf16[4,2048]{1,0:T(4,128)(2,1)S(1)} %constant_dynamic-slice_fusion.1), channel_id=1, source_target_pairs={{0,8},{8,0},{1,9},{9,1},{2,10},{10,2},{3,11},{11,3},{4,12},{12,4},... | collective-permute-start | bytes 49160 | tf_op jit(solution)/shard_map/ppermute | solution.py:37
  10.1 19.1 %collective-permute-start.1 = (bf16[4,112,2048]{2,1,0:T(8,128)(2,1)}, bf16[4,112,2048]{2,1,0:T(8,128)(2,1)}, u32[]{:S(2)}, u32[]{:S(2)}) collective-permute-start(bf16[4,112,2048]{2,1,0:T(8,128)(2,1)} %pad_maximum_fusion), channel_id=1, source_target_pairs={{0,8},{8,0},{1,9},{9,1},{2,10},{10,2},{3,11},{11,3},{4,12},{12,4},... | collective-permute-start | bytes 5505032 | tf_op jit(solution)/shard_map/ppermute | solution.py:37
  10.4 18.7 %all-to-all-start = ((bf16[8,8,2048]{2,1,0:T(8,128)(2,1)}), bf16[8,8,2048]{2,1,0:T(8,128)(2,1)S(1)}, u32[]{:S(2)}, u32[]{:S(2)}) async-start(bf16[8,8,2048]{2,1,0:T(8,128)(2,1)} %broadcast_in_dim.2), calls=%async_computation | async-start | bytes 524288 | tf_op jit(solution)/shard_map/all_to_all | solution.py:45
  16.9 6.0 %copy-start.2 = (f32[896,1024]{1,0:T(8,128)S(1)}, f32[896,1024]{1,0:T(8,128)}, u32[]{:S(2)}) copy-start(f32[896,1024]{1,0:T(8,128)} %refs_12_.1) | copy-start | bytes 11010052
  29.1 9.8 %collective-permute-start.2 = (bf16[64,2048]{1,0:T(8,128)(2,1)S(1)}, bf16[64,2048]{1,0:T(8,128)(2,1)S(1)}, u32[]{:S(2)}, u32[]{:S(2)}) collective-permute-start(bf16[64,2048]{1,0:T(8,128)(2,1)S(1)} %bitcast.91), channel_id=1, source_target_pairs={{0,128},{8,24},{16,144},{24,8},{32,160},{40,56},{48,176},{56,40},{... | collective-permute-start | bytes 786440 | tf_op jit(solution)/shard_map/ppermute | solution.py:33
  31.1 10.7 %collective-permute-start.4 = (bf16[64,2048]{1,0:T(8,128)(2,1)S(1)}, bf16[64,2048]{1,0:T(8,128)(2,1)}, u32[]{:S(2)}, u32[]{:S(2)}) collective-permute-start(bf16[64,2048]{1,0:T(8,128)(2,1)S(1)} %bitcast.92), channel_id=1, source_target_pairs={{0,192},{8,56},{16,208},{24,40},{32,224},{40,24},{48,240},{56,8},{... | collective-permute-start | bytes 786440 | tf_op jit(solution)/shard_map/ppermute | solution.py:33
  33.7 35.1 %collective-permute-start.14 = (f32[512,512]{1,0:T(8,128)}, f32[512,512]{1,0:T(8,128)}, u32[]{:S(2)}, u32[]{:S(2)}) collective-permute-start(f32[512,512]{1,0:T(8,128)} %fusion), channel_id=1, source_target_pairs={{0,8},{8,0},{1,9},{9,1},{2,10},{10,2},{3,11},{11,3},{4,12},{12,4},... | collective-permute-start | bytes 3145736 | tf_op jit(solution)/shard_map/ppermute | solution.py:37
  38.9 18.4 %copy-start.1 = (bf16[2,512,2048]{2,1,0:T(8,128)(2,1)S(1)}, bf16[2,512,2048]{2,1,0:T(8,128)(2,1)}, u32[]{:S(2)}) copy-start(bf16[2,512,2048]{2,1,0:T(8,128)(2,1)} %weights.1) | copy-start | bytes 12582916
  39.0 5.8 %collective-permute-start.3 = (bf16[32,2048]{1,0:T(8,128)(2,1)S(1)}, bf16[32,2048]{1,0:T(8,128)(2,1)S(1)}, u32[]{:S(2)}, u32[]{:S(2)}) collective-permute-start(bf16[32,2048]{1,0:T(8,128)(2,1)S(1)} %slice.108), channel_id=1, source_target_pairs={{0,192},{8,56},{16,208},{24,40},{32,224},{40,24},{48,240},{56,8},{... | collective-permute-start | bytes 393224 | tf_op jit(solution)/shard_map/ppermute | solution.py:33
  42.8 15.6 %collective-permute-start.9 = (bf16[128,2048]{1,0:T(8,128)(2,1)S(1)}, bf16[128,2048]{1,0:T(8,128)(2,1)S(1)}, u32[]{:S(2)}, u32[]{:S(2)}) collective-permute-start(bf16[128,2048]{1,0:T(8,128)(2,1)S(1)} %constant_dynamic-update-slice_fusion.3), channel_id=1, source_target_pairs={{0,48},{8,200},{16,32},{24,216},{32,16},{40,232},{48,0},{56,248},{... | collective-permute-start | bytes 1572872 | tf_op jit(solution)/shard_map/ppermute | solution.py:33
  43.7 18.0 %collective-permute-start.7 = (bf16[128,2048]{1,0:T(8,128)(2,1)S(1)}, bf16[128,2048]{1,0:T(8,128)(2,1)S(1)}, u32[]{:S(2)}, u32[]{:S(2)}) collective-permute-start(bf16[128,2048]{1,0:T(8,128)(2,1)S(1)} %constant_dynamic-update-slice_fusion.3), channel_id=1, source_target_pairs={{0,16},{8,136},{16,0},{24,152},{32,48},{40,168},{48,32},{56,184},{... | collective-permute-start | bytes 1572872 | tf_op jit(solution)/shard_map/ppermute | solution.py:33
  44.6 5.6 %collective-permute-start.5 = (bf16[32,2048]{1,0:T(8,128)(2,1)S(1)}, bf16[32,2048]{1,0:T(8,128)(2,1)S(1)}, u32[]{:S(2)}, u32[]{:S(2)}) collective-permute-start(bf16[32,2048]{1,0:T(8,128)(2,1)S(1)} %slice.109), channel_id=1, source_target_pairs={{0,128},{8,24},{16,144},{24,8},{32,160},{40,56},{48,176},{56,40},{... | collective-permute-start | bytes 393224 | tf_op jit(solution)/shard_map/ppermute | solution.py:33
  50.9 11.4 %collective-permute-start.8 = (bf16[128,2048]{1,0:T(8,128)(2,1)}, bf16[128,2048]{1,0:T(8,128)(2,1)S(1)}, u32[]{:S(2)}, u32[]{:S(2)}) collective-permute-start(bf16[128,2048]{1,0:T(8,128)(2,1)} %constant_dynamic-update-slice_fusion), channel_id=1, source_target_pairs={{0,48},{8,200},{16,32},{24,216},{32,16},{40,232},{48,0},{56,248},{... | collective-permute-start | bytes 1572872 | tf_op jit(solution)/shard_map/ppermute | solution.py:33
  52.7 8.5 %collective-permute-start.6 = (bf16[128,2048]{1,0:T(8,128)(2,1)}, bf16[128,2048]{1,0:T(8,128)(2,1)S(1)}, u32[]{:S(2)}, u32[]{:S(2)}) collective-permute-start(bf16[128,2048]{1,0:T(8,128)(2,1)} %constant_dynamic-update-slice_fusion), channel_id=1, source_target_pairs={{0,16},{8,136},{16,0},{24,152},{32,48},{40,168},{48,32},{56,184},{... | collective-permute-start | bytes 1572872 | tf_op jit(solution)/shard_map/ppermute | solution.py:33
  58.4 12.9 %collective-permute-start.11 = (bf16[128,2048]{1,0:T(8,128)(2,1)S(1)}, bf16[128,2048]{1,0:T(8,128)(2,1)S(1)}, u32[]{:S(2)}, u32[]{:S(2)}) collective-permute-start(bf16[128,2048]{1,0:T(8,128)(2,1)S(1)} %collective-permute-done.9), channel_id=1, source_target_pairs={{0,16},{8,136},{16,0},{24,152},{32,48},{40,168},{48,32},{56,184},{... | collective-permute-start | bytes 1572872 | tf_op jit(solution)/shard_map/ppermute | solution.py:33
  63.3 14.3 %collective-permute-start.12 = (f32[768,256]{1,0:T(8,128)S(1)}, f32[768,256]{1,0:T(8,128)}, u32[]{:S(2)}, u32[]{:S(2)}) collective-permute-start(f32[768,256]{1,0:T(8,128)S(1)} %convolution_dynamic-update-slice_fusion), channel_id=1, source_target_pairs={{0,8},{8,0},{1,9},{9,1},{2,10},{10,2},{3,11},{11,3},{4,12},{12,4},... | collective-permute-start | bytes 2359304 | tf_op jit(solution)/shard_map/ppermute | solution.py:37
  65.2 9.5 %collective-permute-start.10 = (bf16[128,2048]{1,0:T(8,128)(2,1)S(1)}, bf16[128,2048]{1,0:T(8,128)(2,1)S(1)}, u32[]{:S(2)}, u32[]{:S(2)}) collective-permute-start(bf16[128,2048]{1,0:T(8,128)(2,1)S(1)} %collective-permute-done.6), channel_id=1, source_target_pairs={{0,48},{8,200},{16,32},{24,216},{32,16},{40,232},{48,0},{56,248},{... | collective-permute-start | bytes 1572872 | tf_op jit(solution)/shard_map/ppermute | solution.py:33
  68.8 8.0 %copy-start.6 = (f32[768,256]{1,0:T(8,128)}, f32[768,256]{1,0:T(8,128)S(1)}, u32[]{:S(2)}) copy-start(f32[768,256]{1,0:T(8,128)S(1)} %convolution_dynamic-update-slice_fusion.6.refs_0_) | copy-start | bytes 2359300
  75.3 2.3 %collective-permute-start.13 = (f32[256,256]{1,0:T(8,128)S(1)}, f32[256,256]{1,0:T(8,128)S(1)}, u32[]{:S(2)}, u32[]{:S(2)}) collective-permute-start(f32[256,256]{1,0:T(8,128)S(1)} %pad_maximum_fusion.2), channel_id=1, source_target_pairs={{0,8},{8,0},{1,9},{9,1},{2,10},{10,2},{3,11},{11,3},{4,12},{12,4},... | collective-permute-start | bytes 786440 | tf_op jit(solution)/shard_map/ppermute | solution.py:37
  77.6 0.7 copy-start.9
  81.8 23.9 %all-to-all-start.1 = ((bf16[32,16,1152]{2,1,0:T(8,128)(2,1)}), bf16[32,16,1152]{2,1,0:T(8,128)(2,1)S(1)}, u32[]{:S(2)}, u32[]{:S(2)}) async-start(bf16[32,16,1152]{2,1,0:T(8,128)(2,1)} %get-tuple-element.32), calls=%async_computation.1 | async-start | bytes 2359296 | tf_op jit(solution)/shard_map/all_to_all | solution.py:45
  87.1 4.8 %collective-permute-start.16 = (bf16[112,512]{1,0:T(8,128)(2,1)}, bf16[112,512]{1,0:T(8,128)(2,1)S(1)}, u32[]{:S(2)}, u32[]{:S(2)}) collective-permute-start(bf16[112,512]{1,0:T(8,128)(2,1)} %get-tuple-element.31.refs_0_), channel_id=1, source_target_pairs={{0,7},{1,0},{2,1},{3,2},{4,3},{5,4},{6,5},{7,6},{8,15},{9,8},{10,9... | collective-permute-start | bytes 344072 | tf_op jit(solution)/shard_map/ppermute | solution.py:41
  87.2 6.2 %collective-permute-start.15 = (bf16[112,512]{1,0:T(8,128)(2,1)}, bf16[112,512]{1,0:T(8,128)(2,1)S(1)}, u32[]{:S(2)}, u32[]{:S(2)}) collective-permute-start(bf16[112,512]{1,0:T(8,128)(2,1)} %get-tuple-element.31.refs_0_), channel_id=1, source_target_pairs={{0,1},{1,2},{2,3},{3,4},{4,5},{5,6},{6,7},{7,0},{8,9},{9,10},{10,1... | collective-permute-start | bytes 344072 | tf_op jit(solution)/shard_map/ppermute | solution.py:41
  91.8 6.7 %copy-start.11 = (bf16[112,512]{1,0:T(8,128)(2,1)}, bf16[112,512]{1,0:T(8,128)(2,1)S(1)}, u32[]{:S(2)}) copy-start(bf16[112,512]{1,0:T(8,128)(2,1)S(1)} %collective-permute-done.16.refs_2_) | copy-start | bytes 344068
  91.8 3.9 %collective-permute-start.18 = (bf16[112,512]{1,0:T(8,128)(2,1)S(1)}, bf16[112,512]{1,0:T(8,128)(2,1)S(1)}, u32[]{:S(2)}, u32[]{:S(2)}) collective-permute-start(bf16[112,512]{1,0:T(8,128)(2,1)S(1)} %collective-permute-done.16.refs_2_), channel_id=1, source_target_pairs={{0,7},{1,0},{2,1},{3,2},{4,3},{5,4},{6,5},{7,6},{8,15},{9,8},{10,9... | collective-permute-start | bytes 344072 | tf_op jit(solution)/shard_map/ppermute | solution.py:41
  93.3 5.2 %copy-start.12 = (bf16[112,512]{1,0:T(8,128)(2,1)}, bf16[112,512]{1,0:T(8,128)(2,1)S(1)}, u32[]{:S(2)}) copy-start(bf16[112,512]{1,0:T(8,128)(2,1)S(1)} %collective-permute-done.15.refs_1_) | copy-start | bytes 344068
  93.3 5.1 %collective-permute-start.17 = (bf16[112,512]{1,0:T(8,128)(2,1)S(1)}, bf16[112,512]{1,0:T(8,128)(2,1)}, u32[]{:S(2)}, u32[]{:S(2)}) collective-permute-start(bf16[112,512]{1,0:T(8,128)(2,1)S(1)} %collective-permute-done.15.refs_1_), channel_id=1, source_target_pairs={{0,1},{1,2},{2,3},{3,4},{4,5},{5,6},{6,7},{7,0},{8,9},{9,10},{10,1... | collective-permute-start | bytes 344072 | tf_op jit(solution)/shard_map/ppermute | solution.py:41
  95.8 0.6 copy-start.13
  105.8 1.0 copy-start.3
  109.3 14.8 %all-to-all-start.2 = ((bf16[8,16,896]{2,1,0:T(8,128)(2,1)}), bf16[8,16,896]{2,1,0:T(8,128)(2,1)S(1)}, u32[]{:S(2)}, u32[]{:S(2)}) async-start(bf16[8,16,896]{2,1,0:T(8,128)(2,1)} %choose.1), calls=%async_computation.2 | async-start | bytes 458752 | tf_op jit(solution)/shard_map/all_to_all | solution.py:45
  124.1 0.7 copy-start.5
  140.4 13.1 %copy-start.4 = (bf16[16,16,1024]{2,1,0:T(8,128)(2,1)}, bf16[16,16,1024]{2,1,0:T(8,128)(2,1)S(1)}, u32[]{:S(2)}) copy-start(bf16[16,16,1024]{2,1,0:T(8,128)(2,1)S(1)} %all_to_all.20) | copy-start | bytes 1572868
  140.4 13.1 %collective-permute-start.23 = (bf16[256,1024]{1,0:T(8,128)(2,1)S(1)}, bf16[256,1024]{1,0:T(8,128)(2,1)S(1)}, u32[]{:S(2)}, u32[]{:S(2)}) collective-permute-start(bf16[256,1024]{1,0:T(8,128)(2,1)S(1)} %bitcast.88), channel_id=1, source_target_pairs={{0,8},{8,0},{1,9},{9,1},{2,10},{10,2},{3,11},{11,3},{4,12},{12,4},... | collective-permute-start | bytes 1572872 | tf_op jit(solution)/shard_map/ppermute | solution.py:37
  142.3 6.1 %collective-permute-start.19 = (bf16[112,512]{1,0:T(8,128)(2,1)}, bf16[112,512]{1,0:T(8,128)(2,1)S(1)}, u32[]{:S(2)}, u32[]{:S(2)}) collective-permute-start(bf16[112,512]{1,0:T(8,128)(2,1)} %collective-permute-done.17.refs_3_), channel_id=1, source_target_pairs={{0,1},{1,2},{2,3},{3,4},{4,5},{5,6},{6,7},{7,0},{8,9},{9,10},{10,1... | collective-permute-start | bytes 344072 | tf_op jit(solution)/shard_map/ppermute | solution.py:41
  142.4 6.1 %collective-permute-start.20 = (bf16[112,512]{1,0:T(8,128)(2,1)}, bf16[112,512]{1,0:T(8,128)(2,1)S(1)}, u32[]{:S(2)}, u32[]{:S(2)}) collective-permute-start(bf16[112,512]{1,0:T(8,128)(2,1)} %copy-done.13), channel_id=1, source_target_pairs={{0,7},{1,0},{2,1},{3,2},{4,3},{5,4},{6,5},{7,6},{8,15},{9,8},{10,9... | collective-permute-start | bytes 344072 | tf_op jit(solution)/shard_map/ppermute | solution.py:41
  148.4 5.1 %copy-start.8 = (bf16[112,512]{1,0:T(8,128)(2,1)}, bf16[112,512]{1,0:T(8,128)(2,1)S(1)}, u32[]{:S(2)}) copy-start(bf16[112,512]{1,0:T(8,128)(2,1)S(1)} %collective-permute-done.19.refs_5_) | copy-start | bytes 344068
  148.4 4.4 %collective-permute-start.21 = (bf16[64,512]{1,0:T(8,128)(2,1)S(1)}, bf16[64,512]{1,0:T(8,128)(2,1)S(1)}, u32[]{:S(2)}, u32[]{:S(2)}) collective-permute-start(bf16[64,512]{1,0:T(8,128)(2,1)S(1)} %slice.114), channel_id=1, source_target_pairs={{0,1},{1,2},{2,3},{3,4},{4,5},{5,6},{6,7},{7,0},{8,9},{9,10},{10,1... | collective-permute-start | bytes 196616 | tf_op jit(solution)/shard_map/ppermute | solution.py:41
  148.5 5.0 %copy-start.10 = (bf16[112,512]{1,0:T(8,128)(2,1)}, bf16[112,512]{1,0:T(8,128)(2,1)S(1)}, u32[]{:S(2)}) copy-start(bf16[112,512]{1,0:T(8,128)(2,1)S(1)} %collective-permute-done.20.refs_6_) | copy-start | bytes 344068
  148.6 3.9 %collective-permute-start.22 = (bf16[48,512]{1,0:T(8,128)(2,1)S(1)}, bf16[48,512]{1,0:T(8,128)(2,1)S(1)}, u32[]{:S(2)}, u32[]{:S(2)}) collective-permute-start(bf16[48,512]{1,0:T(8,128)(2,1)S(1)} %slice.115), channel_id=1, source_target_pairs={{0,7},{1,0},{2,1},{3,2},{4,3},{5,4},{6,5},{7,6},{8,15},{9,8},{10,9... | collective-permute-start | bytes 147464 | tf_op jit(solution)/shard_map/ppermute | solution.py:41
  153.5 0.8 copy-start.7

commit v4 on v2

--- a/solution.py
+++ b/solution.py
@@ -72,6 +72,7 @@
             out_specs=pl.BlockSpec((1, 512, depth), lambda f, pos: (f, 0, 0)),
         ),
         out_shape=jax.ShapeDtypeStruct((2, 512, depth), BF16),
+        compiler_params=pltpu.CompilerParams(vmem_limit_bytes=12 << 20),
         name="weights",
     )(pos, gate_t, up_t, far_w)
 
@@ -127,6 +128,7 @@
         in_specs=[SMEM] + [VMEM] * 13,
         out_specs=(VMEM, VMEM),
         scratch_shapes=[pltpu.VMEM((512, 256), F32)],
+        compiler_params=pltpu.CompilerParams(vmem_limit_bytes=12 << 20),
         name="activate",
     )(pos, *own, *far, *error, wh)
 
@@ -149,6 +151,7 @@
             out_specs=pl.BlockSpec((8, 16, 896), lambda i, first: (0, 0, 0)),
         ),
         out_shape=jax.ShapeDtypeStruct((8, 16, 896), BF16),
+        compiler_params=pltpu.CompilerParams(vmem_limit_bytes=6 << 20),
         name="choose",
     )(first, arrived)
 
@@ -185,20 +188,21 @@
         in_specs=[SMEM, VMEM],
         out_specs=(VMEM, VMEM),
         scratch_shapes=[pltpu.VMEM((16, 24 * n), F32)],
+        compiler_params=pltpu.CompilerParams(vmem_limit_bytes=6 << 20),
         name="assemble",
     )(shift, pieces)
 
 
 def slab_kernel(pos_ref, count_ref, *refs):
-    pieces = refs[:9]
-    near, far, total_ref, wh_ref, slab_ref, new_ref, grad_ref, panel_ref = refs[9:]
+    pieces = refs[:8]
+    near, far, total_ref, wh_ref, slab_ref, new_ref, grad_ref, panel_ref = refs[8:]
     z = pos_ref[4]
     n = pieces[0].shape[0]
 
     @pl.when(pl.program_id(0) == 0)
     def _():
-        for piece, d, r0 in zip(pieces, (0, -1, 1, -2, 2, -3, 3, -4, 4), (0,) * 8 + (64,)):
-            at = pl.multiple_of(((z + d + 8) % 8) * n + r0, 16)
+        for piece, d in zip(pieces, (0, -1, 1, -2, 2, -3, 3, 4)):
+            at = pl.multiple_of(((z + d + 8) % 8) * n, 16)
             panel_ref[pl.ds(at, piece.shape[0]), :] = piece[...]
 
     scale = 1.0 / jnp.full((1, 1), count_ref[0].astype(F32), F32)
@@ -234,6 +238,7 @@
             jax.ShapeDtypeStruct((rows, width), F32),
             jax.ShapeDtypeStruct((16, width), F32),
         ),
+        compiler_params=pltpu.CompilerParams(vmem_limit_bytes=20 << 20),
         name="slab",
     )(pos, count, *pieces, near, far, total, wh, slab)
 
@@ -315,12 +320,13 @@
     wh = jnp.concatenate([sums[0], sums[1]], 1)
     pieces, f3, g3, wh = lax.optimization_barrier((pieces, f3, g3, wh))
     f4, g4 = shift_z(f3[:64], 1), shift_z(g3[64:], -1)
+    h4 = jnp.concatenate([f4, g4], 0)
     start = slab_offset[0] + z * width
     shift = start - jnp.minimum(start // panel_width, 29) * panel_width
     chunk, total = assemble_call(pieces, jnp.stack([shift, c]).astype(jnp.int32), width, n)
     near = exchange(chunk, PLANE).reshape(256, width)
     return slab_call(
-        pos, token_count, (hidden_t, f1, g1, f2, g2, f3, g3, f4, g4), near, core_swap(near), total, wh, hessian_slab
+        pos, token_count, (hidden_t, f1, g1, f2, g2, f3, g3, h4), near, core_swap(near), total, wh, hessian_slab
     )
 
 

time: 154 us -> 149 us (0.968)
  waiting for transfers between devices: 34.1 us -> 46.5 us
  matrix products: 22.1 us -> 14.2 us
  Pallas kernels: 17.7 us -> 10 us
  other arithmetic: 7 us -> 3.75 us
  local copies, waits for them, and re-layouts: 12 us -> 13.8 us
    ppermute x9, waiting for transfers between devices: 3.56 us -> 13.7 us  [plane_permute(): return lax.ppermute(array, CAL_GR, pairs)]
    dot_general x16, matrix products: 15.8 us -> 7.83 us  [products(): lax.dot_general(tokens, half, NT, preferred_element_type=F32)]
    unnamed x26 -> x22, local copies, waits for them, and re-layouts: 3.95 us -> 8.54 us
    pallas_call x1, Pallas kernels: 3.66 us -> 1.3 us  [activate_call(): pl.pallas_call(activate, out_shape=(jax.ShapeDtypeStruct((32, 16, 640 + w...]
    pallas_call x1, Pallas kernels: 4.26 us -> 2.27 us  [weights_call(): pl.pallas_call(weights_kernel, grid_spec=pltpu.PrefetchScalarGridSpec(num...]
    convert_element_type x1, other arithmetic: 2.18 us -> 0.25 us  [on_device(): wh = (wh_own + wh_far).astype(BF16)]
    slice x2, local copies, waits for them, and re-layouts: 1.65 us -> 0.01 us  [on_device(): f4, g4 = (shift_z(f3[:64], 1), shift_z(g3[64:], -1))]
  transfers between devices with their start and end apart: 26 -> 26, of which waited for: 10 -> 14; matrix products, arithmetic and copies ran while one was open for 22% -> 12% of each run, Pallas kernels for 4% -> 2%
where the time goes in v4:
time: 149 us; the launch traced here: 148 us
  waiting for transfers between devices  46.5 us (31%)
  starting transfers between devices  45 us (30%)
  matrix products  14.2 us (10%)
  local copies, waits for them, and re-layouts  13.8 us (9%)
  blocking collectives  12.7 us (9%)
  Pallas kernels  10 us (7%)
  other arithmetic  3.75 us (3%)
  between operations  2.39 us (2%)
    all_to_all x3, waiting for transfers between devices, exchange(): return lax.all_to_all(array, axes, split_axis=0, concat_axis=0, tiled=True)  23.6 us
    all_to_all x3, starting transfers between devices, exchange(): return lax.all_to_all(array, axes, split_axis=0, concat_axis=0, tiled=True)  16.2 us
    ppermute x9, waiting for transfers between devices, plane_permute(): return lax.ppermute(array, CAL_GR, pairs)  13.7 us
    all_to_all x1, blocking collectives, exchange(): return lax.all_to_all(array, axes, split_axis=0, concat_axis=0, tiled=True)  12.7 us
    ppermute x9, starting transfers between devices, plane_permute(): return lax.ppermute(array, CAL_GR, pairs)  10.7 us
    ppermute x6, starting transfers between devices, core_swap(): return lax.ppermute(array, 'gr_2', [(0, 1), (1, 0)])  9.83 us
    unnamed x22, local copies, waits for them, and re-layouts  8.54 us
    ppermute x8, starting transfers between devices, shift_z(): return lax.ppermute(array, 'gc', [(i, (i + d) % 8) for i in range(8)])  8.38 us
  transfers between devices with their start and end apart: 26, of which 14 were waited for; matrix products, arithmetic and copies ran while one was open for 12% of the time, Pallas kernels for 2%

profile of v4, /device:TPU:1, one launch (start us, length us, event | category | flops | bytes accessed | tf_op | source)
XLA Modules:
  0.0 148.4 jit_solution(11177305832794743655)
XLA Ops:
  0.7 0.9 constant_dynamic-slice_fusion.1
  1.5 3.2 %collective-permute-start = (bf16[4,2048]{1,0:T(4,128)(2,1)S(1)}, bf16[4,2048]{1,0:T(4,128)(2,1)S(1)}, u32[]{:S(2)}, u32[]{:S(2)}) collective-permute-start(bf16[4,2048]{1,0:T(4,128)(2,1)S(1)} %constant_dynamic-slice_fusion.1), channel_id=1, source_target_pairs={{0,8},{8,0},{1,9},{9,1},{2,10},{10,2},{3,11},{11,3},{4,12},{12,4},... | collective-permute-start | bytes 49160 | tf_op jit(solution)/shard_map/ppermute | solution.py:37
  4.7 0.8 collective-permute-done
  5.6 0.7 broadcast_select_fusion.1
  6.3 0.7 broadcast_in_dim.2
  7.0 1.6 %dynamic-slice_bitcast_fusion.14 = (bf16[1,112,2048]{2,1,0:T(8,128)(2,1)S(1)}, bf16[1,112,2048]{2,1,0:T(8,128)(2,1)S(1)}, bf16[1,112,2048]{2,1,0:T(8,128)(2,1)S(1)}, bf16[1,112,2048]{2,1,0:T(8,128)(2,1)S(1)}) fusion(bf16[8192,112]{0,1:T(8,128)(2,1)} %param.9, s32[]{:T(128)S(6)} %select_n.61, s32[]{:T(128)S(6)} %select_n.62, bf16[8192,112]{0,1:T(8,128)(2,1)} %param.8), kind=kLoop, calls=%fused_computation.33 | loop fusion | bytes 3670024 | tf_op jit(solution)/shard_map/stack | solution.py:263
  8.6 1.5 pad_maximum_fusion
  10.4 6.5 %all-to-all-start = ((bf16[8,8,2048]{2,1,0:T(8,128)(2,1)}), bf16[8,8,2048]{2,1,0:T(8,128)(2,1)S(1)}, u32[]{:S(2)}, u32[]{:S(2)}) async-start(bf16[8,8,2048]{2,1,0:T(8,128)(2,1)} %broadcast_in_dim.2), calls=%async_computation | async-start | bytes 524288 | tf_op jit(solution)/shard_map/all_to_all | solution.py:45
  17.0 4.5 %fusion = f32[512,512]{1,0:T(8,128)} fusion(f32[512,896]{1,0:T(8,128)S(1)} %copy-done, f32[896,1024]{1,0:T(8,128)} %refs_12_.1, s32[]{:T(128)S(6)} %select_n.60), kind=kOutput, calls=%fused_computation.1 | convolution fusion | flops 1409286144 | bytes 4718596 | tf_op jit(solution)/shard_map/dot_general | solution.py:275
  21.6 1.9 %fusion.2 = f32[512,512]{1,0:T(8,128)S(1)} fusion(f32[512,896]{1,0:T(8,128)S(1)} %copy-done, f32[896,1024]{1,0:T(8,128)S(1)} %copy-done.1, s32[]{:T(128)S(6)} %select_n.59), kind=kOutput, calls=%fused_computation.3 | convolution fusion | flops 1409286144 | bytes 4718596 | tf_op jit(solution)/shard_map/dot_general | solution.py:275
  23.5 5.6 %all-to-all-done = bf16[8,8,2048]{2,1,0:T(8,128)(2,1)S(1)} async-done(((bf16[8,8,2048]{2,1,0:T(8,128)(2,1)}), bf16[8,8,2048]{2,1,0:T(8,128)(2,1)S(1)}, u32[]{:S(2)}, u32[]{:S(2)}) %all-to-all-start) | async-done | bytes 262176 | tf_op jit(solution)/shard_map/all_to_all | solution.py:45
  29.1 2.9 %collective-permute-start.2 = (bf16[64,2048]{1,0:T(8,128)(2,1)S(1)}, bf16[64,2048]{1,0:T(8,128)(2,1)}, u32[]{:S(2)}, u32[]{:S(2)}) collective-permute-start(bf16[64,2048]{1,0:T(8,128)(2,1)S(1)} %bitcast.91), channel_id=1, source_target_pairs={{0,64},{8,40},{16,80},{24,56},{32,96},{40,8},{48,112},{56,24},{128... | collective-permute-start | bytes 786440 | tf_op jit(solution)/shard_map/ppermute | solution.py:33
  32.1 0.8 collective-permute-start.4
  32.9 1.2 collective-permute-start.13
  34.1 1.5 %copy-done.3 = bf16[8192,112]{0,1:T(8,128)(2,1)S(1)} copy-done((bf16[8192,112]{0,1:T(8,128)(2,1)S(1)}, bf16[8192,112]{0,1:T(8,128)(2,1)}, u32[]{:S(2)}) %copy-start.3) | copy-done | bytes 1835032
  35.6 1.5 %copy-done.4 = bf16[8192,112]{0,1:T(8,128)(2,1)S(1)} copy-done((bf16[8192,112]{0,1:T(8,128)(2,1)S(1)}, bf16[8192,112]{0,1:T(8,128)(2,1)}, u32[]{:S(2)}) %copy-start.4) | copy-done | bytes 1835032
  37.1 2.3 %weights.1 = bf16[2,512,2048]{2,1,0:T(8,128)(2,1)S(1)} custom-call(s32[5]{0:T(128)S(1)} %stack.45.pos_ref, bf16[112,8192]{1,0:T(8,128)(2,1)S(1)} %bitcast.86, bf16[112,8192]{1,0:T(8,128)(2,1)S(1)} %bitcast.87, bf16[2,2,112,2048]{3,2,1,0:T(8,128)(2,1)} %bitcast.16.far), custom_call_target="tpu_custom_call" | custom-call | tf_op jit(solution)/shard_map/weights/pallas_call | solution.py:66
  39.4 1.0 constant_dynamic-update-slice_fusion
  40.3 1.9 %collective-permute-start.7 = (bf16[128,2048]{1,0:T(8,128)(2,1)S(1)}, bf16[128,2048]{1,0:T(8,128)(2,1)S(1)}, u32[]{:S(2)}, u32[]{:S(2)}) collective-permute-start(bf16[128,2048]{1,0:T(8,128)(2,1)S(1)} %constant_dynamic-update-slice_fusion), channel_id=1, source_target_pairs={{0,48},{8,200},{16,32},{24,216},{32,16},{40,232},{48,0},{56,248},{... | collective-permute-start | bytes 1572872 | tf_op jit(solution)/shard_map/ppermute | solution.py:33
  42.3 1.1 collective-permute-start.5
  43.5 0.9 collective-permute-start.8
  44.9 0.5 convolution_dynamic-update-slice_fusion.5
  45.4 0.5 fusion.10.refs_1_
  45.9 0.5 convolution_dynamic-update-slice_fusion.4
  46.4 4.2 %collective-permute-done.5 = bf16[128,2048]{1,0:T(8,128)(2,1)S(1)} collective-permute-done((bf16[128,2048]{1,0:T(8,128)(2,1)S(1)}, bf16[128,2048]{1,0:T(8,128)(2,1)S(1)}, u32[]{:S(2)}, u32[]{:S(2)}) %collective-permute-start.5) | collective-permute-done | bytes 524320 | tf_op jit(solution)/shard_map/ppermute | solution.py:33
  50.6 0.5 convolution_dynamic-update-slice_fusion.3
  51.1 5.1 %collective-permute-done.6 = bf16[128,2048]{1,0:T(8,128)(2,1)S(1)} collective-permute-done((bf16[128,2048]{1,0:T(8,128)(2,1)S(1)}, bf16[128,2048]{1,0:T(8,128)(2,1)S(1)}, u32[]{:S(2)}, u32[]{:S(2)}) %collective-permute-start.6) | collective-permute-done | bytes 524320 | tf_op jit(solution)/shard_map/ppermute | solution.py:33
  56.7 0.5 convolution_dynamic-update-slice_fusion.1
  57.7 2.2 %collective-permute-start.11 = (f32[768,256]{1,0:T(8,128)S(1)}, f32[768,256]{1,0:T(8,128)S(1)}, u32[]{:S(2)}, u32[]{:S(2)}) collective-permute-start(f32[768,256]{1,0:T(8,128)S(1)} %convolution_dynamic-update-slice_fusion), channel_id=1, source_target_pairs={{0,8},{8,0},{1,9},{9,1},{2,10},{10,2},{3,11},{11,3},{4,12},{12,4},... | collective-permute-start | bytes 2359304 | tf_op jit(solution)/shard_map/ppermute | solution.py:37
  59.9 1.8 %collective-permute-start.9 = (bf16[128,2048]{1,0:T(8,128)(2,1)S(1)}, bf16[128,2048]{1,0:T(8,128)(2,1)S(1)}, u32[]{:S(2)}, u32[]{:S(2)}) collective-permute-start(bf16[128,2048]{1,0:T(8,128)(2,1)S(1)} %collective-permute-done.5), channel_id=1, source_target_pairs={{0,48},{8,200},{16,32},{24,216},{32,16},{40,232},{48,0},{56,248},{... | collective-permute-start | bytes 1572872 | tf_op jit(solution)/shard_map/ppermute | solution.py:33
  61.7 1.1 collective-permute-start.10
  62.8 0.5 fusion.11.refs_4_
  63.8 0.5 fusion.7.refs_3_
  64.3 0.5 fusion.12.refs_2_
  65.1 4.3 %collective-permute-done.9 = bf16[128,2048]{1,0:T(8,128)(2,1)S(1)} collective-permute-done((bf16[128,2048]{1,0:T(8,128)(2,1)S(1)}, bf16[128,2048]{1,0:T(8,128)(2,1)S(1)}, u32[]{:S(2)}, u32[]{:S(2)}) %collective-permute-start.9) | collective-permute-done | bytes 524320 | tf_op jit(solution)/shard_map/ppermute | solution.py:33
  70.0 0.5 fusion.13
  70.5 1.0 collective-permute-start.12
  71.5 0.5 fusion.9.refs_7_
  72.6 1.3 activate.1
  74.0 1.0 copy-done.5
  75.0 6.3 %all-to-all-start.1 = ((bf16[32,16,1152]{2,1,0:T(8,128)(2,1)}), bf16[32,16,1152]{2,1,0:T(8,128)(2,1)S(1)}, u32[]{:S(2)}, u32[]{:S(2)}) async-start(bf16[32,16,1152]{2,1,0:T(8,128)(2,1)} %copy-done.5), calls=%async_computation.1 | async-start | bytes 2359296 | tf_op jit(solution)/shard_map/all_to_all | solution.py:45
  81.4 1.5 collective-permute-start.14
  83.5 2.3 %collective-permute-done.15.refs_2_ = bf16[112,512]{1,0:T(8,128)(2,1)S(1)} collective-permute-done((bf16[112,512]{1,0:T(8,128)(2,1)S(1)}, bf16[112,512]{1,0:T(8,128)(2,1)S(1)}, u32[]{:S(2)}, u32[]{:S(2)}) %collective-permute-start.15) | collective-permute-done | bytes 114720 | tf_op jit(solution)/shard_map/ppermute | solution.py:41
  85.8 1.5 %collective-permute-start.17 = (bf16[112,512]{1,0:T(8,128)(2,1)S(1)}, bf16[112,512]{1,0:T(8,128)(2,1)S(1)}, u32[]{:S(2)}, u32[]{:S(2)}) collective-permute-start(bf16[112,512]{1,0:T(8,128)(2,1)S(1)} %collective-permute-done.15.refs_2_), channel_id=1, source_target_pairs={{0,7},{1,0},{2,1},{3,2},{4,3},{5,4},{6,5},{7,6},{8,15},{9,8},{10,9... | collective-permute-start | bytes 344072 | tf_op jit(solution)/shard_map/ppermute | solution.py:41
  87.3 0.6 copy-done.6
  88.1 1.7 %collective-permute-done.17.refs_4_ = bf16[112,512]{1,0:T(8,128)(2,1)S(1)} collective-permute-done((bf16[112,512]{1,0:T(8,128)(2,1)S(1)}, bf16[112,512]{1,0:T(8,128)(2,1)S(1)}, u32[]{:S(2)}, u32[]{:S(2)}) %collective-permute-start.17) | collective-permute-done | bytes 114720 | tf_op jit(solution)/shard_map/ppermute | solution.py:41
  89.8 2.7 %collective-permute-done.16.refs_3_ = bf16[112,512]{1,0:T(8,128)(2,1)} collective-permute-done((bf16[112,512]{1,0:T(8,128)(2,1)S(1)}, bf16[112,512]{1,0:T(8,128)(2,1)}, u32[]{:S(2)}, u32[]{:S(2)}) %collective-permute-start.16) | collective-permute-done | bytes 114720 | tf_op jit(solution)/shard_map/ppermute | solution.py:41
  92.5 7.5 %all-to-all-done.1.arrived_ref = bf16[32,16,1152]{2,1,0:T(8,128)(2,1)S(1)} async-done(((bf16[32,16,1152]{2,1,0:T(8,128)(2,1)}), bf16[32,16,1152]{2,1,0:T(8,128)(2,1)S(1)}, u32[]{:S(2)}, u32[]{:S(2)}) %all-to-all-start.1) | async-done | bytes 1179680 | tf_op jit(solution)/shard_map/all_to_all | solution.py:45
  100.3 2.4 %collective-permute-start.19 = (bf16[112,512]{1,0:T(8,128)(2,1)}, bf16[112,512]{1,0:T(8,128)(2,1)S(1)}, u32[]{:S(2)}, u32[]{:S(2)}) collective-permute-start(bf16[112,512]{1,0:T(8,128)(2,1)} %copy-done.8), channel_id=1, source_target_pairs={{0,7},{1,0},{2,1},{3,2},{4,3},{5,4},{6,5},{7,6},{8,15},{9,8},{10,9... | collective-permute-start | bytes 344072 | tf_op jit(solution)/shard_map/ppermute | solution.py:41
  102.7 0.9 slice.95
  103.5 1.4 choose.1
  104.9 3.4 %all-to-all-start.2 = ((bf16[8,16,896]{2,1,0:T(8,128)(2,1)}), bf16[8,16,896]{2,1,0:T(8,128)(2,1)S(1)}, u32[]{:S(2)}, u32[]{:S(2)}) async-start(bf16[8,16,896]{2,1,0:T(8,128)(2,1)} %choose.1), calls=%async_computation.2 | async-start | bytes 458752 | tf_op jit(solution)/shard_map/all_to_all | solution.py:45
  108.3 1.1 convert_reduce_fusion
  109.5 10.4 %all-to-all-done.2.refs_1_ = bf16[8,16,896]{2,1,0:T(8,128)(2,1)S(1)} async-done(((bf16[8,16,896]{2,1,0:T(8,128)(2,1)}), bf16[8,16,896]{2,1,0:T(8,128)(2,1)S(1)}, u32[]{:S(2)}, u32[]{:S(2)}) %all-to-all-start.2) | async-done | bytes 229408 | tf_op jit(solution)/shard_map/all_to_all | solution.py:45
  120.0 0.8 assemble.1
  120.7 12.7 %all_to_all.20 = bf16[16,16,1024]{2,1,0:T(8,128)(2,1)S(1)} all-to-all(bf16[16,16,1024]{2,1,0:T(8,128)(2,1)S(1)} %get-tuple-element.41), channel_id=1, replica_groups=mesh['cal'=2,'gr_0'=2,'gr_1'=4,'gr_2'=2,'gc'=8] {'cal','gr_0','gr_1'}, dimensions={0} | all-to-all | bytes 1048576 | tf_op jit(solution)/shard_map/all_to_all | solution.py:45
  133.4 2.0 %collective-permute-start.22 = (bf16[256,1024]{1,0:T(8,128)(2,1)S(1)}, bf16[256,1024]{1,0:T(8,128)(2,1)S(1)}, u32[]{:S(2)}, u32[]{:S(2)}) collective-permute-start(bf16[256,1024]{1,0:T(8,128)(2,1)S(1)} %bitcast.88), channel_id=1, source_target_pairs={{0,8},{8,0},{1,9},{9,1},{2,10},{10,2},{3,11},{11,3},{4,12},{12,4},... | collective-permute-start | bytes 1572872 | tf_op jit(solution)/shard_map/ppermute | solution.py:37
  135.5 2.7 %collective-permute-start.21 = (bf16[48,512]{1,0:T(8,128)(2,1)S(1)}, bf16[48,512]{1,0:T(8,128)(2,1)S(1)}, u32[]{:S(2)}, u32[]{:S(2)}) collective-permute-start(bf16[48,512]{1,0:T(8,128)(2,1)S(1)} %slice.99), channel_id=1, source_target_pairs={{0,7},{1,0},{2,1},{3,2},{4,3},{5,4},{6,5},{7,6},{8,15},{9,8},{10,9... | collective-permute-start | bytes 147464 | tf_op jit(solution)/shard_map/ppermute | solution.py:41
  138.8 0.5 collective-permute-done.21
  139.3 0.9 collective-permute-done.20
  140.3 2.0 %copy-done.2 = f32[896,1024]{1,0:T(8,128)S(1)} copy-done((f32[896,1024]{1,0:T(8,128)S(1)}, f32[896,1024]{1,0:T(8,128)}, u32[]{:S(2)}) %copy-start.2) | copy-done | bytes 3670040
  142.3 0.9 copy-done.7
  143.2 0.9 copy-done.9
  144.1 4.3 %slab.1 = (f32[896,1024]{1,0:T(8,128)}, f32[16,1024]{1,0:T(8,128)}) custom-call(s32[5]{0:T(128)S(1)} %stack.45.pos_ref, s32[1]{0:T(128)S(6)} %copy.17.count_ref, bf16[112,512]{1,0:T(8,128)(2,1)S(1)} %get-tuple-element.33.refs_0_, bf16[112,512]{1,0:T(8,128)(2,1)S(1)} %copy-done.7, bf16[112,512]{1,0:T(8,128)(2,1)S(1)} %collective-permute-done.15.refs_2_, ...), custom_call_target="tpu_custom_call" | custom-call | tf_op jit(solution)/shard_map/slab/pallas_call | solution.py:227
  (57 shorter events, 4.7 us)
Async XLA Ops:
  0.6 16.2 %copy-start = (f32[512,896]{1,0:T(8,128)S(1)}, f32[512,896]{1,0:T(8,128)}, u32[]{:S(2)}) copy-start(f32[512,896]{1,0:T(8,128)} %param.11) | copy-start | bytes 5505028
  1.5 4.0 %collective-permute-start = (bf16[4,2048]{1,0:T(4,128)(2,1)S(1)}, bf16[4,2048]{1,0:T(4,128)(2,1)S(1)}, u32[]{:S(2)}, u32[]{:S(2)}) collective-permute-start(bf16[4,2048]{1,0:T(4,128)(2,1)S(1)} %constant_dynamic-slice_fusion.1), channel_id=1, source_target_pairs={{0,8},{8,0},{1,9},{9,1},{2,10},{10,2},{3,11},{11,3},{4,12},{12,4},... | collective-permute-start | bytes 49160 | tf_op jit(solution)/shard_map/ppermute | solution.py:37
  10.0 19.1 %collective-permute-start.1 = (bf16[4,112,2048]{2,1,0:T(8,128)(2,1)}, bf16[4,112,2048]{2,1,0:T(8,128)(2,1)}, u32[]{:S(2)}, u32[]{:S(2)}) collective-permute-start(bf16[4,112,2048]{2,1,0:T(8,128)(2,1)} %pad_maximum_fusion), channel_id=1, source_target_pairs={{0,8},{8,0},{1,9},{9,1},{2,10},{10,2},{3,11},{11,3},{4,12},{12,4},... | collective-permute-start | bytes 5505032 | tf_op jit(solution)/shard_map/ppermute | solution.py:37
  10.4 18.7 %all-to-all-start = ((bf16[8,8,2048]{2,1,0:T(8,128)(2,1)}), bf16[8,8,2048]{2,1,0:T(8,128)(2,1)S(1)}, u32[]{:S(2)}, u32[]{:S(2)}) async-start(bf16[8,8,2048]{2,1,0:T(8,128)(2,1)} %broadcast_in_dim.2), calls=%async_computation | async-start | bytes 524288 | tf_op jit(solution)/shard_map/all_to_all | solution.py:45
  16.9 4.7 %copy-start.1 = (f32[896,1024]{1,0:T(8,128)S(1)}, f32[896,1024]{1,0:T(8,128)}, u32[]{:S(2)}) copy-start(f32[896,1024]{1,0:T(8,128)} %refs_12_.1) | copy-start | bytes 11010052
  29.1 10.3 %collective-permute-start.2 = (bf16[64,2048]{1,0:T(8,128)(2,1)S(1)}, bf16[64,2048]{1,0:T(8,128)(2,1)}, u32[]{:S(2)}, u32[]{:S(2)}) collective-permute-start(bf16[64,2048]{1,0:T(8,128)(2,1)S(1)} %bitcast.91), channel_id=1, source_target_pairs={{0,64},{8,40},{16,80},{24,56},{32,96},{40,8},{48,112},{56,24},{128... | collective-permute-start | bytes 786440 | tf_op jit(solution)/shard_map/ppermute | solution.py:33
  32.1 11.3 %collective-permute-start.4 = (bf16[64,2048]{1,0:T(8,128)(2,1)S(1)}, bf16[64,2048]{1,0:T(8,128)(2,1)S(1)}, u32[]{:S(2)}, u32[]{:S(2)}) collective-permute-start(bf16[64,2048]{1,0:T(8,128)(2,1)S(1)} %bitcast.92), channel_id=1, source_target_pairs={{0,192},{8,56},{16,208},{24,40},{32,224},{40,24},{48,240},{56,8},{... | collective-permute-start | bytes 786440 | tf_op jit(solution)/shard_map/ppermute | solution.py:33
  32.9 10.5 %collective-permute-start.3 = (bf16[64,2048]{1,0:T(8,128)(2,1)S(1)}, bf16[64,2048]{1,0:T(8,128)(2,1)S(1)}, u32[]{:S(2)}, u32[]{:S(2)}) collective-permute-start(bf16[64,2048]{1,0:T(8,128)(2,1)S(1)} %bitcast.93), channel_id=1, source_target_pairs={{0,128},{8,24},{16,144},{24,8},{32,160},{40,56},{48,176},{56,40},{... | collective-permute-start | bytes 786440 | tf_op jit(solution)/shard_map/ppermute | solution.py:33
  32.9 31.9 %collective-permute-start.13 = (f32[512,512]{1,0:T(8,128)}, f32[512,512]{1,0:T(8,128)S(1)}, u32[]{:S(2)}, u32[]{:S(2)}) collective-permute-start(f32[512,512]{1,0:T(8,128)} %fusion), channel_id=1, source_target_pairs={{0,8},{8,0},{1,9},{9,1},{2,10},{10,2},{3,11},{11,3},{4,12},{12,4},... | collective-permute-start | bytes 3145736 | tf_op jit(solution)/shard_map/ppermute | solution.py:37
  34.1 1.5 %copy-start.3 = (bf16[8192,112]{0,1:T(8,128)(2,1)S(1)}, bf16[8192,112]{0,1:T(8,128)(2,1)}, u32[]{:S(2)}) copy-start(bf16[8192,112]{0,1:T(8,128)(2,1)} %param.8) | copy-start | bytes 5505028
  35.6 1.5 %copy-start.4 = (bf16[8192,112]{0,1:T(8,128)(2,1)S(1)}, bf16[8192,112]{0,1:T(8,128)(2,1)}, u32[]{:S(2)}) copy-start(bf16[8192,112]{0,1:T(8,128)(2,1)} %param.9) | copy-start | bytes 5505028
  40.3 16.3 %collective-permute-start.7 = (bf16[128,2048]{1,0:T(8,128)(2,1)S(1)}, bf16[128,2048]{1,0:T(8,128)(2,1)S(1)}, u32[]{:S(2)}, u32[]{:S(2)}) collective-permute-start(bf16[128,2048]{1,0:T(8,128)(2,1)S(1)} %constant_dynamic-update-slice_fusion), channel_id=1, source_target_pairs={{0,48},{8,200},{16,32},{24,216},{32,16},{40,232},{48,0},{56,248},{... | collective-permute-start | bytes 1572872 | tf_op jit(solution)/shard_map/ppermute | solution.py:33
  42.3 8.3 %collective-permute-start.5 = (bf16[128,2048]{1,0:T(8,128)(2,1)S(1)}, bf16[128,2048]{1,0:T(8,128)(2,1)S(1)}, u32[]{:S(2)}, u32[]{:S(2)}) collective-permute-start(bf16[128,2048]{1,0:T(8,128)(2,1)S(1)} %constant_dynamic-update-slice_fusion), channel_id=1, source_target_pairs={{0,16},{8,136},{16,0},{24,152},{32,48},{40,168},{48,32},{56,184},{... | collective-permute-start | bytes 1572872 | tf_op jit(solution)/shard_map/ppermute | solution.py:33
  43.5 13.8 %collective-permute-start.8 = (bf16[128,2048]{1,0:T(8,128)(2,1)S(1)}, bf16[128,2048]{1,0:T(8,128)(2,1)S(1)}, u32[]{:S(2)}, u32[]{:S(2)}) collective-permute-start(bf16[128,2048]{1,0:T(8,128)(2,1)S(1)} %constant_dynamic-update-slice_fusion.2), channel_id=1, source_target_pairs={{0,48},{8,200},{16,32},{24,216},{32,16},{40,232},{48,0},{56,248},{... | collective-permute-start | bytes 1572872 | tf_op jit(solution)/shard_map/ppermute | solution.py:33
  44.4 11.8 %collective-permute-start.6 = (bf16[128,2048]{1,0:T(8,128)(2,1)S(1)}, bf16[128,2048]{1,0:T(8,128)(2,1)S(1)}, u32[]{:S(2)}, u32[]{:S(2)}) collective-permute-start(bf16[128,2048]{1,0:T(8,128)(2,1)S(1)} %constant_dynamic-update-slice_fusion.2), channel_id=1, source_target_pairs={{0,16},{8,136},{16,0},{24,152},{32,48},{40,168},{48,32},{56,184},{... | collective-permute-start | bytes 1572872 | tf_op jit(solution)/shard_map/ppermute | solution.py:33
  57.7 14.9 %collective-permute-start.11 = (f32[768,256]{1,0:T(8,128)S(1)}, f32[768,256]{1,0:T(8,128)S(1)}, u32[]{:S(2)}, u32[]{:S(2)}) collective-permute-start(f32[768,256]{1,0:T(8,128)S(1)} %convolution_dynamic-update-slice_fusion), channel_id=1, source_target_pairs={{0,8},{8,0},{1,9},{9,1},{2,10},{10,2},{3,11},{11,3},{4,12},{12,4},... | collective-permute-start | bytes 2359304 | tf_op jit(solution)/shard_map/ppermute | solution.py:37
  59.9 9.5 %collective-permute-start.9 = (bf16[128,2048]{1,0:T(8,128)(2,1)S(1)}, bf16[128,2048]{1,0:T(8,128)(2,1)S(1)}, u32[]{:S(2)}, u32[]{:S(2)}) collective-permute-start(bf16[128,2048]{1,0:T(8,128)(2,1)S(1)} %collective-permute-done.5), channel_id=1, source_target_pairs={{0,48},{8,200},{16,32},{24,216},{32,16},{40,232},{48,0},{56,248},{... | collective-permute-start | bytes 1572872 | tf_op jit(solution)/shard_map/ppermute | solution.py:33
  61.7 8.3 %collective-permute-start.10 = (bf16[128,2048]{1,0:T(8,128)(2,1)S(1)}, bf16[128,2048]{1,0:T(8,128)(2,1)S(1)}, u32[]{:S(2)}, u32[]{:S(2)}) collective-permute-start(bf16[128,2048]{1,0:T(8,128)(2,1)S(1)} %collective-permute-done.8), channel_id=1, source_target_pairs={{0,16},{8,136},{16,0},{24,152},{32,48},{40,168},{48,32},{56,184},{... | collective-permute-start | bytes 1572872 | tf_op jit(solution)/shard_map/ppermute | solution.py:33
  70.5 2.1 %collective-permute-start.12 = (f32[256,256]{1,0:T(8,128)S(1)}, f32[256,256]{1,0:T(8,128)S(1)}, u32[]{:S(2)}, u32[]{:S(2)}) collective-permute-start(f32[256,256]{1,0:T(8,128)S(1)} %pad_maximum_fusion.1), channel_id=1, source_target_pairs={{0,8},{8,0},{1,9},{9,1},{2,10},{10,2},{3,11},{11,3},{4,12},{12,4},... | collective-permute-start | bytes 786440 | tf_op jit(solution)/shard_map/ppermute | solution.py:37
  74.0 1.0 copy-start.5
  75.0 25.0 %all-to-all-start.1 = ((bf16[32,16,1152]{2,1,0:T(8,128)(2,1)}), bf16[32,16,1152]{2,1,0:T(8,128)(2,1)S(1)}, u32[]{:S(2)}, u32[]{:S(2)}) async-start(bf16[32,16,1152]{2,1,0:T(8,128)(2,1)} %copy-done.5), calls=%async_computation.1 | async-start | bytes 2359296 | tf_op jit(solution)/shard_map/all_to_all | solution.py:45
  81.3 4.5 %collective-permute-start.15 = (bf16[112,512]{1,0:T(8,128)(2,1)S(1)}, bf16[112,512]{1,0:T(8,128)(2,1)S(1)}, u32[]{:S(2)}, u32[]{:S(2)}) collective-permute-start(bf16[112,512]{1,0:T(8,128)(2,1)S(1)} %get-tuple-element.33.refs_0_), channel_id=1, source_target_pairs={{0,7},{1,0},{2,1},{3,2},{4,3},{5,4},{6,5},{7,6},{8,15},{9,8},{10,9... | collective-permute-start | bytes 344072 | tf_op jit(solution)/shard_map/ppermute | solution.py:41
  81.4 6.0 %collective-permute-start.14 = (bf16[112,512]{1,0:T(8,128)(2,1)S(1)}, bf16[112,512]{1,0:T(8,128)(2,1)S(1)}, u32[]{:S(2)}, u32[]{:S(2)}) collective-permute-start(bf16[112,512]{1,0:T(8,128)(2,1)S(1)} %get-tuple-element.33.refs_0_), channel_id=1, source_target_pairs={{0,1},{1,2},{2,3},{3,4},{4,5},{5,6},{6,7},{7,0},{8,9},{9,10},{10,1... | collective-permute-start | bytes 344072 | tf_op jit(solution)/shard_map/ppermute | solution.py:41
  85.8 3.9 %collective-permute-start.17 = (bf16[112,512]{1,0:T(8,128)(2,1)S(1)}, bf16[112,512]{1,0:T(8,128)(2,1)S(1)}, u32[]{:S(2)}, u32[]{:S(2)}) collective-permute-start(bf16[112,512]{1,0:T(8,128)(2,1)S(1)} %collective-permute-done.15.refs_2_), channel_id=1, source_target_pairs={{0,7},{1,0},{2,1},{3,2},{4,3},{5,4},{6,5},{7,6},{8,15},{9,8},{10,9... | collective-permute-start | bytes 344072 | tf_op jit(solution)/shard_map/ppermute | solution.py:41
  87.3 5.1 %collective-permute-start.16 = (bf16[112,512]{1,0:T(8,128)(2,1)S(1)}, bf16[112,512]{1,0:T(8,128)(2,1)}, u32[]{:S(2)}, u32[]{:S(2)}) collective-permute-start(bf16[112,512]{1,0:T(8,128)(2,1)S(1)} %collective-permute-done.14.refs_1_), channel_id=1, source_target_pairs={{0,1},{1,2},{2,3},{3,4},{4,5},{5,6},{6,7},{7,0},{8,9},{9,10},{10,1... | collective-permute-start | bytes 344072 | tf_op jit(solution)/shard_map/ppermute | solution.py:41
  87.3 0.6 copy-start.6
  89.8 10.2 %copy-start.8 = (bf16[112,512]{1,0:T(8,128)(2,1)}, bf16[112,512]{1,0:T(8,128)(2,1)S(1)}, u32[]{:S(2)}) copy-start(bf16[112,512]{1,0:T(8,128)(2,1)S(1)} %collective-permute-done.17.refs_4_) | copy-start | bytes 344068
  100.0 9.5 %collective-permute-start.18 = (bf16[112,512]{1,0:T(8,128)(2,1)}, bf16[112,512]{1,0:T(8,128)(2,1)S(1)}, u32[]{:S(2)}, u32[]{:S(2)}) collective-permute-start(bf16[112,512]{1,0:T(8,128)(2,1)} %collective-permute-done.16.refs_3_), channel_id=1, source_target_pairs={{0,1},{1,2},{2,3},{3,4},{4,5},{5,6},{6,7},{7,0},{8,9},{9,10},{10,1... | collective-permute-start | bytes 344072 | tf_op jit(solution)/shard_map/ppermute | solution.py:41
  100.3 9.2 %collective-permute-start.19 = (bf16[112,512]{1,0:T(8,128)(2,1)}, bf16[112,512]{1,0:T(8,128)(2,1)S(1)}, u32[]{:S(2)}, u32[]{:S(2)}) collective-permute-start(bf16[112,512]{1,0:T(8,128)(2,1)} %copy-done.8), channel_id=1, source_target_pairs={{0,7},{1,0},{2,1},{3,2},{4,3},{5,4},{6,5},{7,6},{8,15},{9,8},{10,9... | collective-permute-start | bytes 344072 | tf_op jit(solution)/shard_map/ppermute | solution.py:41
  104.9 15.0 %all-to-all-start.2 = ((bf16[8,16,896]{2,1,0:T(8,128)(2,1)}), bf16[8,16,896]{2,1,0:T(8,128)(2,1)S(1)}, u32[]{:S(2)}, u32[]{:S(2)}) async-start(bf16[8,16,896]{2,1,0:T(8,128)(2,1)} %choose.1), calls=%async_computation.2 | async-start | bytes 458752 | tf_op jit(solution)/shard_map/all_to_all | solution.py:45
  133.4 6.8 %collective-permute-start.22 = (bf16[256,1024]{1,0:T(8,128)(2,1)S(1)}, bf16[256,1024]{1,0:T(8,128)(2,1)S(1)}, u32[]{:S(2)}, u32[]{:S(2)}) collective-permute-start(bf16[256,1024]{1,0:T(8,128)(2,1)S(1)} %bitcast.88), channel_id=1, source_target_pairs={{0,8},{8,0},{1,9},{9,1},{2,10},{10,2},{3,11},{11,3},{4,12},{12,4},... | collective-permute-start | bytes 1572872 | tf_op jit(solution)/shard_map/ppermute | solution.py:37
  135.4 4.8 %collective-permute-start.20 = (bf16[64,512]{1,0:T(8,128)(2,1)S(1)}, bf16[64,512]{1,0:T(8,128)(2,1)S(1)}, u32[]{:S(2)}, u32[]{:S(2)}) collective-permute-start(bf16[64,512]{1,0:T(8,128)(2,1)S(1)} %slice.98), channel_id=1, source_target_pairs={{0,1},{1,2},{2,3},{3,4},{4,5},{5,6},{6,7},{7,0},{8,9},{9,10},{10,1... | collective-permute-start | bytes 196616 | tf_op jit(solution)/shard_map/ppermute | solution.py:41
  135.5 3.8 %collective-permute-start.21 = (bf16[48,512]{1,0:T(8,128)(2,1)S(1)}, bf16[48,512]{1,0:T(8,128)(2,1)S(1)}, u32[]{:S(2)}, u32[]{:S(2)}) collective-permute-start(bf16[48,512]{1,0:T(8,128)(2,1)S(1)} %slice.99), channel_id=1, source_target_pairs={{0,7},{1,0},{2,1},{3,2},{4,3},{5,4},{6,5},{7,6},{8,15},{9,8},{10,9... | collective-permute-start | bytes 147464 | tf_op jit(solution)/shard_map/ppermute | solution.py:41
  140.2 2.0 %copy-start.2 = (f32[896,1024]{1,0:T(8,128)S(1)}, f32[896,1024]{1,0:T(8,128)}, u32[]{:S(2)}) copy-start(f32[896,1024]{1,0:T(8,128)} %refs_12_.1) | copy-start | bytes 11010052
  142.3 0.9 copy-start.7
  143.2 0.9 copy-start.9

commit v5 on v4

--- a/solution.py
+++ b/solution.py
@@ -39,6 +39,10 @@
 
 def shift_z(array, d):
     return lax.ppermute(array, "gc", [(i, (i + d) % 8) for i in range(8)])
+
+
+def swap_z(array, k):
+    return lax.ppermute(array, "gc", [(i, i ^ k) for i in range(8)])
 
 
 def exchange(array, axes):
@@ -133,12 +137,11 @@
     )(pos, *own, *far, *error, wh)
 
 
-def choose(first_ref, arrived_ref, out_ref):
-    total = jnp.sum(arrived_ref[:, :, 128:].astype(F32), axis=0).astype(BF16)
+def choose(first_ref, arrived_ref, out_ref, total_ref):
     for k in range(8):
         for p in range(3):
             out_ref[k, :, p * 128 : (p + 1) * 128] = arrived_ref[first_ref[k] + p, :, :128]
-        out_ref[k, :, 384:] = total
+    total_ref[...] = jnp.sum(arrived_ref[:, :, 128:].astype(F32), axis=0)
 
 
 def choose_call(first, arrived):
@@ -148,31 +151,32 @@
             num_scalar_prefetch=1,
             grid=(1,),
             in_specs=[pl.BlockSpec((32, 16, 640), lambda i, first: (0, 0, 0))],
-            out_specs=pl.BlockSpec((8, 16, 896), lambda i, first: (0, 0, 0)),
-        ),
-        out_shape=jax.ShapeDtypeStruct((8, 16, 896), BF16),
+            out_specs=(
+                pl.BlockSpec((8, 16, 384), lambda i, first: (0, 0, 0)),
+                pl.BlockSpec((16, 512), lambda i, first: (0, 0)),
+            ),
+        ),
+        out_shape=(
+            jax.ShapeDtypeStruct((8, 16, 384), BF16),
+            jax.ShapeDtypeStruct((16, 512), F32),
+        ),
         compiler_params=pltpu.CompilerParams(vmem_limit_bytes=6 << 20),
         name="choose",
     )(first, arrived)
 
 
-def assemble(n, shift_ref, y_ref, chunk_ref, total_ref, line_ref):
+def assemble(n, shift_ref, y_ref, chunk_ref, line_ref):
     for p in range(3):
         for z in range(8):
             line_ref[:, pl.ds((p * 8 + z) * n, n)] = y_ref[z, :, p * 128 : p * 128 + n].astype(F32)
     width = chunk_ref.shape[2]
-    d, c = shift_ref[0], shift_ref[1]
+    d = shift_ref[0]
     base = pl.multiple_of((d // 128) * 128, 128)
     near = line_ref[:, pl.ds(base, width + 128)]
     turned = pltpu.roll(near, width + 128 - (d - base), 1)
     chunk = turned[:, :width].astype(BF16)
     for k in range(chunk_ref.shape[0]):
         chunk_ref[k] = chunk
-    high, low = split_bf16(jnp.sum(y_ref[:, :, 384:].astype(F32), axis=0))
-    for half in range(2):
-        at = pl.ds(pl.multiple_of((half ^ c) * 256, 256), 256)
-        total_ref[:16, at] = high[:, half * 256 : (half + 1) * 256]
-        total_ref[16:, at] = low[:, half * 256 : (half + 1) * 256]
 
 
 def assemble_call(pieces, shift, width, n):
@@ -181,12 +185,9 @@
 
     return pl.pallas_call(
         kernel,
-        out_shape=(
-            jax.ShapeDtypeStruct((16, 16, width), BF16),
-            jax.ShapeDtypeStruct((32, 512), BF16),
-        ),
+        out_shape=jax.ShapeDtypeStruct((16, 16, width), BF16),
         in_specs=[SMEM, VMEM],
-        out_specs=(VMEM, VMEM),
+        out_specs=VMEM,
         scratch_shapes=[pltpu.VMEM((16, 24 * n), F32)],
         compiler_params=pltpu.CompilerParams(vmem_limit_bytes=6 << 20),
         name="assemble",
@@ -209,9 +210,12 @@
     gram = jnp.dot(panel_ref[:, :256], near[...], preferred_element_type=F32)
     gram += jnp.dot(panel_ref[:, 256:], far[...], preferred_element_type=F32)
     new_ref[...] = slab_ref[...] + gram * scale
-    added = jnp.dot(total_ref[:, :256], near[...], preferred_element_type=F32)
-    added += jnp.dot(total_ref[:, 256:], far[...], preferred_element_type=F32)
-    grad_ref[...] = wh_ref[...] + (added[:16] + added[16:]) * scale
+    added = jnp.zeros_like(grad_ref)
+    for half, rows in ((pos_ref[3], near), (1 - pos_ref[3], far)):
+        part = total_ref[:, pl.ds(pl.multiple_of(half * 256, 256), 256)]
+        for term in split_bf16(part):
+            added += jnp.dot(term, rows[...], preferred_element_type=F32)
+    grad_ref[...] = wh_ref[...] + added * scale
 
 
 def slab_call(pos, count, pieces, near, far, total, wh, slab):
@@ -290,11 +294,11 @@
     weights = weights_call(pos, gate_t, up_t, far_w.reshape(2, 2, n, quarter))
     sb = jnp.concatenate([b1, b3], 0)
     s3b = plane_permute(sb, 1, 3)
-    s1b = plane_permute(sb, 1, 1)
     sa = jnp.concatenate([b0, b2], 0)
     s1a = plane_permute(sa, 1, 1)
     s3a = plane_permute(sa, 1, 3)
     s2b = plane_permute(s3b, 1, 1)
+    s1b = plane_permute(sb, 1, 1)
     s2a = plane_permute(s1a, 1, 3)
     wh_far = core_swap(wh_sent)
     wh = (wh_own + wh_far).astype(BF16)
@@ -314,17 +318,21 @@
     f3, g3 = shift_z(f2, 1), shift_z(g2, -1)
     panel_width = 8 * n
     starts = slab_offset[0] + jnp.arange(8, dtype=jnp.int32) * width
-    wanted = choose_call(jnp.minimum(starts // panel_width, 29), arrived)
+    wanted, total = choose_call(jnp.minimum(starts // panel_width, 29), arrived)
     pieces = exchange(wanted, "gc")
     sums = jnp.sum(arrived[:, :, 640:].reshape(16, 2, 16, half).astype(F32), axis=0)
     wh = jnp.concatenate([sums[0], sums[1]], 1)
-    pieces, f3, g3, wh = lax.optimization_barrier((pieces, f3, g3, wh))
+    total += swap_z(total, 1)
+    total += swap_z(total, 2)
+    pieces, f3, g3, wh, total = lax.optimization_barrier((pieces, f3, g3, wh, total))
+    total += swap_z(total, 4)
     f4, g4 = shift_z(f3[:64], 1), shift_z(g3[64:], -1)
     h4 = jnp.concatenate([f4, g4], 0)
     start = slab_offset[0] + z * width
     shift = start - jnp.minimum(start // panel_width, 29) * panel_width
-    chunk, total = assemble_call(pieces, jnp.stack([shift, c]).astype(jnp.int32), width, n)
+    chunk = assemble_call(pieces, shift.reshape(1).astype(jnp.int32), width, n)
     near = exchange(chunk, PLANE).reshape(256, width)
+    near, h4, total = lax.optimization_barrier((near, h4, total))
     return slab_call(
         pos, token_count, (hidden_t, f1, g1, f2, g2, f3, g3, h4), near, core_swap(near), total, wh, hessian_slab
     )

time: 149 us -> 145 us (0.973)
  blocking collectives: 12.7 us -> 0 us
  starting transfers between devices: 45 us -> 56.7 us
  waiting for transfers between devices: 46.5 us -> 44.6 us
    all_to_all x1 -> x0, blocking collectives: 12.7 us -> none  [exchange(): return lax.all_to_all(array, axes, split_axis=0, concat_axis=0, tiled=True)]
    all_to_all x3 -> x4, waiting for transfers between devices: 23.6 us -> 13.1 us  [exchange(): return lax.all_to_all(array, axes, split_axis=0, concat_axis=0, tiled=True)]
    ppermute x0 -> x3, waiting for transfers between devices: none -> 9.02 us  [swap_z(): return lax.ppermute(array, 'gc', [(i, i ^ k) for i in range(8)])]
    ppermute x0 -> x3, starting transfers between devices: none -> 7.07 us  [swap_z(): return lax.ppermute(array, 'gc', [(i, i ^ k) for i in range(8)])]
    all_to_all x3 -> x4, starting transfers between devices: 16.2 us -> 19.7 us  [exchange(): return lax.all_to_all(array, axes, split_axis=0, concat_axis=0, tiled=True)]
    unnamed x22 -> x24, local copies, waits for them, and re-layouts: 8.54 us -> 9.18 us
  transfers between devices with their start and end apart: 26 -> 30, of which waited for: 14 -> 15; matrix products, arithmetic and copies ran while one was open for 12% -> 11% of each run, Pallas kernels for 2% -> 2%
where the time goes in v5:
time: 145 us; the launch traced here: 144 us
  starting transfers between devices  56.7 us (39%)
  waiting for transfers between devices  44.6 us (31%)
  matrix products  14.2 us (10%)
  local copies, waits for them, and re-layouts  13.6 us (9%)
  Pallas kernels  9.63 us (7%)
  other arithmetic  2.65 us (2%)
  between operations  2.41 us (2%)
    all_to_all x4, starting transfers between devices, exchange(): return lax.all_to_all(array, axes, split_axis=0, concat_axis=0, tiled=True)  19.7 us
    ppermute x9, waiting for transfers between devices, plane_permute(): return lax.ppermute(array, CAL_GR, pairs)  13.7 us
    all_to_all x4, waiting for transfers between devices, exchange(): return lax.all_to_all(array, axes, split_axis=0, concat_axis=0, tiled=True)  13.1 us
    ppermute x9, starting transfers between devices, plane_permute(): return lax.ppermute(array, CAL_GR, pairs)  10.7 us
    ppermute x6, starting transfers between devices, core_swap(): return lax.ppermute(array, 'gr_2', [(0, 1), (1, 0)])  10.6 us
    unnamed x24, local copies, waits for them, and re-layouts  9.18 us
    ppermute x3, waiting for transfers between devices, swap_z(): return lax.ppermute(array, 'gc', [(i, i ^ k) for i in range(8)])  9.02 us
    ppermute x8, starting transfers between devices, shift_z(): return lax.ppermute(array, 'gc', [(i, (i + d) % 8) for i in range(8)])  8.66 us
  transfers between devices with their start and end apart: 30, of which 15 were waited for; matrix products, arithmetic and copies ran while one was open for 11% of the time, Pallas kernels for 2%

profile of v5, /device:TPU:1, one launch (start us, length us, event | category | flops | bytes accessed | tf_op | source)
XLA Modules:
  0.0 143.8 jit_solution(1898887374562277756)
XLA Ops:
  0.7 0.9 constant_dynamic-slice_fusion.1
  1.5 3.2 %collective-permute-start = (bf16[4,2048]{1,0:T(4,128)(2,1)S(1)}, bf16[4,2048]{1,0:T(4,128)(2,1)S(1)}, u32[]{:S(2)}, u32[]{:S(2)}) collective-permute-start(bf16[4,2048]{1,0:T(4,128)(2,1)S(1)} %constant_dynamic-slice_fusion.1), channel_id=1, source_target_pairs={{0,8},{8,0},{1,9},{9,1},{2,10},{10,2},{3,11},{11,3},{4,12},{12,4},... | collective-permute-start | bytes 49160 | tf_op jit(solution)/shard_map/ppermute | solution.py:37
  4.7 0.8 collective-permute-done
  5.6 0.7 broadcast_select_fusion.1
  6.3 0.7 broadcast_in_dim.2
  7.0 1.6 %dynamic-slice_bitcast_fusion.14 = (bf16[1,112,2048]{2,1,0:T(8,128)(2,1)S(1)}, bf16[1,112,2048]{2,1,0:T(8,128)(2,1)S(1)}, bf16[1,112,2048]{2,1,0:T(8,128)(2,1)S(1)}, bf16[1,112,2048]{2,1,0:T(8,128)(2,1)S(1)}) fusion(bf16[8192,112]{0,1:T(8,128)(2,1)} %param.9, s32[]{:T(128)S(6)} %select_n.61, s32[]{:T(128)S(6)} %select_n.62, bf16[8192,112]{0,1:T(8,128)(2,1)} %param.8), kind=kLoop, calls=%fused_computation.33 | loop fusion | bytes 3670024 | tf_op jit(solution)/shard_map/stack | solution.py:267
  8.6 1.5 %pad_maximum_fusion = bf16[4,112,2048]{2,1,0:T(8,128)(2,1)} fusion(bf16[1,112,2048]{2,1,0:T(8,128)(2,1)S(1)} %get-tuple-element.55, bf16[1,112,2048]{2,1,0:T(8,128)(2,1)S(1)} %get-tuple-element.60, bf16[1,112,2048]{2,1,0:T(8,128)(2,1)S(1)} %get-tuple-element.54, bf16[1,112,2048]{2,1,0:T(8,128)(2,1)S(1)} %get-tuple-element.61), kind=kLoop, calls=%fused_computation | loop fusion | flops 2752512 | bytes 3670016 | tf_op jit(solution)/shard_map/stack | solution.py:267
  10.4 6.5 %all-to-all-start = ((bf16[8,8,2048]{2,1,0:T(8,128)(2,1)}), bf16[8,8,2048]{2,1,0:T(8,128)(2,1)S(1)}, u32[]{:S(2)}, u32[]{:S(2)}) async-start(bf16[8,8,2048]{2,1,0:T(8,128)(2,1)} %broadcast_in_dim.2), calls=%async_computation | async-start | bytes 524288 | tf_op jit(solution)/shard_map/all_to_all | solution.py:49
  17.0 4.5 %fusion = f32[512,512]{1,0:T(8,128)} fusion(f32[512,896]{1,0:T(8,128)S(1)} %copy-done, f32[896,1024]{1,0:T(8,128)} %refs_12_.1, s32[]{:T(128)S(6)} %select_n.60), kind=kOutput, calls=%fused_computation.1 | convolution fusion | flops 1409286144 | bytes 4718596 | tf_op jit(solution)/shard_map/dot_general | solution.py:279
  21.6 1.9 %fusion.2 = f32[512,512]{1,0:T(8,128)S(1)} fusion(f32[512,896]{1,0:T(8,128)S(1)} %copy-done, f32[896,1024]{1,0:T(8,128)S(1)} %copy-done.1, s32[]{:T(128)S(6)} %select_n.59), kind=kOutput, calls=%fused_computation.3 | convolution fusion | flops 1409286144 | bytes 4718596 | tf_op jit(solution)/shard_map/dot_general | solution.py:279
  23.5 5.6 %all-to-all-done = bf16[8,8,2048]{2,1,0:T(8,128)(2,1)S(1)} async-done(((bf16[8,8,2048]{2,1,0:T(8,128)(2,1)}), bf16[8,8,2048]{2,1,0:T(8,128)(2,1)S(1)}, u32[]{:S(2)}, u32[]{:S(2)}) %all-to-all-start) | async-done | bytes 262176 | tf_op jit(solution)/shard_map/all_to_all | solution.py:49
  29.1 2.9 %collective-permute-start.2 = (bf16[64,2048]{1,0:T(8,128)(2,1)S(1)}, bf16[64,2048]{1,0:T(8,128)(2,1)}, u32[]{:S(2)}, u32[]{:S(2)}) collective-permute-start(bf16[64,2048]{1,0:T(8,128)(2,1)S(1)} %bitcast.91), channel_id=1, source_target_pairs={{0,64},{8,40},{16,80},{24,56},{32,96},{40,8},{48,112},{56,24},{128... | collective-permute-start | bytes 786440 | tf_op jit(solution)/shard_map/ppermute | solution.py:33
  32.1 0.8 collective-permute-start.4
  32.9 1.2 collective-permute-start.13
  34.1 1.5 %copy-done.3 = bf16[8192,112]{0,1:T(8,128)(2,1)S(1)} copy-done((bf16[8192,112]{0,1:T(8,128)(2,1)S(1)}, bf16[8192,112]{0,1:T(8,128)(2,1)}, u32[]{:S(2)}) %copy-start.3) | copy-done | bytes 1835032
  35.6 1.5 %copy-done.4 = bf16[8192,112]{0,1:T(8,128)(2,1)S(1)} copy-done((bf16[8192,112]{0,1:T(8,128)(2,1)S(1)}, bf16[8192,112]{0,1:T(8,128)(2,1)}, u32[]{:S(2)}) %copy-start.4) | copy-done | bytes 1835032
  37.1 2.3 %weights.1 = bf16[2,512,2048]{2,1,0:T(8,128)(2,1)S(1)} custom-call(s32[5]{0:T(128)S(1)} %stack.38.pos_ref, bf16[112,8192]{1,0:T(8,128)(2,1)S(1)} %bitcast.86, bf16[112,8192]{1,0:T(8,128)(2,1)S(1)} %bitcast.87, bf16[2,2,112,2048]{3,2,1,0:T(8,128)(2,1)} %bitcast.16.far), custom_call_target="tpu_custom_call" | custom-call | tf_op jit(solution)/shard_map/weights/pallas_call | solution.py:70
  39.4 1.0 constant_dynamic-update-slice_fusion
  40.4 1.9 %collective-permute-start.7 = (bf16[128,2048]{1,0:T(8,128)(2,1)S(1)}, bf16[128,2048]{1,0:T(8,128)(2,1)S(1)}, u32[]{:S(2)}, u32[]{:S(2)}) collective-permute-start(bf16[128,2048]{1,0:T(8,128)(2,1)S(1)} %constant_dynamic-update-slice_fusion), channel_id=1, source_target_pairs={{0,48},{8,200},{16,32},{24,216},{32,16},{40,232},{48,0},{56,248},{... | collective-permute-start | bytes 1572872 | tf_op jit(solution)/shard_map/ppermute | solution.py:33
  42.3 1.1 collective-permute-start.5
  43.5 0.9 collective-permute-start.8
  45.4 0.5 fusion.10.refs_1_
  45.9 0.5 convolution_dynamic-update-slice_fusion.4
  46.4 4.2 %collective-permute-done.5 = bf16[128,2048]{1,0:T(8,128)(2,1)S(1)} collective-permute-done((bf16[128,2048]{1,0:T(8,128)(2,1)S(1)}, bf16[128,2048]{1,0:T(8,128)(2,1)S(1)}, u32[]{:S(2)}, u32[]{:S(2)}) %collective-permute-start.5) | collective-permute-done | bytes 524320 | tf_op jit(solution)/shard_map/ppermute | solution.py:33
  50.6 0.5 convolution_dynamic-update-slice_fusion.3
  51.1 5.1 %collective-permute-done.6 = bf16[128,2048]{1,0:T(8,128)(2,1)S(1)} collective-permute-done((bf16[128,2048]{1,0:T(8,128)(2,1)S(1)}, bf16[128,2048]{1,0:T(8,128)(2,1)S(1)}, u32[]{:S(2)}, u32[]{:S(2)}) %collective-permute-start.6) | collective-permute-done | bytes 524320 | tf_op jit(solution)/shard_map/ppermute | solution.py:33
  56.7 0.5 convolution_dynamic-update-slice_fusion.1
  57.7 2.2 %collective-permute-start.11 = (f32[768,256]{1,0:T(8,128)S(1)}, f32[768,256]{1,0:T(8,128)S(1)}, u32[]{:S(2)}, u32[]{:S(2)}) collective-permute-start(f32[768,256]{1,0:T(8,128)S(1)} %convolution_dynamic-update-slice_fusion), channel_id=1, source_target_pairs={{0,8},{8,0},{1,9},{9,1},{2,10},{10,2},{3,11},{11,3},{4,12},{12,4},... | collective-permute-start | bytes 2359304 | tf_op jit(solution)/shard_map/ppermute | solution.py:37
  59.9 1.8 %collective-permute-start.9 = (bf16[128,2048]{1,0:T(8,128)(2,1)S(1)}, bf16[128,2048]{1,0:T(8,128)(2,1)S(1)}, u32[]{:S(2)}, u32[]{:S(2)}) collective-permute-start(bf16[128,2048]{1,0:T(8,128)(2,1)S(1)} %collective-permute-done.5), channel_id=1, source_target_pairs={{0,48},{8,200},{16,32},{24,216},{32,16},{40,232},{48,0},{56,248},{... | collective-permute-start | bytes 1572872 | tf_op jit(solution)/shard_map/ppermute | solution.py:33
  61.7 1.1 collective-permute-start.10
  62.8 0.5 fusion.11.refs_4_
  64.3 0.5 fusion.12.refs_2_
  65.1 4.3 %collective-permute-done.9 = bf16[128,2048]{1,0:T(8,128)(2,1)S(1)} collective-permute-done((bf16[128,2048]{1,0:T(8,128)(2,1)S(1)}, bf16[128,2048]{1,0:T(8,128)(2,1)S(1)}, u32[]{:S(2)}, u32[]{:S(2)}) %collective-permute-start.9) | collective-permute-done | bytes 524320 | tf_op jit(solution)/shard_map/ppermute | solution.py:33
  70.0 0.5 fusion.13
  70.5 1.0 collective-permute-start.12
  72.7 1.3 activate.1
  74.0 1.0 copy-done.5
  75.0 6.3 %all-to-all-start.1 = ((bf16[32,16,1152]{2,1,0:T(8,128)(2,1)}), bf16[32,16,1152]{2,1,0:T(8,128)(2,1)S(1)}, u32[]{:S(2)}, u32[]{:S(2)}) async-start(bf16[32,16,1152]{2,1,0:T(8,128)(2,1)} %copy-done.5), calls=%async_computation.1 | async-start | bytes 2359296 | tf_op jit(solution)/shard_map/all_to_all | solution.py:49
  81.4 1.5 %collective-permute-start.14 = (bf16[112,512]{1,0:T(8,128)(2,1)S(1)}, bf16[112,512]{1,0:T(8,128)(2,1)S(1)}, u32[]{:S(2)}, u32[]{:S(2)}) collective-permute-start(bf16[112,512]{1,0:T(8,128)(2,1)S(1)} %get-tuple-element.37.refs_0_), channel_id=1, source_target_pairs={{0,1},{1,2},{2,3},{3,4},{4,5},{5,6},{6,7},{7,0},{8,9},{9,10},{10,1... | collective-permute-start | bytes 344072 | tf_op jit(solution)/shard_map/ppermute | solution.py:41
  82.8 3.0 %collective-permute-done.15.refs_2_ = bf16[112,512]{1,0:T(8,128)(2,1)S(1)} collective-permute-done((bf16[112,512]{1,0:T(8,128)(2,1)S(1)}, bf16[112,512]{1,0:T(8,128)(2,1)S(1)}, u32[]{:S(2)}, u32[]{:S(2)}) %collective-permute-start.15) | collective-permute-done | bytes 114720 | tf_op jit(solution)/shard_map/ppermute | solution.py:41
  85.8 1.5 %collective-permute-start.17 = (bf16[112,512]{1,0:T(8,128)(2,1)S(1)}, bf16[112,512]{1,0:T(8,128)(2,1)S(1)}, u32[]{:S(2)}, u32[]{:S(2)}) collective-permute-start(bf16[112,512]{1,0:T(8,128)(2,1)S(1)} %collective-permute-done.15.refs_2_), channel_id=1, source_target_pairs={{0,7},{1,0},{2,1},{3,2},{4,3},{5,4},{6,5},{7,6},{8,15},{9,8},{10,9... | collective-permute-start | bytes 344072 | tf_op jit(solution)/shard_map/ppermute | solution.py:41
  87.4 0.6 copy-done.6
  88.7 1.1 collective-permute-done.17.refs_4_
  89.8 2.7 %collective-permute-done.16.refs_3_ = bf16[112,512]{1,0:T(8,128)(2,1)} collective-permute-done((bf16[112,512]{1,0:T(8,128)(2,1)S(1)}, bf16[112,512]{1,0:T(8,128)(2,1)}, u32[]{:S(2)}, u32[]{:S(2)}) %collective-permute-start.16) | collective-permute-done | bytes 114720 | tf_op jit(solution)/shard_map/ppermute | solution.py:41
  92.5 7.5 %all-to-all-done.1.arrived_ref = bf16[32,16,1152]{2,1,0:T(8,128)(2,1)S(1)} async-done(((bf16[32,16,1152]{2,1,0:T(8,128)(2,1)}), bf16[32,16,1152]{2,1,0:T(8,128)(2,1)S(1)}, u32[]{:S(2)}, u32[]{:S(2)}) %all-to-all-start.1) | async-done | bytes 1179680 | tf_op jit(solution)/shard_map/all_to_all | solution.py:49
  100.3 2.4 %collective-permute-start.19 = (bf16[112,512]{1,0:T(8,128)(2,1)}, bf16[112,512]{1,0:T(8,128)(2,1)S(1)}, u32[]{:S(2)}, u32[]{:S(2)}) collective-permute-start(bf16[112,512]{1,0:T(8,128)(2,1)} %copy-done.8), channel_id=1, source_target_pairs={{0,7},{1,0},{2,1},{3,2},{4,3},{5,4},{6,5},{7,6},{8,15},{9,8},{10,9... | collective-permute-start | bytes 344072 | tf_op jit(solution)/shard_map/ppermute | solution.py:41
  102.7 0.7 choose.1
  103.5 0.6 copy-done.10
  104.2 3.4 %all-to-all-start.2 = ((bf16[8,16,384]{2,1,0:T(8,128)(2,1)}), bf16[8,16,384]{2,1,0:T(8,128)(2,1)S(1)}, u32[]{:S(2)}, u32[]{:S(2)}) async-start(bf16[8,16,384]{2,1,0:T(8,128)(2,1)} %copy-done.10), calls=%async_computation.2 | async-start | bytes 196608 | tf_op jit(solution)/shard_map/all_to_all | solution.py:49
  107.6 1.4 collective-permute-start.20
  108.9 3.4 %collective-permute-done.20 = f32[16,512]{1,0:T(8,128)S(1)} collective-permute-done((f32[16,512]{1,0:T(8,128)S(1)}, f32[16,512]{1,0:T(8,128)S(1)}, u32[]{:S(2)}, u32[]{:S(2)}) %collective-permute-start.20) | collective-permute-done | bytes 32800 | tf_op jit(solution)/shard_map/ppermute | solution.py:45
  112.4 1.6 %collective-permute-start.21 = (f32[16,512]{1,0:T(8,128)S(1)}, f32[16,512]{1,0:T(8,128)S(1)}, u32[]{:S(2)}, u32[]{:S(2)}) collective-permute-start(f32[16,512]{1,0:T(8,128)S(1)} %add.67), channel_id=1, source_target_pairs={{0,2},{1,3},{2,0},{3,1},{4,6},{5,7},{6,4},{7,5},{8,10},{9,11},{10,... | collective-permute-start | bytes 98312 | tf_op jit(solution)/shard_map/ppermute | solution.py:45
  113.9 2.6 %collective-permute-done.21 = f32[16,512]{1,0:T(8,128)S(1)} collective-permute-done((f32[16,512]{1,0:T(8,128)S(1)}, f32[16,512]{1,0:T(8,128)S(1)}, u32[]{:S(2)}, u32[]{:S(2)}) %collective-permute-start.21) | collective-permute-done | bytes 32800 | tf_op jit(solution)/shard_map/ppermute | solution.py:45
  116.5 1.0 assemble.1
  117.5 3.6 %all-to-all-start.3 = ((bf16[16,16,1024]{2,1,0:T(8,128)(2,1)}), bf16[16,16,1024]{2,1,0:T(8,128)(2,1)S(1)}, u32[]{:S(2)}, u32[]{:S(2)}) async-start(bf16[16,16,1024]{2,1,0:T(8,128)(2,1)} %assemble.1), calls=%async_computation.3 | async-start | bytes 1048576 | tf_op jit(solution)/shard_map/all_to_all | solution.py:49
  121.5 2.6 %collective-permute-start.23 = (bf16[48,512]{1,0:T(8,128)(2,1)S(1)}, bf16[48,512]{1,0:T(8,128)(2,1)S(1)}, u32[]{:S(2)}, u32[]{:S(2)}) collective-permute-start(bf16[48,512]{1,0:T(8,128)(2,1)S(1)} %slice.99), channel_id=1, source_target_pairs={{0,7},{1,0},{2,1},{3,2},{4,3},{5,4},{6,5},{7,6},{8,15},{9,8},{10,9... | collective-permute-start | bytes 147464 | tf_op jit(solution)/shard_map/ppermute | solution.py:41
  124.1 4.1 %collective-permute-start.24 = (f32[16,512]{1,0:T(8,128)S(1)}, f32[16,512]{1,0:T(8,128)S(1)}, u32[]{:S(2)}, u32[]{:S(2)}) collective-permute-start(f32[16,512]{1,0:T(8,128)S(1)} %add.68), channel_id=1, source_target_pairs={{0,4},{1,5},{2,6},{3,7},{4,0},{5,1},{6,2},{7,3},{8,12},{9,13},{10,... | collective-permute-start | bytes 98312 | tf_op jit(solution)/shard_map/ppermute | solution.py:45
  128.2 3.0 %collective-permute-done.24 = f32[16,512]{1,0:T(8,128)S(1)} collective-permute-done((f32[16,512]{1,0:T(8,128)S(1)}, f32[16,512]{1,0:T(8,128)S(1)}, u32[]{:S(2)}, u32[]{:S(2)}) %collective-permute-start.24) | collective-permute-done | bytes 32800 | tf_op jit(solution)/shard_map/ppermute | solution.py:45
  131.3 2.7 %collective-permute-start.25 = (bf16[256,1024]{1,0:T(8,128)(2,1)S(1)}, bf16[256,1024]{1,0:T(8,128)(2,1)S(1)}, u32[]{:S(2)}, u32[]{:S(2)}) collective-permute-start(bf16[256,1024]{1,0:T(8,128)(2,1)S(1)} %bitcast.88), channel_id=1, source_target_pairs={{0,8},{8,0},{1,9},{9,1},{2,10},{10,2},{3,11},{11,3},{4,12},{12,4},... | collective-permute-start | bytes 1572872 | tf_op jit(solution)/shard_map/ppermute | solution.py:37
  134.7 0.9 collective-permute-done.25.refs_9_
  135.6 2.0 %copy-done.2 = f32[896,1024]{1,0:T(8,128)S(1)} copy-done((f32[896,1024]{1,0:T(8,128)S(1)}, f32[896,1024]{1,0:T(8,128)}, u32[]{:S(2)}) %copy-start.2) | copy-done | bytes 3670040
  137.6 0.9 copy-done.7
  138.5 0.9 copy-done.9
  139.4 4.3 %slab.1 = (f32[896,1024]{1,0:T(8,128)}, f32[16,1024]{1,0:T(8,128)}) custom-call(s32[5]{0:T(128)S(1)} %stack.38.pos_ref, s32[1]{0:T(128)S(6)} %copy.17.count_ref, bf16[112,512]{1,0:T(8,128)(2,1)S(1)} %get-tuple-element.37.refs_0_, bf16[112,512]{1,0:T(8,128)(2,1)S(1)} %copy-done.7, bf16[112,512]{1,0:T(8,128)(2,1)S(1)} %collective-permute-done.15.refs_2_, ...), custom_call_target="tpu_custom_call" | custom-call | tf_op jit(solution)/shard_map/slab/pallas_call | solution.py:231
  (68 shorter events, 6.6 us)
Async XLA Ops:
  0.6 16.2 %copy-start = (f32[512,896]{1,0:T(8,128)S(1)}, f32[512,896]{1,0:T(8,128)}, u32[]{:S(2)}) copy-start(f32[512,896]{1,0:T(8,128)} %param.11) | copy-start | bytes 5505028
  1.5 4.0 %collective-permute-start = (bf16[4,2048]{1,0:T(4,128)(2,1)S(1)}, bf16[4,2048]{1,0:T(4,128)(2,1)S(1)}, u32[]{:S(2)}, u32[]{:S(2)}) collective-permute-start(bf16[4,2048]{1,0:T(4,128)(2,1)S(1)} %constant_dynamic-slice_fusion.1), channel_id=1, source_target_pairs={{0,8},{8,0},{1,9},{9,1},{2,10},{10,2},{3,11},{11,3},{4,12},{12,4},... | collective-permute-start | bytes 49160 | tf_op jit(solution)/shard_map/ppermute | solution.py:37
  10.1 19.1 %collective-permute-start.1 = (bf16[4,112,2048]{2,1,0:T(8,128)(2,1)}, bf16[4,112,2048]{2,1,0:T(8,128)(2,1)}, u32[]{:S(2)}, u32[]{:S(2)}) collective-permute-start(bf16[4,112,2048]{2,1,0:T(8,128)(2,1)} %pad_maximum_fusion), channel_id=1, source_target_pairs={{0,8},{8,0},{1,9},{9,1},{2,10},{10,2},{3,11},{11,3},{4,12},{12,4},... | collective-permute-start | bytes 5505032 | tf_op jit(solution)/shard_map/ppermute | solution.py:37
  10.4 18.7 %all-to-all-start = ((bf16[8,8,2048]{2,1,0:T(8,128)(2,1)}), bf16[8,8,2048]{2,1,0:T(8,128)(2,1)S(1)}, u32[]{:S(2)}, u32[]{:S(2)}) async-start(bf16[8,8,2048]{2,1,0:T(8,128)(2,1)} %broadcast_in_dim.2), calls=%async_computation | async-start | bytes 524288 | tf_op jit(solution)/shard_map/all_to_all | solution.py:49
  16.9 4.7 %copy-start.1 = (f32[896,1024]{1,0:T(8,128)S(1)}, f32[896,1024]{1,0:T(8,128)}, u32[]{:S(2)}) copy-start(f32[896,1024]{1,0:T(8,128)} %refs_12_.1) | copy-start | bytes 11010052
  29.1 10.3 %collective-permute-start.2 = (bf16[64,2048]{1,0:T(8,128)(2,1)S(1)}, bf16[64,2048]{1,0:T(8,128)(2,1)}, u32[]{:S(2)}, u32[]{:S(2)}) collective-permute-start(bf16[64,2048]{1,0:T(8,128)(2,1)S(1)} %bitcast.91), channel_id=1, source_target_pairs={{0,64},{8,40},{16,80},{24,56},{32,96},{40,8},{48,112},{56,24},{128... | collective-permute-start | bytes 786440 | tf_op jit(solution)/shard_map/ppermute | solution.py:33
  32.1 11.3 %collective-permute-start.4 = (bf16[64,2048]{1,0:T(8,128)(2,1)S(1)}, bf16[64,2048]{1,0:T(8,128)(2,1)S(1)}, u32[]{:S(2)}, u32[]{:S(2)}) collective-permute-start(bf16[64,2048]{1,0:T(8,128)(2,1)S(1)} %bitcast.92), channel_id=1, source_target_pairs={{0,192},{8,56},{16,208},{24,40},{32,224},{40,24},{48,240},{56,8},{... | collective-permute-start | bytes 786440 | tf_op jit(solution)/shard_map/ppermute | solution.py:33
  32.9 10.5 %collective-permute-start.3 = (bf16[64,2048]{1,0:T(8,128)(2,1)S(1)}, bf16[64,2048]{1,0:T(8,128)(2,1)S(1)}, u32[]{:S(2)}, u32[]{:S(2)}) collective-permute-start(bf16[64,2048]{1,0:T(8,128)(2,1)S(1)} %bitcast.93), channel_id=1, source_target_pairs={{0,128},{8,24},{16,144},{24,8},{32,160},{40,56},{48,176},{56,40},{... | collective-permute-start | bytes 786440 | tf_op jit(solution)/shard_map/ppermute | solution.py:33
  32.9 31.9 %collective-permute-start.13 = (f32[512,512]{1,0:T(8,128)}, f32[512,512]{1,0:T(8,128)S(1)}, u32[]{:S(2)}, u32[]{:S(2)}) collective-permute-start(f32[512,512]{1,0:T(8,128)} %fusion), channel_id=1, source_target_pairs={{0,8},{8,0},{1,9},{9,1},{2,10},{10,2},{3,11},{11,3},{4,12},{12,4},... | collective-permute-start | bytes 3145736 | tf_op jit(solution)/shard_map/ppermute | solution.py:37
  34.1 1.5 %copy-start.3 = (bf16[8192,112]{0,1:T(8,128)(2,1)S(1)}, bf16[8192,112]{0,1:T(8,128)(2,1)}, u32[]{:S(2)}) copy-start(bf16[8192,112]{0,1:T(8,128)(2,1)} %param.8) | copy-start | bytes 5505028
  35.6 1.5 %copy-start.4 = (bf16[8192,112]{0,1:T(8,128)(2,1)S(1)}, bf16[8192,112]{0,1:T(8,128)(2,1)}, u32[]{:S(2)}) copy-start(bf16[8192,112]{0,1:T(8,128)(2,1)} %param.9) | copy-start | bytes 5505028
  40.4 16.3 %collective-permute-start.7 = (bf16[128,2048]{1,0:T(8,128)(2,1)S(1)}, bf16[128,2048]{1,0:T(8,128)(2,1)S(1)}, u32[]{:S(2)}, u32[]{:S(2)}) collective-permute-start(bf16[128,2048]{1,0:T(8,128)(2,1)S(1)} %constant_dynamic-update-slice_fusion), channel_id=1, source_target_pairs={{0,48},{8,200},{16,32},{24,216},{32,16},{40,232},{48,0},{56,248},{... | collective-permute-start | bytes 1572872 | tf_op jit(solution)/shard_map/ppermute | solution.py:33
  42.3 8.3 %collective-permute-start.5 = (bf16[128,2048]{1,0:T(8,128)(2,1)S(1)}, bf16[128,2048]{1,0:T(8,128)(2,1)S(1)}, u32[]{:S(2)}, u32[]{:S(2)}) collective-permute-start(bf16[128,2048]{1,0:T(8,128)(2,1)S(1)} %constant_dynamic-update-slice_fusion), channel_id=1, source_target_pairs={{0,16},{8,136},{16,0},{24,152},{32,48},{40,168},{48,32},{56,184},{... | collective-permute-start | bytes 1572872 | tf_op jit(solution)/shard_map/ppermute | solution.py:33
  43.5 13.8 %collective-permute-start.8 = (bf16[128,2048]{1,0:T(8,128)(2,1)S(1)}, bf16[128,2048]{1,0:T(8,128)(2,1)S(1)}, u32[]{:S(2)}, u32[]{:S(2)}) collective-permute-start(bf16[128,2048]{1,0:T(8,128)(2,1)S(1)} %constant_dynamic-update-slice_fusion.2), channel_id=1, source_target_pairs={{0,48},{8,200},{16,32},{24,216},{32,16},{40,232},{48,0},{56,248},{... | collective-permute-start | bytes 1572872 | tf_op jit(solution)/shard_map/ppermute | solution.py:33
  44.4 11.8 %collective-permute-start.6 = (bf16[128,2048]{1,0:T(8,128)(2,1)S(1)}, bf16[128,2048]{1,0:T(8,128)(2,1)S(1)}, u32[]{:S(2)}, u32[]{:S(2)}) collective-permute-start(bf16[128,2048]{1,0:T(8,128)(2,1)S(1)} %constant_dynamic-update-slice_fusion.2), channel_id=1, source_target_pairs={{0,16},{8,136},{16,0},{24,152},{32,48},{40,168},{48,32},{56,184},{... | collective-permute-start | bytes 1572872 | tf_op jit(solution)/shard_map/ppermute | solution.py:33
  57.7 14.9 %collective-permute-start.11 = (f32[768,256]{1,0:T(8,128)S(1)}, f32[768,256]{1,0:T(8,128)S(1)}, u32[]{:S(2)}, u32[]{:S(2)}) collective-permute-start(f32[768,256]{1,0:T(8,128)S(1)} %convolution_dynamic-update-slice_fusion), channel_id=1, source_target_pairs={{0,8},{8,0},{1,9},{9,1},{2,10},{10,2},{3,11},{11,3},{4,12},{12,4},... | collective-permute-start | bytes 2359304 | tf_op jit(solution)/shard_map/ppermute | solution.py:37
  59.9 9.5 %collective-permute-start.9 = (bf16[128,2048]{1,0:T(8,128)(2,1)S(1)}, bf16[128,2048]{1,0:T(8,128)(2,1)S(1)}, u32[]{:S(2)}, u32[]{:S(2)}) collective-permute-start(bf16[128,2048]{1,0:T(8,128)(2,1)S(1)} %collective-permute-done.5), channel_id=1, source_target_pairs={{0,48},{8,200},{16,32},{24,216},{32,16},{40,232},{48,0},{56,248},{... | collective-permute-start | bytes 1572872 | tf_op jit(solution)/shard_map/ppermute | solution.py:33
  61.7 8.3 %collective-permute-start.10 = (bf16[128,2048]{1,0:T(8,128)(2,1)S(1)}, bf16[128,2048]{1,0:T(8,128)(2,1)S(1)}, u32[]{:S(2)}, u32[]{:S(2)}) collective-permute-start(bf16[128,2048]{1,0:T(8,128)(2,1)S(1)} %collective-permute-done.8), channel_id=1, source_target_pairs={{0,16},{8,136},{16,0},{24,152},{32,48},{40,168},{48,32},{56,184},{... | collective-permute-start | bytes 1572872 | tf_op jit(solution)/shard_map/ppermute | solution.py:33
  70.5 2.1 %collective-permute-start.12 = (f32[256,256]{1,0:T(8,128)S(1)}, f32[256,256]{1,0:T(8,128)S(1)}, u32[]{:S(2)}, u32[]{:S(2)}) collective-permute-start(f32[256,256]{1,0:T(8,128)S(1)} %pad_maximum_fusion.1), channel_id=1, source_target_pairs={{0,8},{8,0},{1,9},{9,1},{2,10},{10,2},{3,11},{11,3},{4,12},{12,4},... | collective-permute-start | bytes 786440 | tf_op jit(solution)/shard_map/ppermute | solution.py:37
  74.0 1.0 copy-start.5
  75.0 25.0 %all-to-all-start.1 = ((bf16[32,16,1152]{2,1,0:T(8,128)(2,1)}), bf16[32,16,1152]{2,1,0:T(8,128)(2,1)S(1)}, u32[]{:S(2)}, u32[]{:S(2)}) async-start(bf16[32,16,1152]{2,1,0:T(8,128)(2,1)} %copy-done.5), calls=%async_computation.1 | async-start | bytes 2359296 | tf_op jit(solution)/shard_map/all_to_all | solution.py:49
  81.3 4.5 %collective-permute-start.15 = (bf16[112,512]{1,0:T(8,128)(2,1)S(1)}, bf16[112,512]{1,0:T(8,128)(2,1)S(1)}, u32[]{:S(2)}, u32[]{:S(2)}) collective-permute-start(bf16[112,512]{1,0:T(8,128)(2,1)S(1)} %get-tuple-element.37.refs_0_), channel_id=1, source_target_pairs={{0,7},{1,0},{2,1},{3,2},{4,3},{5,4},{6,5},{7,6},{8,15},{9,8},{10,9... | collective-permute-start | bytes 344072 | tf_op jit(solution)/shard_map/ppermute | solution.py:41
  81.4 6.0 %collective-permute-start.14 = (bf16[112,512]{1,0:T(8,128)(2,1)S(1)}, bf16[112,512]{1,0:T(8,128)(2,1)S(1)}, u32[]{:S(2)}, u32[]{:S(2)}) collective-permute-start(bf16[112,512]{1,0:T(8,128)(2,1)S(1)} %get-tuple-element.37.refs_0_), channel_id=1, source_target_pairs={{0,1},{1,2},{2,3},{3,4},{4,5},{5,6},{6,7},{7,0},{8,9},{9,10},{10,1... | collective-permute-start | bytes 344072 | tf_op jit(solution)/shard_map/ppermute | solution.py:41
  85.8 3.9 %collective-permute-start.17 = (bf16[112,512]{1,0:T(8,128)(2,1)S(1)}, bf16[112,512]{1,0:T(8,128)(2,1)S(1)}, u32[]{:S(2)}, u32[]{:S(2)}) collective-permute-start(bf16[112,512]{1,0:T(8,128)(2,1)S(1)} %collective-permute-done.15.refs_2_), channel_id=1, source_target_pairs={{0,7},{1,0},{2,1},{3,2},{4,3},{5,4},{6,5},{7,6},{8,15},{9,8},{10,9... | collective-permute-start | bytes 344072 | tf_op jit(solution)/shard_map/ppermute | solution.py:41
  87.3 5.1 %collective-permute-start.16 = (bf16[112,512]{1,0:T(8,128)(2,1)S(1)}, bf16[112,512]{1,0:T(8,128)(2,1)}, u32[]{:S(2)}, u32[]{:S(2)}) collective-permute-start(bf16[112,512]{1,0:T(8,128)(2,1)S(1)} %collective-permute-done.14.refs_1_), channel_id=1, source_target_pairs={{0,1},{1,2},{2,3},{3,4},{4,5},{5,6},{6,7},{7,0},{8,9},{9,10},{10,1... | collective-permute-start | bytes 344072 | tf_op jit(solution)/shard_map/ppermute | solution.py:41
  87.3 0.7 copy-start.6
  89.8 10.2 %copy-start.8 = (bf16[112,512]{1,0:T(8,128)(2,1)}, bf16[112,512]{1,0:T(8,128)(2,1)S(1)}, u32[]{:S(2)}) copy-start(bf16[112,512]{1,0:T(8,128)(2,1)S(1)} %collective-permute-done.17.refs_4_) | copy-start | bytes 344068
  100.0 16.5 %collective-permute-start.18 = (bf16[112,512]{1,0:T(8,128)(2,1)}, bf16[112,512]{1,0:T(8,128)(2,1)S(1)}, u32[]{:S(2)}, u32[]{:S(2)}) collective-permute-start(bf16[112,512]{1,0:T(8,128)(2,1)} %collective-permute-done.16.refs_3_), channel_id=1, source_target_pairs={{0,1},{1,2},{2,3},{3,4},{4,5},{5,6},{6,7},{7,0},{8,9},{9,10},{10,1... | collective-permute-start | bytes 344072 | tf_op jit(solution)/shard_map/ppermute | solution.py:41
  100.3 16.2 %collective-permute-start.19 = (bf16[112,512]{1,0:T(8,128)(2,1)}, bf16[112,512]{1,0:T(8,128)(2,1)S(1)}, u32[]{:S(2)}, u32[]{:S(2)}) collective-permute-start(bf16[112,512]{1,0:T(8,128)(2,1)} %copy-done.8), channel_id=1, source_target_pairs={{0,7},{1,0},{2,1},{3,2},{4,3},{5,4},{6,5},{7,6},{8,15},{9,8},{10,9... | collective-permute-start | bytes 344072 | tf_op jit(solution)/shard_map/ppermute | solution.py:41
  103.5 0.6 copy-start.10
  104.2 12.3 %all-to-all-start.2 = ((bf16[8,16,384]{2,1,0:T(8,128)(2,1)}), bf16[8,16,384]{2,1,0:T(8,128)(2,1)S(1)}, u32[]{:S(2)}, u32[]{:S(2)}) async-start(bf16[8,16,384]{2,1,0:T(8,128)(2,1)} %copy-done.10), calls=%async_computation.2 | async-start | bytes 196608 | tf_op jit(solution)/shard_map/all_to_all | solution.py:49
  107.6 4.8 %collective-permute-start.20 = (f32[16,512]{1,0:T(8,128)S(1)}, f32[16,512]{1,0:T(8,128)S(1)}, u32[]{:S(2)}, u32[]{:S(2)}) collective-permute-start(f32[16,512]{1,0:T(8,128)S(1)} %get-tuple-element.43), channel_id=1, source_target_pairs={{0,1},{1,0},{2,3},{3,2},{4,5},{5,4},{6,7},{7,6},{8,9},{9,8},{10,11... | collective-permute-start | bytes 98312 | tf_op jit(solution)/shard_map/ppermute | solution.py:45
  112.4 4.1 %collective-permute-start.21 = (f32[16,512]{1,0:T(8,128)S(1)}, f32[16,512]{1,0:T(8,128)S(1)}, u32[]{:S(2)}, u32[]{:S(2)}) collective-permute-start(f32[16,512]{1,0:T(8,128)S(1)} %add.67), channel_id=1, source_target_pairs={{0,2},{1,3},{2,0},{3,1},{4,6},{5,7},{6,4},{7,5},{8,10},{9,11},{10,... | collective-permute-start | bytes 98312 | tf_op jit(solution)/shard_map/ppermute | solution.py:45
  117.5 13.8 %all-to-all-start.3 = ((bf16[16,16,1024]{2,1,0:T(8,128)(2,1)}), bf16[16,16,1024]{2,1,0:T(8,128)(2,1)S(1)}, u32[]{:S(2)}, u32[]{:S(2)}) async-start(bf16[16,16,1024]{2,1,0:T(8,128)(2,1)} %assemble.1), calls=%async_computation.3 | async-start | bytes 1048576 | tf_op jit(solution)/shard_map/all_to_all | solution.py:49
  121.1 10.1 %collective-permute-start.22 = (bf16[64,512]{1,0:T(8,128)(2,1)S(1)}, bf16[64,512]{1,0:T(8,128)(2,1)S(1)}, u32[]{:S(2)}, u32[]{:S(2)}) collective-permute-start(bf16[64,512]{1,0:T(8,128)(2,1)S(1)} %slice.98), channel_id=1, source_target_pairs={{0,1},{1,2},{2,3},{3,4},{4,5},{5,6},{6,7},{7,0},{8,9},{9,10},{10,1... | collective-permute-start | bytes 196616 | tf_op jit(solution)/shard_map/ppermute | solution.py:41
  121.5 9.8 %collective-permute-start.23 = (bf16[48,512]{1,0:T(8,128)(2,1)S(1)}, bf16[48,512]{1,0:T(8,128)(2,1)S(1)}, u32[]{:S(2)}, u32[]{:S(2)}) collective-permute-start(bf16[48,512]{1,0:T(8,128)(2,1)S(1)} %slice.99), channel_id=1, source_target_pairs={{0,7},{1,0},{2,1},{3,2},{4,3},{5,4},{6,5},{7,6},{8,15},{9,8},{10,9... | collective-permute-start | bytes 147464 | tf_op jit(solution)/shard_map/ppermute | solution.py:41
  124.1 7.2 %collective-permute-start.24 = (f32[16,512]{1,0:T(8,128)S(1)}, f32[16,512]{1,0:T(8,128)S(1)}, u32[]{:S(2)}, u32[]{:S(2)}) collective-permute-start(f32[16,512]{1,0:T(8,128)S(1)} %add.68), channel_id=1, source_target_pairs={{0,4},{1,5},{2,6},{3,7},{4,0},{5,1},{6,2},{7,3},{8,12},{9,13},{10,... | collective-permute-start | bytes 98312 | tf_op jit(solution)/shard_map/ppermute | solution.py:45
  131.3 4.3 %collective-permute-start.25 = (bf16[256,1024]{1,0:T(8,128)(2,1)S(1)}, bf16[256,1024]{1,0:T(8,128)(2,1)S(1)}, u32[]{:S(2)}, u32[]{:S(2)}) collective-permute-start(bf16[256,1024]{1,0:T(8,128)(2,1)S(1)} %bitcast.88), channel_id=1, source_target_pairs={{0,8},{8,0},{1,9},{9,1},{2,10},{10,2},{3,11},{11,3},{4,12},{12,4},... | collective-permute-start | bytes 1572872 | tf_op jit(solution)/shard_map/ppermute | solution.py:37
  135.6 2.0 %copy-start.2 = (f32[896,1024]{1,0:T(8,128)S(1)}, f32[896,1024]{1,0:T(8,128)}, u32[]{:S(2)}) copy-start(f32[896,1024]{1,0:T(8,128)} %refs_12_.1) | copy-start | bytes 11010052
  137.6 0.9 copy-start.7
  138.5 0.9 copy-start.9

commit v6 on v5

--- a/solution.py
+++ b/solution.py
@@ -196,12 +196,20 @@
 
 def slab_kernel(pos_ref, count_ref, *refs):
     pieces = refs[:8]
-    near, far, total_ref, wh_ref, slab_ref, new_ref, grad_ref, panel_ref = refs[8:]
+    near, far, total_ref, wh_ref, slab_ref, new_ref, grad_ref, panel_ref, old_ref, sems = refs[8:]
     z = pos_ref[4]
     n = pieces[0].shape[0]
 
+    steps, _, step = old_ref.shape
+    copies = [
+        pltpu.make_async_copy(slab_ref.at[:, k * step : (k + 1) * step], old_ref.at[k], sems.at[k])
+        for k in range(steps)
+    ]
+
     @pl.when(pl.program_id(0) == 0)
     def _():
+        for copy in copies:
+            copy.start()
         for piece, d in zip(pieces, (0, -1, 1, -2, 2, -3, 3, 4)):
             at = pl.multiple_of(((z + d + 8) % 8) * n, 16)
             panel_ref[pl.ds(at, piece.shape[0]), :] = piece[...]
@@ -209,7 +217,13 @@
     scale = 1.0 / jnp.full((1, 1), count_ref[0].astype(F32), F32)
     gram = jnp.dot(panel_ref[:, :256], near[...], preferred_element_type=F32)
     gram += jnp.dot(panel_ref[:, 256:], far[...], preferred_element_type=F32)
-    new_ref[...] = slab_ref[...] + gram * scale
+    for k, copy in enumerate(copies):
+
+        @pl.when(pl.program_id(0) == k)
+        def _(k=k, copy=copy):
+            copy.wait()
+            new_ref[...] = old_ref[k] + gram * scale
+
     added = jnp.zeros_like(grad_ref)
     for half, rows in ((pos_ref[3], near), (1 - pos_ref[3], far)):
         part = total_ref[:, pl.ds(pl.multiple_of(half * 256, 256), 256)]
@@ -220,7 +234,7 @@
 
 def slab_call(pos, count, pieces, near, far, total, wh, slab):
     rows, width = slab.shape
-    step = 512
+    step = 256
 
     def fixed(a):
         return pl.BlockSpec(a.shape, lambda k, *_: (0,) * a.ndim)
@@ -234,15 +248,20 @@
             num_scalar_prefetch=2,
             grid=(width // step,),
             in_specs=[fixed(p) for p in pieces]
-            + [columns(256), columns(256), fixed(total), columns(16), columns(rows)],
+            + [columns(256), columns(256), fixed(total), columns(16)]
+            + [pl.BlockSpec(memory_space=pltpu.HBM)],
             out_specs=(columns(rows), columns(16)),
-            scratch_shapes=[pltpu.VMEM((rows, 512), BF16)],
+            scratch_shapes=[
+                pltpu.VMEM((rows, 512), BF16),
+                pltpu.VMEM((width // step, rows, step), F32),
+                pltpu.SemaphoreType.DMA((width // step,)),
+            ],
         ),
         out_shape=(
             jax.ShapeDtypeStruct((rows, width), F32),
             jax.ShapeDtypeStruct((16, width), F32),
         ),
-        compiler_params=pltpu.CompilerParams(vmem_limit_bytes=20 << 20),
+        compiler_params=pltpu.CompilerParams(vmem_limit_bytes=50 << 20),
         name="slab",
     )(pos, count, *pieces, near, far, total, wh, slab)
 
@@ -324,7 +343,6 @@
     wh = jnp.concatenate([sums[0], sums[1]], 1)
     total += swap_z(total, 1)
     total += swap_z(total, 2)
-    pieces, f3, g3, wh, total = lax.optimization_barrier((pieces, f3, g3, wh, total))
     total += swap_z(total, 4)
     f4, g4 = shift_z(f3[:64], 1), shift_z(g3[64:], -1)
     h4 = jnp.concatenate([f4, g4], 0)

time: 145 us -> 158 us (1.090)
  waiting for transfers between devices: 44.6 us -> 51 us
  local copies, waits for them, and re-layouts: 13.6 us -> 18.9 us
  starting transfers between devices: 56.7 us -> 53.7 us
  other arithmetic: 2.65 us -> 4.68 us
  Pallas kernels: 9.63 us -> 11.4 us
    all_to_all x4, waiting for transfers between devices: 13.1 us -> 20.9 us  [exchange(): return lax.all_to_all(array, axes, split_axis=0, concat_axis=0, tiled=True)]
    unnamed x24 -> x44, local copies, waits for them, and re-layouts: 9.18 us -> 14.4 us
    ppermute x3, starting transfers between devices: 7.07 us -> 2.68 us  [swap_z(): return lax.ppermute(array, 'gc', [(i, i ^ k) for i in range(8)])]
    pallas_call x1, Pallas kernels: 4.35 us -> 6.36 us  [slab_call(): pl.pallas_call(slab_kernel, grid_spec=pltpu.PrefetchScalarGridSpec(num_sc...]
  transfers between devices with their start and end apart: 30 -> 30, of which waited for: 15 -> 16; matrix products, arithmetic and copies ran while one was open for 11% -> 12% of each run, Pallas kernels for 2% -> 1%
where the time goes in v6:
time: 158 us; the launch traced here: 156 us
  starting transfers between devices  53.7 us (34%)
  waiting for transfers between devices  51 us (32%)
  local copies, waits for them, and re-layouts  18.9 us (12%)
  matrix products  14.2 us (9%)
  Pallas kernels  11.4 us (7%)
  other arithmetic  4.68 us (3%)
  between operations  2.64 us (2%)
    all_to_all x4, waiting for transfers between devices, exchange(): return lax.all_to_all(array, axes, split_axis=0, concat_axis=0, tiled=True)  20.9 us
    all_to_all x4, starting transfers between devices, exchange(): return lax.all_to_all(array, axes, split_axis=0, concat_axis=0, tiled=True)  19.9 us
    unnamed x44, local copies, waits for them, and re-layouts  14.4 us
    ppermute x9, waiting for transfers between devices, plane_permute(): return lax.ppermute(array, CAL_GR, pairs)  13.7 us
    ppermute x6, starting transfers between devices, core_swap(): return lax.ppermute(array, 'gr_2', [(0, 1), (1, 0)])  11.8 us
    ppermute x9, starting transfers between devices, plane_permute(): return lax.ppermute(array, CAL_GR, pairs)  10.7 us
    ppermute x8, starting transfers between devices, shift_z(): return lax.ppermute(array, 'gc', [(i, (i + d) % 8) for i in range(8)])  8.59 us
    ppermute x3, waiting for transfers between devices, swap_z(): return lax.ppermute(array, 'gc', [(i, i ^ k) for i in range(8)])  8.42 us
  transfers between devices with their start and end apart: 30, of which 16 were waited for; matrix products, arithmetic and copies ran while one was open for 12% of the time, Pallas kernels for 1%

profile of v6, /device:TPU:1, one launch (start us, length us, event | category | flops | bytes accessed | tf_op | source)
XLA Modules:
  0.0 156.5 jit_solution(9438370814132852764)
XLA Ops:
  0.7 0.9 constant_dynamic-slice_fusion.1
  1.5 3.2 %collective-permute-start = (bf16[4,2048]{1,0:T(4,128)(2,1)S(1)}, bf16[4,2048]{1,0:T(4,128)(2,1)S(1)}, u32[]{:S(2)}, u32[]{:S(2)}) collective-permute-start(bf16[4,2048]{1,0:T(4,128)(2,1)S(1)} %constant_dynamic-slice_fusion.1), channel_id=1, source_target_pairs={{0,8},{8,0},{1,9},{9,1},{2,10},{10,2},{3,11},{11,3},{4,12},{12,4},... | collective-permute-start | bytes 49160 | tf_op jit(solution)/shard_map/ppermute | solution.py:37
  4.7 0.8 collective-permute-done
  5.6 0.7 broadcast_select_fusion.1
  6.3 0.7 broadcast_in_dim.2
  7.0 1.6 dynamic-slice_bitcast_fusion.14
  8.6 1.5 pad_maximum_fusion
  10.4 6.5 %all-to-all-start = ((bf16[8,8,2048]{2,1,0:T(8,128)(2,1)}), bf16[8,8,2048]{2,1,0:T(8,128)(2,1)S(1)}, u32[]{:S(2)}, u32[]{:S(2)}) async-start(bf16[8,8,2048]{2,1,0:T(8,128)(2,1)} %broadcast_in_dim.2), calls=%async_computation | async-start | bytes 524288 | tf_op jit(solution)/shard_map/all_to_all | solution.py:49
  17.0 4.5 %fusion = f32[512,512]{1,0:T(8,128)} fusion(f32[512,896]{1,0:T(8,128)S(1)} %copy-done, f32[896,1024]{1,0:T(8,128)} %refs_12_.1, s32[]{:T(128)S(6)} %select_n.60), kind=kOutput, calls=%fused_computation.1 | convolution fusion | flops 1409286144 | bytes 4718596 | tf_op jit(solution)/shard_map/dot_general | solution.py:298
  21.6 1.9 %fusion.2 = f32[512,512]{1,0:T(8,128)S(1)} fusion(f32[512,896]{1,0:T(8,128)S(1)} %copy-done, f32[896,1024]{1,0:T(8,128)S(1)} %copy-done.20, s32[]{:T(128)S(6)} %select_n.59), kind=kOutput, calls=%fused_computation.3 | convolution fusion | flops 1409286144 | bytes 4718596 | tf_op jit(solution)/shard_map/dot_general | solution.py:298
  23.5 5.6 %all-to-all-done = bf16[8,8,2048]{2,1,0:T(8,128)(2,1)S(1)} async-done(((bf16[8,8,2048]{2,1,0:T(8,128)(2,1)}), bf16[8,8,2048]{2,1,0:T(8,128)(2,1)S(1)}, u32[]{:S(2)}, u32[]{:S(2)}) %all-to-all-start) | async-done | bytes 262176 | tf_op jit(solution)/shard_map/all_to_all | solution.py:49
  29.1 2.9 %collective-permute-start.2 = (bf16[64,2048]{1,0:T(8,128)(2,1)S(1)}, bf16[64,2048]{1,0:T(8,128)(2,1)}, u32[]{:S(2)}, u32[]{:S(2)}) collective-permute-start(bf16[64,2048]{1,0:T(8,128)(2,1)S(1)} %bitcast.91), channel_id=1, source_target_pairs={{0,64},{8,40},{16,80},{24,56},{32,96},{40,8},{48,112},{56,24},{128... | collective-permute-start | bytes 786440 | tf_op jit(solution)/shard_map/ppermute | solution.py:33
  32.1 0.8 collective-permute-start.4
  32.9 1.2 collective-permute-start.13
  34.1 1.5 copy-done.1
  35.6 1.5 copy-done.2
  37.1 2.3 %weights.1 = bf16[2,512,2048]{2,1,0:T(8,128)(2,1)S(1)} custom-call(s32[5]{0:T(128)S(1)} %stack.38.pos_ref, bf16[112,8192]{1,0:T(8,128)(2,1)S(1)} %bitcast.86, bf16[112,8192]{1,0:T(8,128)(2,1)S(1)} %bitcast.87, bf16[2,2,112,2048]{3,2,1,0:T(8,128)(2,1)} %bitcast.16.far), custom_call_target="tpu_custom_call" | custom-call | tf_op jit(solution)/shard_map/weights/pallas_call | solution.py:70
  39.4 1.0 constant_dynamic-update-slice_fusion
  40.4 1.9 %collective-permute-start.7 = (bf16[128,2048]{1,0:T(8,128)(2,1)S(1)}, bf16[128,2048]{1,0:T(8,128)(2,1)S(1)}, u32[]{:S(2)}, u32[]{:S(2)}) collective-permute-start(bf16[128,2048]{1,0:T(8,128)(2,1)S(1)} %constant_dynamic-update-slice_fusion), channel_id=1, source_target_pairs={{0,48},{8,200},{16,32},{24,216},{32,16},{40,232},{48,0},{56,248},{... | collective-permute-start | bytes 1572872 | tf_op jit(solution)/shard_map/ppermute | solution.py:33
  42.3 1.1 collective-permute-start.5
  43.5 0.9 collective-permute-start.8
  46.4 4.2 %collective-permute-done.5 = bf16[128,2048]{1,0:T(8,128)(2,1)S(1)} collective-permute-done((bf16[128,2048]{1,0:T(8,128)(2,1)S(1)}, bf16[128,2048]{1,0:T(8,128)(2,1)S(1)}, u32[]{:S(2)}, u32[]{:S(2)}) %collective-permute-start.5) | collective-permute-done | bytes 524320 | tf_op jit(solution)/shard_map/ppermute | solution.py:33
  51.1 5.1 %collective-permute-done.6 = bf16[128,2048]{1,0:T(8,128)(2,1)S(1)} collective-permute-done((bf16[128,2048]{1,0:T(8,128)(2,1)S(1)}, bf16[128,2048]{1,0:T(8,128)(2,1)S(1)}, u32[]{:S(2)}, u32[]{:S(2)}) %collective-permute-start.6) | collective-permute-done | bytes 524320 | tf_op jit(solution)/shard_map/ppermute | solution.py:33
  57.7 2.2 %collective-permute-start.11 = (f32[768,256]{1,0:T(8,128)S(1)}, f32[768,256]{1,0:T(8,128)S(1)}, u32[]{:S(2)}, u32[]{:S(2)}) collective-permute-start(f32[768,256]{1,0:T(8,128)S(1)} %convolution_dynamic-update-slice_fusion), channel_id=1, source_target_pairs={{0,8},{8,0},{1,9},{9,1},{2,10},{10,2},{3,11},{11,3},{4,12},{12,4},... | collective-permute-start | bytes 2359304 | tf_op jit(solution)/shard_map/ppermute | solution.py:37
  59.9 1.8 %collective-permute-start.9 = (bf16[128,2048]{1,0:T(8,128)(2,1)S(1)}, bf16[128,2048]{1,0:T(8,128)(2,1)S(1)}, u32[]{:S(2)}, u32[]{:S(2)}) collective-permute-start(bf16[128,2048]{1,0:T(8,128)(2,1)S(1)} %collective-permute-done.5), channel_id=1, source_target_pairs={{0,48},{8,200},{16,32},{24,216},{32,16},{40,232},{48,0},{56,248},{... | collective-permute-start | bytes 1572872 | tf_op jit(solution)/shard_map/ppermute | solution.py:33
  61.7 1.1 collective-permute-start.10
  65.1 4.3 %collective-permute-done.9 = bf16[128,2048]{1,0:T(8,128)(2,1)S(1)} collective-permute-done((bf16[128,2048]{1,0:T(8,128)(2,1)S(1)}, bf16[128,2048]{1,0:T(8,128)(2,1)S(1)}, u32[]{:S(2)}, u32[]{:S(2)}) %collective-permute-start.9) | collective-permute-done | bytes 524320 | tf_op jit(solution)/shard_map/ppermute | solution.py:33
  70.5 1.0 collective-permute-start.12
  72.7 1.3 activate.1
  74.0 1.0 copy-done.4
  75.0 6.3 %all-to-all-start.1 = ((bf16[32,16,1152]{2,1,0:T(8,128)(2,1)}), bf16[32,16,1152]{2,1,0:T(8,128)(2,1)S(1)}, u32[]{:S(2)}, u32[]{:S(2)}) async-start(bf16[32,16,1152]{2,1,0:T(8,128)(2,1)} %copy-done.4), calls=%async_computation.1 | async-start | bytes 2359296 | tf_op jit(solution)/shard_map/all_to_all | solution.py:49
  81.4 1.5 collective-permute-start.14
  82.8 3.0 %collective-permute-done.15.refs_2_ = bf16[112,512]{1,0:T(8,128)(2,1)S(1)} collective-permute-done((bf16[112,512]{1,0:T(8,128)(2,1)S(1)}, bf16[112,512]{1,0:T(8,128)(2,1)S(1)}, u32[]{:S(2)}, u32[]{:S(2)}) %collective-permute-start.15) | collective-permute-done | bytes 114720 | tf_op jit(solution)/shard_map/ppermute | solution.py:41
  85.8 1.5 collective-permute-start.17
  87.3 0.6 copy-done.13
  88.0 0.6 copy-done.15
  89.8 0.6 copy-done.17
  90.4 2.7 %collective-permute-done.16.refs_3_ = bf16[112,512]{1,0:T(8,128)(2,1)} collective-permute-done((bf16[112,512]{1,0:T(8,128)(2,1)S(1)}, bf16[112,512]{1,0:T(8,128)(2,1)}, u32[]{:S(2)}, u32[]{:S(2)}) %collective-permute-start.16) | collective-permute-done | bytes 114720 | tf_op jit(solution)/shard_map/ppermute | solution.py:41
  93.1 6.9 %all-to-all-done.1.arrived_ref = bf16[32,16,1152]{2,1,0:T(8,128)(2,1)S(1)} async-done(((bf16[32,16,1152]{2,1,0:T(8,128)(2,1)}), bf16[32,16,1152]{2,1,0:T(8,128)(2,1)S(1)}, u32[]{:S(2)}, u32[]{:S(2)}) %all-to-all-start.1) | async-done | bytes 1179680 | tf_op jit(solution)/shard_map/all_to_all | solution.py:49
  100.0 1.3 choose.1
  101.9 3.4 %all-to-all-start.2 = ((bf16[8,16,384]{2,1,0:T(8,128)(2,1)}), bf16[8,16,384]{2,1,0:T(8,128)(2,1)S(1)}, u32[]{:S(2)}, u32[]{:S(2)}) async-start(bf16[8,16,384]{2,1,0:T(8,128)(2,1)} %get-tuple-element.37), calls=%async_computation.2 | async-start | bytes 196608 | tf_op jit(solution)/shard_map/all_to_all | solution.py:49
  105.3 8.4 %all-to-all-done.2.refs_1_ = bf16[8,16,384]{2,1,0:T(8,128)(2,1)S(1)} async-done(((bf16[8,16,384]{2,1,0:T(8,128)(2,1)}), bf16[8,16,384]{2,1,0:T(8,128)(2,1)S(1)}, u32[]{:S(2)}, u32[]{:S(2)}) %all-to-all-start.2) | async-done | bytes 98336 | tf_op jit(solution)/shard_map/all_to_all | solution.py:49
  114.0 0.8 copy-done.3
  114.7 3.8 %all-to-all-start.3 = ((bf16[16,16,1024]{2,1,0:T(8,128)(2,1)}), bf16[16,16,1024]{2,1,0:T(8,128)(2,1)S(1)}, u32[]{:S(2)}, u32[]{:S(2)}) async-start(bf16[16,16,1024]{2,1,0:T(8,128)(2,1)} %copy-done.3), calls=%async_computation.3 | async-start | bytes 1048576 | tf_op jit(solution)/shard_map/all_to_all | solution.py:49
  118.7 2.6 %collective-permute-start.19 = (bf16[112,512]{1,0:T(8,128)(2,1)}, bf16[112,512]{1,0:T(8,128)(2,1)S(1)}, u32[]{:S(2)}, u32[]{:S(2)}) collective-permute-start(bf16[112,512]{1,0:T(8,128)(2,1)} %copy-done.17), channel_id=1, source_target_pairs={{0,7},{1,0},{2,1},{3,2},{4,3},{5,4},{6,5},{7,6},{8,15},{9,8},{10,9... | collective-permute-start | bytes 344072 | tf_op jit(solution)/shard_map/ppermute | solution.py:41
  121.3 3.3 %collective-permute-done.22 = f32[16,512]{1,0:T(8,128)S(1)} collective-permute-done((f32[16,512]{1,0:T(8,128)}, f32[16,512]{1,0:T(8,128)S(1)}, u32[]{:S(2)}, u32[]{:S(2)}) %collective-permute-start.22) | collective-permute-done | bytes 32800 | tf_op jit(solution)/shard_map/ppermute | solution.py:45
  124.6 0.8 add.68
  125.5 2.7 %collective-permute-start.21 = (bf16[48,512]{1,0:T(8,128)(2,1)S(1)}, bf16[48,512]{1,0:T(8,128)(2,1)S(1)}, u32[]{:S(2)}, u32[]{:S(2)}) collective-permute-start(bf16[48,512]{1,0:T(8,128)(2,1)S(1)} %slice.105), channel_id=1, source_target_pairs={{0,7},{1,0},{2,1},{3,2},{4,3},{5,4},{6,5},{7,6},{8,15},{9,8},{10,9... | collective-permute-start | bytes 147464 | tf_op jit(solution)/shard_map/ppermute | solution.py:41
  128.2 1.2 collective-permute-done.23
  129.4 2.7 %collective-permute-start.24 = (f32[16,512]{1,0:T(8,128)S(1)}, f32[16,512]{1,0:T(8,128)S(1)}, u32[]{:S(2)}, u32[]{:S(2)}) collective-permute-start(f32[16,512]{1,0:T(8,128)S(1)} %add.69), channel_id=1, source_target_pairs={{0,4},{1,5},{2,6},{3,7},{4,0},{5,1},{6,2},{7,3},{8,12},{9,13},{10,... | collective-permute-start | bytes 98312 | tf_op jit(solution)/shard_map/ppermute | solution.py:45
  132.0 4.0 %collective-permute-done.24 = f32[16,512]{1,0:T(8,128)S(1)} collective-permute-done((f32[16,512]{1,0:T(8,128)S(1)}, f32[16,512]{1,0:T(8,128)S(1)}, u32[]{:S(2)}, u32[]{:S(2)}) %collective-permute-start.24) | collective-permute-done | bytes 32800 | tf_op jit(solution)/shard_map/ppermute | solution.py:45
  136.0 0.6 add.70.refs_10_
  136.7 0.7 pad_maximum_fusion.2.refs_7_
  137.4 4.0 %collective-permute-start.25 = (bf16[256,1024]{1,0:T(8,128)(2,1)S(1)}, bf16[256,1024]{1,0:T(8,128)(2,1)S(1)}, u32[]{:S(2)}, u32[]{:S(2)}) collective-permute-start(bf16[256,1024]{1,0:T(8,128)(2,1)S(1)} %bitcast.88), channel_id=1, source_target_pairs={{0,8},{8,0},{1,9},{9,1},{2,10},{10,2},{3,11},{11,3},{4,12},{12,4},... | collective-permute-start | bytes 1572872 | tf_op jit(solution)/shard_map/ppermute | solution.py:37
  142.2 0.7 collective-permute-done.25.refs_9_
  142.9 0.9 copy-done.5
  143.8 0.9 copy-done.7
  144.7 0.9 copy-done.9
  145.6 0.8 copy-done.10
  146.3 0.9 copy-done.12
  147.2 0.9 copy-done.14
  148.1 0.9 copy-done.16
  149.0 0.9 copy-done.18
  149.9 6.4 %slab.1 = (f32[896,1024]{1,0:T(8,128)}, f32[16,1024]{1,0:T(8,128)}) custom-call(s32[5]{0:T(128)S(1)} %stack.38.pos_ref, s32[1]{0:T(128)S(6)} %copy.17.count_ref, bf16[112,512]{1,0:T(8,128)(2,1)S(1)} %copy-done.12, bf16[112,512]{1,0:T(8,128)(2,1)S(1)} %copy-done.16, bf16[112,512]{1,0:T(8,128)(2,1)S(1)} %copy-done.14, ...), custom_call_target="tpu_custom_call" | custom-call | tf_op jit(solution)/shard_map/slab/pallas_call | solution.py:245
  (88 shorter events, 11.0 us)
Async XLA Ops:
  0.6 16.3 %copy-start = (f32[512,896]{1,0:T(8,128)S(1)}, f32[512,896]{1,0:T(8,128)}, u32[]{:S(2)}) copy-start(f32[512,896]{1,0:T(8,128)} %param.11) | copy-start | bytes 5505028
  1.5 4.0 %collective-permute-start = (bf16[4,2048]{1,0:T(4,128)(2,1)S(1)}, bf16[4,2048]{1,0:T(4,128)(2,1)S(1)}, u32[]{:S(2)}, u32[]{:S(2)}) collective-permute-start(bf16[4,2048]{1,0:T(4,128)(2,1)S(1)} %constant_dynamic-slice_fusion.1), channel_id=1, source_target_pairs={{0,8},{8,0},{1,9},{9,1},{2,10},{10,2},{3,11},{11,3},{4,12},{12,4},... | collective-permute-start | bytes 49160 | tf_op jit(solution)/shard_map/ppermute | solution.py:37
  10.1 19.1 %collective-permute-start.1 = (bf16[4,112,2048]{2,1,0:T(8,128)(2,1)}, bf16[4,112,2048]{2,1,0:T(8,128)(2,1)}, u32[]{:S(2)}, u32[]{:S(2)}) collective-permute-start(bf16[4,112,2048]{2,1,0:T(8,128)(2,1)} %pad_maximum_fusion), channel_id=1, source_target_pairs={{0,8},{8,0},{1,9},{9,1},{2,10},{10,2},{3,11},{11,3},{4,12},{12,4},... | collective-permute-start | bytes 5505032 | tf_op jit(solution)/shard_map/ppermute | solution.py:37
  10.4 18.7 %all-to-all-start = ((bf16[8,8,2048]{2,1,0:T(8,128)(2,1)}), bf16[8,8,2048]{2,1,0:T(8,128)(2,1)S(1)}, u32[]{:S(2)}, u32[]{:S(2)}) async-start(bf16[8,8,2048]{2,1,0:T(8,128)(2,1)} %broadcast_in_dim.2), calls=%async_computation | async-start | bytes 524288 | tf_op jit(solution)/shard_map/all_to_all | solution.py:49
  16.9 4.7 %copy-start.20 = (f32[896,1024]{1,0:T(8,128)S(1)}, f32[896,1024]{1,0:T(8,128)}, u32[]{:S(2)}) copy-start(f32[896,1024]{1,0:T(8,128)} %refs_12_.1) | copy-start | bytes 11010052
  29.1 10.3 %collective-permute-start.2 = (bf16[64,2048]{1,0:T(8,128)(2,1)S(1)}, bf16[64,2048]{1,0:T(8,128)(2,1)}, u32[]{:S(2)}, u32[]{:S(2)}) collective-permute-start(bf16[64,2048]{1,0:T(8,128)(2,1)S(1)} %bitcast.91), channel_id=1, source_target_pairs={{0,64},{8,40},{16,80},{24,56},{32,96},{40,8},{48,112},{56,24},{128... | collective-permute-start | bytes 786440 | tf_op jit(solution)/shard_map/ppermute | solution.py:33
  32.1 11.3 %collective-permute-start.4 = (bf16[64,2048]{1,0:T(8,128)(2,1)S(1)}, bf16[64,2048]{1,0:T(8,128)(2,1)S(1)}, u32[]{:S(2)}, u32[]{:S(2)}) collective-permute-start(bf16[64,2048]{1,0:T(8,128)(2,1)S(1)} %bitcast.92), channel_id=1, source_target_pairs={{0,192},{8,56},{16,208},{24,40},{32,224},{40,24},{48,240},{56,8},{... | collective-permute-start | bytes 786440 | tf_op jit(solution)/shard_map/ppermute | solution.py:33
  32.9 10.5 %collective-permute-start.3 = (bf16[64,2048]{1,0:T(8,128)(2,1)S(1)}, bf16[64,2048]{1,0:T(8,128)(2,1)S(1)}, u32[]{:S(2)}, u32[]{:S(2)}) collective-permute-start(bf16[64,2048]{1,0:T(8,128)(2,1)S(1)} %bitcast.93), channel_id=1, source_target_pairs={{0,128},{8,24},{16,144},{24,8},{32,160},{40,56},{48,176},{56,40},{... | collective-permute-start | bytes 786440 | tf_op jit(solution)/shard_map/ppermute | solution.py:33
  32.9 31.9 %collective-permute-start.13 = (f32[512,512]{1,0:T(8,128)}, f32[512,512]{1,0:T(8,128)S(1)}, u32[]{:S(2)}, u32[]{:S(2)}) collective-permute-start(f32[512,512]{1,0:T(8,128)} %fusion), channel_id=1, source_target_pairs={{0,8},{8,0},{1,9},{9,1},{2,10},{10,2},{3,11},{11,3},{4,12},{12,4},... | collective-permute-start | bytes 3145736 | tf_op jit(solution)/shard_map/ppermute | solution.py:37
  34.1 1.5 copy-start.1
  35.6 1.5 copy-start.2
  40.4 16.3 %collective-permute-start.7 = (bf16[128,2048]{1,0:T(8,128)(2,1)S(1)}, bf16[128,2048]{1,0:T(8,128)(2,1)S(1)}, u32[]{:S(2)}, u32[]{:S(2)}) collective-permute-start(bf16[128,2048]{1,0:T(8,128)(2,1)S(1)} %constant_dynamic-update-slice_fusion), channel_id=1, source_target_pairs={{0,48},{8,200},{16,32},{24,216},{32,16},{40,232},{48,0},{56,248},{... | collective-permute-start | bytes 1572872 | tf_op jit(solution)/shard_map/ppermute | solution.py:33
  42.3 8.3 %collective-permute-start.5 = (bf16[128,2048]{1,0:T(8,128)(2,1)S(1)}, bf16[128,2048]{1,0:T(8,128)(2,1)S(1)}, u32[]{:S(2)}, u32[]{:S(2)}) collective-permute-start(bf16[128,2048]{1,0:T(8,128)(2,1)S(1)} %constant_dynamic-update-slice_fusion), channel_id=1, source_target_pairs={{0,16},{8,136},{16,0},{24,152},{32,48},{40,168},{48,32},{56,184},{... | collective-permute-start | bytes 1572872 | tf_op jit(solution)/shard_map/ppermute | solution.py:33
  43.5 13.8 %collective-permute-start.8 = (bf16[128,2048]{1,0:T(8,128)(2,1)S(1)}, bf16[128,2048]{1,0:T(8,128)(2,1)S(1)}, u32[]{:S(2)}, u32[]{:S(2)}) collective-permute-start(bf16[128,2048]{1,0:T(8,128)(2,1)S(1)} %constant_dynamic-update-slice_fusion.2), channel_id=1, source_target_pairs={{0,48},{8,200},{16,32},{24,216},{32,16},{40,232},{48,0},{56,248},{... | collective-permute-start | bytes 1572872 | tf_op jit(solution)/shard_map/ppermute | solution.py:33
  44.4 11.8 %collective-permute-start.6 = (bf16[128,2048]{1,0:T(8,128)(2,1)S(1)}, bf16[128,2048]{1,0:T(8,128)(2,1)S(1)}, u32[]{:S(2)}, u32[]{:S(2)}) collective-permute-start(bf16[128,2048]{1,0:T(8,128)(2,1)S(1)} %constant_dynamic-update-slice_fusion.2), channel_id=1, source_target_pairs={{0,16},{8,136},{16,0},{24,152},{32,48},{40,168},{48,32},{56,184},{... | collective-permute-start | bytes 1572872 | tf_op jit(solution)/shard_map/ppermute | solution.py:33
  57.7 14.9 %collective-permute-start.11 = (f32[768,256]{1,0:T(8,128)S(1)}, f32[768,256]{1,0:T(8,128)S(1)}, u32[]{:S(2)}, u32[]{:S(2)}) collective-permute-start(f32[768,256]{1,0:T(8,128)S(1)} %convolution_dynamic-update-slice_fusion), channel_id=1, source_target_pairs={{0,8},{8,0},{1,9},{9,1},{2,10},{10,2},{3,11},{11,3},{4,12},{12,4},... | collective-permute-start | bytes 2359304 | tf_op jit(solution)/shard_map/ppermute | solution.py:37
  59.9 9.5 %collective-permute-start.9 = (bf16[128,2048]{1,0:T(8,128)(2,1)S(1)}, bf16[128,2048]{1,0:T(8,128)(2,1)S(1)}, u32[]{:S(2)}, u32[]{:S(2)}) collective-permute-start(bf16[128,2048]{1,0:T(8,128)(2,1)S(1)} %collective-permute-done.5), channel_id=1, source_target_pairs={{0,48},{8,200},{16,32},{24,216},{32,16},{40,232},{48,0},{56,248},{... | collective-permute-start | bytes 1572872 | tf_op jit(solution)/shard_map/ppermute | solution.py:33
  61.7 8.3 %collective-permute-start.10 = (bf16[128,2048]{1,0:T(8,128)(2,1)S(1)}, bf16[128,2048]{1,0:T(8,128)(2,1)S(1)}, u32[]{:S(2)}, u32[]{:S(2)}) collective-permute-start(bf16[128,2048]{1,0:T(8,128)(2,1)S(1)} %collective-permute-done.8), channel_id=1, source_target_pairs={{0,16},{8,136},{16,0},{24,152},{32,48},{40,168},{48,32},{56,184},{... | collective-permute-start | bytes 1572872 | tf_op jit(solution)/shard_map/ppermute | solution.py:33
  70.5 2.1 %collective-permute-start.12 = (f32[256,256]{1,0:T(8,128)S(1)}, f32[256,256]{1,0:T(8,128)S(1)}, u32[]{:S(2)}, u32[]{:S(2)}) collective-permute-start(f32[256,256]{1,0:T(8,128)S(1)} %pad_maximum_fusion.1), channel_id=1, source_target_pairs={{0,8},{8,0},{1,9},{9,1},{2,10},{10,2},{3,11},{11,3},{4,12},{12,4},... | collective-permute-start | bytes 786440 | tf_op jit(solution)/shard_map/ppermute | solution.py:37
  74.0 1.0 copy-start.4
  75.0 26.9 %copy-start.11 = (bf16[112,512]{1,0:T(8,128)(2,1)}, bf16[112,512]{1,0:T(8,128)(2,1)S(1)}, u32[]{:S(2)}) copy-start(bf16[112,512]{1,0:T(8,128)(2,1)S(1)} %get-tuple-element.32.refs_0_) | copy-start | bytes 344068
  75.0 25.0 %all-to-all-start.1 = ((bf16[32,16,1152]{2,1,0:T(8,128)(2,1)}), bf16[32,16,1152]{2,1,0:T(8,128)(2,1)S(1)}, u32[]{:S(2)}, u32[]{:S(2)}) async-start(bf16[32,16,1152]{2,1,0:T(8,128)(2,1)} %copy-done.4), calls=%async_computation.1 | async-start | bytes 2359296 | tf_op jit(solution)/shard_map/all_to_all | solution.py:49
  81.3 4.5 %collective-permute-start.15 = (bf16[112,512]{1,0:T(8,128)(2,1)S(1)}, bf16[112,512]{1,0:T(8,128)(2,1)S(1)}, u32[]{:S(2)}, u32[]{:S(2)}) collective-permute-start(bf16[112,512]{1,0:T(8,128)(2,1)S(1)} %get-tuple-element.32.refs_0_), channel_id=1, source_target_pairs={{0,7},{1,0},{2,1},{3,2},{4,3},{5,4},{6,5},{7,6},{8,15},{9,8},{10,9... | collective-permute-start | bytes 344072 | tf_op jit(solution)/shard_map/ppermute | solution.py:41
  81.4 6.6 %collective-permute-start.14 = (bf16[112,512]{1,0:T(8,128)(2,1)S(1)}, bf16[112,512]{1,0:T(8,128)(2,1)S(1)}, u32[]{:S(2)}, u32[]{:S(2)}) collective-permute-start(bf16[112,512]{1,0:T(8,128)(2,1)S(1)} %get-tuple-element.32.refs_0_), channel_id=1, source_target_pairs={{0,1},{1,2},{2,3},{3,4},{4,5},{5,6},{6,7},{7,0},{8,9},{9,10},{10,1... | collective-permute-start | bytes 344072 | tf_op jit(solution)/shard_map/ppermute | solution.py:41
  85.8 3.9 %collective-permute-start.17 = (bf16[112,512]{1,0:T(8,128)(2,1)S(1)}, bf16[112,512]{1,0:T(8,128)(2,1)S(1)}, u32[]{:S(2)}, u32[]{:S(2)}) collective-permute-start(bf16[112,512]{1,0:T(8,128)(2,1)S(1)} %collective-permute-done.15.refs_2_), channel_id=1, source_target_pairs={{0,7},{1,0},{2,1},{3,2},{4,3},{5,4},{6,5},{7,6},{8,15},{9,8},{10,9... | collective-permute-start | bytes 344072 | tf_op jit(solution)/shard_map/ppermute | solution.py:41
  87.3 0.6 copy-start.13
  88.0 5.1 %collective-permute-start.16 = (bf16[112,512]{1,0:T(8,128)(2,1)S(1)}, bf16[112,512]{1,0:T(8,128)(2,1)}, u32[]{:S(2)}, u32[]{:S(2)}) collective-permute-start(bf16[112,512]{1,0:T(8,128)(2,1)S(1)} %collective-permute-done.14.refs_1_), channel_id=1, source_target_pairs={{0,1},{1,2},{2,3},{3,4},{4,5},{5,6},{6,7},{7,0},{8,9},{9,10},{10,1... | collective-permute-start | bytes 344072 | tf_op jit(solution)/shard_map/ppermute | solution.py:41
  88.0 0.6 copy-start.15
  89.8 0.7 copy-start.17
  101.3 0.6 copy-start.19
  101.9 11.8 %all-to-all-start.2 = ((bf16[8,16,384]{2,1,0:T(8,128)(2,1)}), bf16[8,16,384]{2,1,0:T(8,128)(2,1)S(1)}, u32[]{:S(2)}, u32[]{:S(2)}) async-start(bf16[8,16,384]{2,1,0:T(8,128)(2,1)} %get-tuple-element.37), calls=%async_computation.2 | async-start | bytes 196608 | tf_op jit(solution)/shard_map/all_to_all | solution.py:49
  113.9 0.8 copy-start.3
  114.7 22.6 %all-to-all-start.3 = ((bf16[16,16,1024]{2,1,0:T(8,128)(2,1)}), bf16[16,16,1024]{2,1,0:T(8,128)(2,1)S(1)}, u32[]{:S(2)}, u32[]{:S(2)}) async-start(bf16[16,16,1024]{2,1,0:T(8,128)(2,1)} %copy-done.3), calls=%async_computation.3 | async-start | bytes 1048576 | tf_op jit(solution)/shard_map/all_to_all | solution.py:49
  118.5 6.8 %collective-permute-start.18 = (bf16[112,512]{1,0:T(8,128)(2,1)}, bf16[112,512]{1,0:T(8,128)(2,1)S(1)}, u32[]{:S(2)}, u32[]{:S(2)}) collective-permute-start(bf16[112,512]{1,0:T(8,128)(2,1)} %collective-permute-done.16.refs_3_), channel_id=1, source_target_pairs={{0,1},{1,2},{2,3},{3,4},{4,5},{5,6},{6,7},{7,0},{8,9},{9,10},{10,1... | collective-permute-start | bytes 344072 | tf_op jit(solution)/shard_map/ppermute | solution.py:41
  118.7 6.7 %collective-permute-start.19 = (bf16[112,512]{1,0:T(8,128)(2,1)}, bf16[112,512]{1,0:T(8,128)(2,1)S(1)}, u32[]{:S(2)}, u32[]{:S(2)}) collective-permute-start(bf16[112,512]{1,0:T(8,128)(2,1)} %copy-done.17), channel_id=1, source_target_pairs={{0,7},{1,0},{2,1},{3,2},{4,3},{5,4},{6,5},{7,6},{8,15},{9,8},{10,9... | collective-permute-start | bytes 344072 | tf_op jit(solution)/shard_map/ppermute | solution.py:41
  121.3 3.3 %collective-permute-start.22 = (f32[16,512]{1,0:T(8,128)}, f32[16,512]{1,0:T(8,128)S(1)}, u32[]{:S(2)}, u32[]{:S(2)}) collective-permute-start(f32[16,512]{1,0:T(8,128)} %copy-done.19), channel_id=1, source_target_pairs={{0,1},{1,0},{2,3},{3,2},{4,5},{5,4},{6,7},{7,6},{8,9},{9,8},{10,11... | collective-permute-start | bytes 98312 | tf_op jit(solution)/shard_map/ppermute | solution.py:45
  125.3 4.0 %collective-permute-start.23 = (f32[16,512]{1,0:T(8,128)S(1)}, f32[16,512]{1,0:T(8,128)S(1)}, u32[]{:S(2)}, u32[]{:S(2)}) collective-permute-start(f32[16,512]{1,0:T(8,128)S(1)} %add.68), channel_id=1, source_target_pairs={{0,2},{1,3},{2,0},{3,1},{4,6},{5,7},{6,4},{7,5},{8,10},{9,11},{10,... | collective-permute-start | bytes 98312 | tf_op jit(solution)/shard_map/ppermute | solution.py:45
  125.3 11.3 %copy-start.6 = (bf16[112,512]{1,0:T(8,128)(2,1)}, bf16[112,512]{1,0:T(8,128)(2,1)S(1)}, u32[]{:S(2)}) copy-start(bf16[112,512]{1,0:T(8,128)(2,1)S(1)} %collective-permute-done.18.refs_5_) | copy-start | bytes 344068
  125.4 11.3 %collective-permute-start.20 = (bf16[64,512]{1,0:T(8,128)(2,1)S(1)}, bf16[64,512]{1,0:T(8,128)(2,1)S(1)}, u32[]{:S(2)}, u32[]{:S(2)}) collective-permute-start(bf16[64,512]{1,0:T(8,128)(2,1)S(1)} %slice.104), channel_id=1, source_target_pairs={{0,1},{1,2},{2,3},{3,4},{4,5},{5,6},{6,7},{7,0},{8,9},{9,10},{10,1... | collective-permute-start | bytes 196616 | tf_op jit(solution)/shard_map/ppermute | solution.py:41
  125.5 11.2 %copy-start.8 = (bf16[112,512]{1,0:T(8,128)(2,1)}, bf16[112,512]{1,0:T(8,128)(2,1)S(1)}, u32[]{:S(2)}) copy-start(bf16[112,512]{1,0:T(8,128)(2,1)S(1)} %collective-permute-done.19.refs_6_) | copy-start | bytes 344068
  125.5 11.2 %collective-permute-start.21 = (bf16[48,512]{1,0:T(8,128)(2,1)S(1)}, bf16[48,512]{1,0:T(8,128)(2,1)S(1)}, u32[]{:S(2)}, u32[]{:S(2)}) collective-permute-start(bf16[48,512]{1,0:T(8,128)(2,1)S(1)} %slice.105), channel_id=1, source_target_pairs={{0,7},{1,0},{2,1},{3,2},{4,3},{5,4},{6,5},{7,6},{8,15},{9,8},{10,9... | collective-permute-start | bytes 147464 | tf_op jit(solution)/shard_map/ppermute | solution.py:41
  129.4 6.7 %collective-permute-start.24 = (f32[16,512]{1,0:T(8,128)S(1)}, f32[16,512]{1,0:T(8,128)S(1)}, u32[]{:S(2)}, u32[]{:S(2)}) collective-permute-start(f32[16,512]{1,0:T(8,128)S(1)} %add.69), channel_id=1, source_target_pairs={{0,4},{1,5},{2,6},{3,7},{4,0},{5,1},{6,2},{7,3},{8,12},{9,13},{10,... | collective-permute-start | bytes 98312 | tf_op jit(solution)/shard_map/ppermute | solution.py:45
  137.4 5.5 %collective-permute-start.25 = (bf16[256,1024]{1,0:T(8,128)(2,1)S(1)}, bf16[256,1024]{1,0:T(8,128)(2,1)S(1)}, u32[]{:S(2)}, u32[]{:S(2)}) collective-permute-start(bf16[256,1024]{1,0:T(8,128)(2,1)S(1)} %bitcast.88), channel_id=1, source_target_pairs={{0,8},{8,0},{1,9},{9,1},{2,10},{10,2},{3,11},{11,3},{4,12},{12,4},... | collective-permute-start | bytes 1572872 | tf_op jit(solution)/shard_map/ppermute | solution.py:37
  142.9 0.9 copy-start.5
  143.8 0.9 copy-start.7
  144.7 0.9 copy-start.9
  145.6 0.8 copy-start.10
  146.3 0.9 copy-start.12
  147.2 0.9 copy-start.14
  148.1 0.9 copy-start.16
  149.0 0.9 copy-start.18
